TPU v7x, 32 devices: a whole 2x2x4 slice. The times are simulated.
32 devices in a mesh: doc: 4 (over y, core), seq: 8 (over z, x).
Axes of the slice: x: 2, y: 2, z: 4, core: 2. Of those that a mesh axis runs over, the one named last changes fastest.
Arguments:
- dec_in: bfloat16 [8, 1024, 1472], P('doc', 'seq'), may hold values from -6 to 6
- enc_in: bfloat16 [8, 4096, 1472], P('doc', 'seq'), may hold values from -6 to 6
- tgt_len: int32 [8], P('doc'), may hold values from 256 to 1024, as said below
- enc_len: int32 [8], P('doc'), may hold values from 200 to 4096, as said below
- self_qkv: bfloat16 [3, 1472, 384], P(None, 'seq', 'doc'), may hold values from -0.078125 to 0.078125
- self_out: bfloat16 [384, 1472], P('doc', 'seq'), may hold values from -1.75 to 1.75
- cross_q: bfloat16 [1472, 384], P('seq', 'doc'), may hold values from -0.078125 to 0.078125
- cross_kv: bfloat16 [2, 1472, 384], P(None, 'seq', 'doc'), may hold values from -0.078125 to 0.078125
- cross_out: bfloat16 [384, 1472], P('doc', 'seq'), may hold values from -1.75 to 1.75
- ff_in: bfloat16 [2, 1472, 3584], P(None, 'seq', 'doc'), may hold values from -0.15625 to 0.15625
- ff_out: bfloat16 [3584, 1472], P('doc', 'seq'), may hold values from -0.125 to 0.125
- gains: bfloat16 [3, 1472], P(None, 'seq'), may hold values from 0.099609375 to 1.8984375
- cotangent: bfloat16 [8, 1024, 1472], P('doc', 'seq'), may hold values from -6 to 6
Outputs:
- layer_out: float32 [8, 1024, 1472], P('doc', 'seq')
- dec_grad: float32 [8, 1024, 1472], P('doc', 'seq')
- enc_grad: float32 [8, 4096, 1472], P('doc', 'seq')
- grad_self_qkv: float32 [3, 1472, 384], P(None, 'seq', 'doc')
- grad_self_out: float32 [384, 1472], P('doc', 'seq')
- grad_cross_q: float32 [1472, 384], P('seq', 'doc')
- grad_cross_kv: float32 [2, 1472, 384], P(None, 'seq', 'doc')
- grad_cross_out: float32 [384, 1472], P('doc', 'seq')
- grad_ff_in: float32 [2, 1472, 3584], P(None, 'seq', 'doc')
- grad_ff_out: float32 [3584, 1472], P('doc', 'seq')
- grad_gains: float32 [3, 1472], P(None, 'seq')
Inputs may be any that keep to these rules, and one draw needn't show every extreme that they name: `tgt_len`: one document of every draw has all 1024 positions in use. `enc_len`: one document of every draw has all 4096 slots live and another has 200.
All inputs are finite; a program needn't handle non-finite values.
Results may differ from a plain program's by a relative error of at most 0.034.
The roundings to bfloat16 on the way count: a program that leaves them out, or rounds other values in their place, can miss the bound.
Values may be sent and summed in bfloat16 or wider, within the bound.
No kernel may reach another device: no remote copies, remote signals or barrier semaphores. Data moves between devices by JAX's collectives and lax.ppermute only.
A program may use at most 384 MiB of HBM per device.

v0:
```python
import jax
import jax.numpy as jnp
from jax import lax
from jax.sharding import PartitionSpec as P

HEADS = 6
HEAD_DIM = 64


EPSILON = 1e-06
NEGATIVE = -1e30


def norm_parts(values, gain_row):
    inverse = lax.rsqrt(jnp.mean(values * values, axis=-1, keepdims=True) + EPSILON)
    return (values * inverse * gain_row, inverse)


def norm_back(values, inverse, gain_row, upstream):
    weighted = upstream * gain_row
    inner_sum = jnp.mean(weighted * values, axis=-1, keepdims=True)
    lowered = weighted * inverse - values * (inverse * inverse * inverse) * inner_sum
    return (lowered, jnp.sum(upstream * values * inverse, axis=0))


def matmul_rows(left_op, right_op):
    return jnp.dot(left_op, right_op, preferred_element_type=jnp.float32)


def matmul_back(left_op, right_op):
    return lax.dot_general(
        left_op, right_op, (((1,), (1,)), ((), ())), preferred_element_type=jnp.float32
    )


def matmul_outer(left_op, right_op):
    return lax.dot_general(
        left_op, right_op, (((0,), (0,)), ((), ())), preferred_element_type=jnp.float32
    )


def head_scores(queries, keys_in, allowed):
    scores = jnp.einsum("bqhd,bkhd->bqhk", queries, keys_in, preferred_element_type=jnp.float32)
    return jnp.where(allowed[:, :, None, :], scores, NEGATIVE)


def weigh_values(raised, values_in):
    return jnp.einsum(
        "bqhk,bkhd->bqhd",
        raised.astype(jnp.bfloat16),
        values_in,
        preferred_element_type=jnp.float32,
    )


def mixed_grads(dmixed, numerator, totals):
    d_numer = (dmixed / totals[..., None]).astype(jnp.bfloat16)
    d_total = (-jnp.sum(dmixed * numerator, axis=-1) / (totals * totals)).astype(jnp.bfloat16)
    return (d_numer, d_total)


def score_grads(raised, d_numer, d_total, values_in):
    through = jnp.einsum("bqhd,bkhd->bqhk", d_numer, values_in, preferred_element_type=jnp.float32)
    return (raised * (through + d_total.astype(jnp.float32)[..., None])).astype(jnp.bfloat16)


def pair_grads(d_scores, raised, queries, keys_in, d_numer):
    d_query = jnp.einsum("bqhk,bkhd->bqhd", d_scores, keys_in, preferred_element_type=jnp.float32)
    d_keys = jnp.einsum("bqhk,bqhd->bkhd", d_scores, queries, preferred_element_type=jnp.float32)
    d_values = jnp.einsum(
        "bqhk,bqhd->bkhd", raised.astype(jnp.bfloat16), d_numer, preferred_element_type=jnp.float32
    )
    return (d_query, d_keys, d_values)


def block_size(docs_here):
    if docs_here % 4 == 0:
        return 4
    if docs_here % 2 == 0:
        return 2
    return 1


def feed_forward(rows_in, cot_in, w_in, w_out):
    gate_pre = matmul_rows(rows_in, w_in[0])
    up_pre = matmul_rows(rows_in, w_in[1])
    hidden = (jax.nn.gelu(gate_pre, approximate=True) * up_pre).astype(jnp.bfloat16)
    branch = matmul_rows(hidden, w_out)
    grad_out = matmul_outer(hidden, cot_in)
    d_hidden = matmul_back(cot_in, w_out)
    unused, gelu_pull = jax.vjp(
        lambda gate_val, up_val: jax.nn.gelu(gate_val, approximate=True) * up_val, gate_pre, up_pre
    )
    d_gate, d_up = gelu_pull(d_hidden)
    d_gate_up = jnp.stack([d_gate, d_up]).astype(jnp.bfloat16)
    grad_in = jnp.einsum("td,ctf->cdf", rows_in, d_gate_up, preferred_element_type=jnp.float32)
    d_rows = jnp.einsum("ctf,cdf->td", d_gate_up, w_in, preferred_element_type=jnp.float32)
    return (branch, grad_in, grad_out, d_rows)


def per_device(
    dec_in,
    enc_in,
    tgt_len,
    enc_len,
    self_qkv,
    self_out,
    cross_q,
    cross_kv,
    cross_out,
    ff_in,
    ff_out,
    gains,
    cotangent,
):
    by_rows = (
        lax.all_gather(self_qkv, "seq", axis=1, tiled=True),
        lax.all_gather(self_out, "seq", axis=1, tiled=True),
        lax.all_gather(cross_q, "seq", axis=0, tiled=True),
        lax.all_gather(cross_kv, "seq", axis=1, tiled=True),
        lax.all_gather(cross_out, "seq", axis=1, tiled=True),
        lax.all_gather(ff_in, "seq", axis=1, tiled=True),
        lax.all_gather(ff_out, "seq", axis=1, tiled=True),
        lax.all_gather(gains, "seq", axis=1, tiled=True),
    )
    w_qkv, w_so, w_cq, w_ckv, w_co, w_in, w_out = (
        lax.all_gather(by_rows[0], "doc", axis=2, tiled=True),
        lax.all_gather(by_rows[1], "doc", axis=0, tiled=True),
        lax.all_gather(by_rows[2], "doc", axis=1, tiled=True),
        lax.all_gather(by_rows[3], "doc", axis=2, tiled=True),
        lax.all_gather(by_rows[4], "doc", axis=0, tiled=True),
        lax.all_gather(by_rows[5], "doc", axis=2, tiled=True),
        lax.all_gather(by_rows[6], "doc", axis=0, tiled=True),
    )
    gain_all = by_rows[7].astype(jnp.float32)
    docs_here, rows_doc, model_width = dec_in.shape
    slot_count = enc_in.shape[1]
    seq_ranks = lax.axis_size("seq")
    my_rank = lax.axis_index("seq")
    length = rows_doc * seq_ranks
    inner_width = HEADS * HEAD_DIM
    rows_all = docs_here * rows_doc
    stream = dec_in.reshape(rows_all, model_width).astype(jnp.float32)
    normed1, inverse1 = norm_parts(stream, gain_all[0])
    normed1 = normed1.astype(jnp.bfloat16)
    proj_qkv = jnp.einsum("td,cdk->ctk", normed1, w_qkv, preferred_element_type=jnp.float32).astype(
        jnp.bfloat16
    )
    self_query = proj_qkv[0].reshape(docs_here, rows_doc, HEADS, HEAD_DIM)
    keys_all, values_all = (
        lax.all_gather(
            proj_qkv[1].reshape(docs_here, rows_doc, inner_width), "seq", axis=1, tiled=True
        ),
        lax.all_gather(
            proj_qkv[2].reshape(docs_here, rows_doc, inner_width), "seq", axis=1, tiled=True
        ),
    )
    keys_all = keys_all.reshape(docs_here, length, HEADS, HEAD_DIM)
    values_all = values_all.reshape(docs_here, length, HEADS, HEAD_DIM)
    query_pos = my_rank * rows_doc + jnp.arange(rows_doc, dtype=jnp.int32)
    key_pos = jnp.arange(length, dtype=jnp.int32)
    self_allowed = (key_pos[None, None, :] <= query_pos[None, :, None]) & (
        key_pos[None, None, :] < tgt_len[:, None, None]
    )
    self_scores = head_scores(self_query, keys_all, self_allowed)
    self_top = jnp.max(self_scores, axis=-1)
    self_raised = jnp.exp(self_scores - self_top[..., None])
    self_total = jnp.sum(self_raised, axis=-1)
    self_numer = weigh_values(self_raised, values_all)
    self_mixed = (
        (self_numer / self_total[..., None]).astype(jnp.bfloat16).reshape(rows_all, inner_width)
    )
    stream1 = stream + matmul_rows(self_mixed, w_so)
    normed2, inverse2 = norm_parts(stream1, gain_all[1])
    normed2 = normed2.astype(jnp.bfloat16)
    cross_query = (
        matmul_rows(normed2, w_cq).astype(jnp.bfloat16).reshape(docs_here, rows_doc, inner_width)
    )
    enc_proj = jnp.einsum(
        "bsd,cdk->cbsk", enc_in, w_ckv, preferred_element_type=jnp.float32
    ).astype(jnp.bfloat16)
    queries_all = lax.all_gather(cross_query, "seq", axis=1, tiled=True)
    per_block = block_size(docs_here)
    block_count = docs_here // per_block

    def split_docs(array):
        return array.reshape((block_count, per_block) + array.shape[1:])

    block_queries = split_docs(queries_all.reshape(docs_here, length, HEADS, HEAD_DIM))
    block_keys = split_docs(enc_proj[0].reshape(docs_here, slot_count, HEADS, HEAD_DIM))
    block_values = split_docs(enc_proj[1].reshape(docs_here, slot_count, HEADS, HEAD_DIM))
    slot_pos = my_rank * slot_count + jnp.arange(slot_count, dtype=jnp.int32)
    slot_live = split_docs(slot_pos[None, :] < enc_len[:, None])

    def cross_scores(queries, keys_in, slot_alive):
        allowed = jnp.broadcast_to(
            slot_alive[:, None, :], (slot_alive.shape[0], queries.shape[1], slot_alive.shape[1])
        )
        return head_scores(queries, keys_in, allowed)

    def local_peak(bundle):
        return jnp.max(cross_scores(bundle[0], bundle[1], bundle[2]), axis=-1)

    local_top = lax.map(local_peak, (block_queries, block_keys, slot_live))
    cross_top = lax.pmax(local_top.reshape(docs_here, length, HEADS), "seq")
    block_top = split_docs(cross_top)

    def cross_partial(bundle):
        queries, keys_in, values_in, slot_alive, peak_row = bundle
        raised = jnp.exp(cross_scores(queries, keys_in, slot_alive) - peak_row[..., None])
        return (weigh_values(raised, values_in), jnp.sum(raised, axis=-1))

    part_numer, part_total = lax.map(
        cross_partial, (block_queries, block_keys, block_values, slot_live, block_top)
    )
    cross_numer, cross_total = (
        lax.psum_scatter(
            part_numer.reshape(docs_here, length, inner_width),
            "seq",
            scatter_dimension=1,
            tiled=True,
        ),
        lax.psum_scatter(
            part_total.reshape(docs_here, length, HEADS), "seq", scatter_dimension=1, tiled=True
        ),
    )
    cross_numer = cross_numer.reshape(docs_here, rows_doc, HEADS, HEAD_DIM)
    cross_mixed = (
        (cross_numer / cross_total[..., None]).astype(jnp.bfloat16).reshape(rows_all, inner_width)
    )
    stream2 = stream1 + matmul_rows(cross_mixed, w_co)
    normed3, inverse3 = norm_parts(stream2, gain_all[2])
    normed3 = normed3.astype(jnp.bfloat16)
    cot_rows = cotangent.reshape(rows_all, model_width)
    ff_branch, grad_in, grad_out, d_normed3 = feed_forward(normed3, cot_rows, w_in, w_out)
    layer_out = (stream2 + ff_branch).reshape(docs_here, rows_doc, model_width)
    back_three, gain_grad3 = norm_back(stream2, inverse3, gain_all[2], d_normed3)
    d_stream2 = cot_rows.astype(jnp.float32) + back_three
    d_branch2 = d_stream2.astype(jnp.bfloat16)
    grad_co = matmul_outer(cross_mixed, d_branch2)
    d_mixed2 = matmul_back(d_branch2, w_co).reshape(docs_here, rows_doc, HEADS, HEAD_DIM)
    d_numer2, d_total2 = mixed_grads(d_mixed2, cross_numer, cross_total)
    numer_back, total_back = (
        lax.all_gather(
            d_numer2.reshape(docs_here, rows_doc, inner_width), "seq", axis=1, tiled=True
        ),
        lax.all_gather(d_total2, "seq", axis=1, tiled=True),
    )

    def cross_back_block(bundle):
        queries, keys_in, values_in, slot_alive, peak_row, d_numer, d_total = bundle
        raised = jnp.exp(cross_scores(queries, keys_in, slot_alive) - peak_row[..., None])
        d_scores = score_grads(raised, d_numer, d_total, values_in)
        return pair_grads(d_scores, raised, queries, keys_in, d_numer)

    part_dq, part_dk, part_dv = lax.map(
        cross_back_block,
        (
            block_queries,
            block_keys,
            block_values,
            slot_live,
            block_top,
            split_docs(numer_back.reshape(docs_here, length, HEADS, HEAD_DIM)),
            split_docs(total_back),
        ),
    )
    d_cross_q = lax.psum_scatter(
        part_dq.reshape(docs_here, length, inner_width), "seq", scatter_dimension=1, tiled=True
    )
    d_cross_q = d_cross_q.astype(jnp.bfloat16).reshape(rows_all, inner_width)
    d_enc_proj = jnp.stack(
        [
            part_dk.reshape(docs_here, slot_count, inner_width),
            part_dv.reshape(docs_here, slot_count, inner_width),
        ]
    ).astype(jnp.bfloat16)
    grad_cq = matmul_outer(normed2, d_cross_q)
    grad_ckv = jnp.einsum("bsd,cbsk->cdk", enc_in, d_enc_proj, preferred_element_type=jnp.float32)
    enc_grad = jnp.einsum("cbsk,cdk->bsd", d_enc_proj, w_ckv, preferred_element_type=jnp.float32)
    back_two, gain_grad2 = norm_back(stream1, inverse2, gain_all[1], matmul_back(d_cross_q, w_cq))
    d_stream1 = d_stream2 + back_two
    d_branch1 = d_stream1.astype(jnp.bfloat16)
    grad_so = matmul_outer(self_mixed, d_branch1)
    d_mixed1 = matmul_back(d_branch1, w_so).reshape(docs_here, rows_doc, HEADS, HEAD_DIM)
    d_numer1, d_total1 = mixed_grads(d_mixed1, self_numer, self_total)
    again_raised = jnp.exp(head_scores(self_query, keys_all, self_allowed) - self_top[..., None])
    d_scores1 = score_grads(again_raised, d_numer1, d_total1, values_all)
    d_query1, part_dk1, part_dv1 = pair_grads(
        d_scores1, again_raised, self_query, keys_all, d_numer1
    )
    d_keys1, d_values1 = (
        lax.psum_scatter(
            part_dk1.reshape(docs_here, length, inner_width), "seq", scatter_dimension=1, tiled=True
        ),
        lax.psum_scatter(
            part_dv1.reshape(docs_here, length, inner_width), "seq", scatter_dimension=1, tiled=True
        ),
    )
    d_qkv = jnp.stack(
        [
            d_query1.reshape(rows_all, inner_width),
            d_keys1.reshape(rows_all, inner_width),
            d_values1.reshape(rows_all, inner_width),
        ]
    ).astype(jnp.bfloat16)
    grad_qkv = jnp.einsum("td,ctk->cdk", normed1, d_qkv, preferred_element_type=jnp.float32)
    d_normed1 = jnp.einsum("ctk,cdk->td", d_qkv, w_qkv, preferred_element_type=jnp.float32)
    back_one, gain_grad1 = norm_back(stream, inverse1, gain_all[0], d_normed1)
    dec_grad = (d_stream1 + back_one).reshape(docs_here, rows_doc, model_width)
    gain_sum = lax.psum(jnp.stack([gain_grad1, gain_grad2, gain_grad3]), ("doc", "seq"))
    share_len = model_width // seq_ranks
    grad_gains = lax.dynamic_slice_in_dim(gain_sum, my_rank * share_len, share_len, 1)
    halfway = (
        lax.psum_scatter(grad_qkv, "doc", scatter_dimension=2, tiled=True),
        lax.psum_scatter(grad_so, "doc", scatter_dimension=0, tiled=True),
        lax.psum_scatter(grad_cq, "doc", scatter_dimension=1, tiled=True),
        lax.psum_scatter(grad_ckv, "doc", scatter_dimension=2, tiled=True),
        lax.psum_scatter(grad_co, "doc", scatter_dimension=0, tiled=True),
        lax.psum_scatter(grad_in, "doc", scatter_dimension=2, tiled=True),
        lax.psum_scatter(grad_out, "doc", scatter_dimension=0, tiled=True),
    )
    reduced = (
        lax.psum_scatter(halfway[0], "seq", scatter_dimension=1, tiled=True),
        lax.psum_scatter(halfway[1], "seq", scatter_dimension=1, tiled=True),
        lax.psum_scatter(halfway[2], "seq", scatter_dimension=0, tiled=True),
        lax.psum_scatter(halfway[3], "seq", scatter_dimension=1, tiled=True),
        lax.psum_scatter(halfway[4], "seq", scatter_dimension=1, tiled=True),
        lax.psum_scatter(halfway[5], "seq", scatter_dimension=1, tiled=True),
        lax.psum_scatter(halfway[6], "seq", scatter_dimension=1, tiled=True),
    )
    return (
        layer_out,
        dec_grad,
        enc_grad,
        reduced[0],
        reduced[1],
        reduced[2],
        reduced[3],
        reduced[4],
        reduced[5],
        reduced[6],
        grad_gains,
    )


def solution(mesh):
    return jax.shard_map(
        per_device,
        mesh=mesh,
        in_specs=(
            P("doc", "seq", None),
            P("doc", "seq", None),
            P("doc"),
            P("doc"),
            P(None, "seq", "doc"),
            P("doc", "seq"),
            P("seq", "doc"),
            P(None, "seq", "doc"),
            P("doc", "seq"),
            P(None, "seq", "doc"),
            P("doc", "seq"),
            P(None, "seq"),
            P("doc", "seq", None),
        ),
        out_specs=(
            P("doc", "seq", None),
            P("doc", "seq", None),
            P("doc", "seq", None),
            P(None, "seq", "doc"),
            P("doc", "seq"),
            P("seq", "doc"),
            P(None, "seq", "doc"),
            P("doc", "seq"),
            P(None, "seq", "doc"),
            P("doc", "seq"),
            P(None, "seq"),
        ),
        check_vma=False,
    )
```

profile of v0, /device:TPU:0, one launch (start us, length us, event | category | flops | bytes accessed | tf_op | source)
XLA Modules:
  0.0 2367.8 jit_solution(9623914491730089420)
XLA Ops:
  7.2 37.2 %all_gather.61 = bf16[3,1472,96]{2,1,0:T(8,128)(2,1)} all-gather(bf16[3,184,96]{2,1,0:T(8,128)(2,1)} %param.17), channel_id=1, replica_groups=mesh['doc'=4,'seq'=8] {'seq'}, dimensions={1}, use_global_device_ids=true | all-gather | bytes 953856 | tf_op jit(solution)/shard_map/all_gather | solution.py:117
  84.0 31.7 %all_gather.65 = bf16[96,1472]{0,1:T(8,128)(2,1)S(1)} all-gather(bf16[96,184]{0,1:T(8,128)(2,1)S(1)} %copy-done.42), channel_id=1, replica_groups=mesh['doc'=4,'seq'=8] {'seq'}, dimensions={1}, use_global_device_ids=true | all-gather | bytes 317952 | tf_op jit(solution)/shard_map/all_gather | solution.py:118
  116.7 31.7 %all_gather.69 = bf16[1472,96]{1,0:T(8,128)(2,1)S(1)} all-gather(bf16[184,96]{1,0:T(8,128)(2,1)S(1)} %copy-done.43), channel_id=1, replica_groups=mesh['doc'=4,'seq'=8] {'seq'}, dimensions={0}, use_global_device_ids=true | all-gather | bytes 317952 | tf_op jit(solution)/shard_map/all_gather | solution.py:119
  150.4 35.5 %all_gather.67 = bf16[2,1472,96]{2,0,1:T(2,128)(2,1)} all-gather(bf16[2,184,96]{2,0,1:T(2,128)(2,1)S(1)} %copy.250), channel_id=1, replica_groups=mesh['doc'=4,'seq'=8] {'seq'}, dimensions={1}, use_global_device_ids=true | all-gather | bytes 635904 | tf_op jit(solution)/shard_map/all_gather | solution.py:120
  251.3 41.5 %all-gather.27.cloned.1.call-done = bf16[2,1024,384]{2,1,0:T(8,128)(2,1)} async-done(((bf16[2,128,384]{2,1,0:T(8,128)(2,1)}), bf16[2,1024,384]{2,1,0:T(8,128)(2,1)}) %all-gather.27.cloned.1.call-update) | async-done | bytes 1572880 | tf_op jit(solution)/shard_map/all_gather | solution.py:182
  309.5 36.7 %pmax.7 = f32[2,1024,6]{1,2,0:T(8,128)S(1)} all-reduce(f32[2,1024,6]{1,2,0:T(8,128)S(1)} %get-tuple-element.180), channel_id=1, replica_groups=mesh['doc'=4,'seq'=8] {'seq'}, use_global_device_ids=true, to_apply=%region_5.6 | all-reduce | flops 12288 | bytes 98304 | tf_op jit(solution)/shard_map/pmax | solution.py:205
  382.7 33.1 %all_gather.72 = bf16[96,1472]{0,1:T(8,128)(2,1)S(1)} all-gather(bf16[96,184]{0,1:T(8,128)(2,1)S(1)} %copy-done.44), channel_id=1, replica_groups=mesh['doc'=4,'seq'=8] {'seq'}, dimensions={1}, use_global_device_ids=true | all-gather | bytes 317952 | tf_op jit(solution)/shard_map/all_gather | solution.py:121
  448.9 56.9 %reduce-scatter.46.cloned.1.call-done = f32[128,12]{1,0:T(8,128)} async-done(((f32[1024,12]{1,0:T(8,128)}), f32[128,12]{1,0:T(8,128)}) %reduce-scatter.46.cloned.1.call-update) | async-done | bytes 6160
  510.2 72.5 %reduce-scatter.24.cloned.1.call-done = f32[2,128,384]{2,1,0:T(8,128)} async-done(((f32[2,1024,384]{2,1,0:T(8,128)}), f32[2,128,384]{2,1,0:T(8,128)}) %reduce-scatter.24.cloned.1.call-update) | async-done | bytes 393232 | tf_op jit(solution)/shard_map/reduce_scatter | solution.py:217
  605.9 67.4 %all-gather.37.cloned.1.call-done = bf16[3584,1472]{0,1:T(8,128)(2,1)} async-done(((bf16[896,1472]{0,1:T(8,128)(2,1)}), bf16[3584,1472]{0,1:T(8,128)(2,1)}) %all-gather.37.cloned.1.call-update) | async-done | bytes 10551312 | tf_op jit(solution)/shard_map/all_gather | solution.py:133
  682.6 124.4 %all-gather.33.cloned.1.call-done = bf16[2,1472,3584]{2,1,0:T(8,128)(2,1)} async-done(((bf16[2,1472,896]{2,1,0:T(8,128)(2,1)}), bf16[2,1472,3584]{2,1,0:T(8,128)(2,1)}) %all-gather.33.cloned.1.call-update) | async-done | bytes 21102608 | tf_op jit(solution)/shard_map/all_gather | solution.py:132
  914.0 72.6 %reduce-scatter.26.cloned.1.call-done = f32[2,128,384]{2,1,0:T(8,128)} async-done(((f32[2,1024,384]{2,1,0:T(8,128)}), f32[2,128,384]{2,1,0:T(8,128)}) %reduce-scatter.26.cloned.1.call-update) | async-done | bytes 393232 | tf_op jit(solution)/shard_map/reduce_scatter | solution.py:268
  1078.0 75.7 %reduce-scatter.28.cloned.1.call-done = f32[2,128,384]{1,2,0:T(8,128)} async-done(((f32[2,1024,384]{1,2,0:T(8,128)}), f32[2,128,384]{1,2,0:T(8,128)}) %reduce-scatter.28.cloned.1.call-update) | async-done | bytes 393232 | tf_op jit(solution)/shard_map/reduce_scatter | solution.py:293
  1218.3 31.5 %all-reduce.10.cloned.1.call-done = f32[2,1472,384]{1,0,2:T(2,128)} async-done(((f32[2,1472,384]{1,0,2:T(2,128)}), f32[2,1472,384]{1,0,2:T(2,128)}) %all-reduce.10.cloned.1.call-update) | async-done | bytes 4522000
  1285.2 35.4 %reduce-scatter.36.cloned.1.call-done = f32[1472,96]{0,1:T(8,128)} async-done(((f32[1472,384]{0,1:T(8,128)}), f32[1472,96]{0,1:T(8,128)}) %reduce-scatter.36.cloned.1.call-update) | async-done | bytes 565264 | tf_op jit(solution)/shard_map/reduce_scatter | solution.py:317
  1320.6 35.4 %reduce-scatter.34.cloned.1.call-done = f32[96,1472]{1,0:T(8,128)} async-done(((f32[384,1472]{1,0:T(8,128)}), f32[96,1472]{1,0:T(8,128)}) %reduce-scatter.34.cloned.1.call-update) | async-done | bytes 565264 | tf_op jit(solution)/shard_map/reduce_scatter | solution.py:316
  1356.0 65.4 %reduce-scatter.48.cloned.1.call-done = f32[96,4416]{1,0:T(8,128)} async-done(((f32[384,4416]{1,0:T(8,128)}), f32[96,4416]{1,0:T(8,128)}) %reduce-scatter.48.cloned.1.call-update) | async-done | bytes 1695760
  1430.1 145.0 %reduce-scatter.44.cloned.1.call-done = f32[896,1472]{0,1:T(8,128)} async-done(((f32[3584,1472]{0,1:T(8,128)}), f32[896,1472]{0,1:T(8,128)}) %reduce-scatter.44.cloned.1.call-update) | async-done | bytes 5275664 | tf_op jit(solution)/shard_map/reduce_scatter | solution.py:321
  1575.3 286.5 %reduce-scatter.40.cloned.1.call-done = f32[2,1472,896]{2,1,0:T(8,128)} async-done(((f32[2,1472,3584]{2,1,0:T(8,128)}), f32[2,1472,896]{2,1,0:T(8,128)}) %reduce-scatter.40.cloned.1.call-update) | async-done | bytes 10551312 | tf_op jit(solution)/shard_map/reduce_scatter | solution.py:320
  1882.1 41.9 %psum.7 = f32[3,1472]{1,0:T(4,128)S(1)} all-reduce(f32[3,1472]{1,0:T(4,128)S(1)} %pad_maximum_fusion.9), channel_id=1, replica_groups=mesh['doc'=4,'seq'=8] {'doc','seq'}, use_global_device_ids=true, to_apply=%region_35.36 | all-reduce | flops 4416 | bytes 35328 | tf_op jit(solution)/shard_map/psum | solution.py:311
  1928.2 71.4 %all-reduce.12.cloned.1.call-done = (f32[96,1472]{1,0:T(8,128)}, f32[1472,96]{0,1:T(8,128)}, f32[2,1472,96]{2,0,1:T(2,128)}, f32[96,1472]{1,0:T(8,128)}) async-done(((f32[96,1472]{1,0:T(8,128)}, f32[1472,96]{0,1:T(8,128)}, f32[2,1472,96]{2,0,1:T(2,128)}, f32[96,1472]{1,0:T(8,128)}), (f32[96,1472]{1,0:T(8,128)}, f32[1472,96]{0,1:T(8,128)}, f32[2,1472,96]{2,0,1:T(2,128)}, ...) | async-done | bytes 2826256
  2005.6 66.7 %reduce-scatter.32.cloned.1.call-done = f32[3,184,96]{2,1,0:T(8,128)} async-done(((f32[3,1472,96]{2,1,0:T(8,128)}), f32[3,184,96]{2,1,0:T(8,128)}) %reduce-scatter.32.cloned.1.call-update) | async-done | bytes 211984 | tf_op jit(solution)/shard_map/reduce_scatter | solution.py:324
  2072.3 105.6 %reduce-scatter.50.cloned.1.call-done = f32[896,184]{0,1:T(8,128)} async-done(((f32[896,1472]{0,1:T(8,128)}), f32[896,184]{0,1:T(8,128)}) %reduce-scatter.50.cloned.1.call-update) | async-done | bytes 659472
  2177.8 183.2 %reduce-scatter.42.cloned.1.call-done = f32[2,184,896]{2,1,0:T(8,128)} async-done(((f32[2,1472,896]{2,1,0:T(8,128)}), f32[2,184,896]{2,1,0:T(8,128)}) %reduce-scatter.42.cloned.1.call-update) | async-done | bytes 1318928 | tf_op jit(solution)/shard_map/reduce_scatter | solution.py:329
  (323 shorter events, 566.4 us)
Async XLA Ops:
  46.8 144.5 %all-gather.19.cloned.1.call-start = ((), (), s32[]{:S(2)}) async-start(), calls=%async_computation.16 | async-start | bytes 1769472 | tf_op jit(solution)/shard_map/all_gather | solution.py:151
  83.9 120.7 %all-gather.21.cloned.1.call-start = ((), (), s32[]{:S(2)}) async-start(), calls=%async_computation.17 | async-start | bytes 1474560 | tf_op jit(solution)/shard_map/all_gather | solution.py:128
  223.1 193.6 %all-gather.35.cloned.1.call-start = ((), (), s32[]{:S(2)}) async-start(), calls=%async_computation.25 | async-start | bytes 2967552 | tf_op jit(solution)/shard_map/all_gather | solution.py:123
  223.8 216.4 %all-gather.31.cloned.1.call-start = ((), (), s32[]{:S(2)}) async-start(), calls=%async_computation.23 | async-start | bytes 5935104 | tf_op jit(solution)/shard_map/all_gather | solution.py:122
  224.6 281.2 %reduce-scatter.46.cloned.1.call-start = ((), (), s32[]{:S(2)}) async-start(), calls=%async_computation.38 | async-start | bytes 589824
  363.5 219.2 %reduce-scatter.24.cloned.1.call-start = ((), (), s32[]{:S(2)}) async-start(), calls=%async_computation.21 | async-start | bytes 3538944 | tf_op jit(solution)/shard_map/reduce_scatter | solution.py:217
  381.9 219.3 %all-gather.29.cloned.1.call-start = ((), (), s32[]{:S(2)}) async-start(), calls=%async_computation.22 | async-start | bytes 1474560 | tf_op jit(solution)/shard_map/all_gather | solution.py:131
  416.7 256.6 %all-gather.37.cloned.1.call-start = ((), (), s32[]{:S(2)}) async-start(), calls=%async_computation.26 | async-start | bytes 13189120 | tf_op jit(solution)/shard_map/all_gather | solution.py:133
  417.4 389.5 %all-gather.33.cloned.1.call-start = ((), (), s32[]{:S(2)}) async-start(), calls=%async_computation.24 | async-start | bytes 26378240 | tf_op jit(solution)/shard_map/all_gather | solution.py:132
  440.3 445.9 %all-gather.39.cloned.1.call-start = ((), (), s32[]{:S(2)}) async-start(), calls=%async_computation.27 | async-start | bytes 1769472 | tf_op jit(solution)/shard_map/all_gather | solution.py:244
  841.4 145.1 %reduce-scatter.26.cloned.1.call-start = ((), (), s32[]{:S(2)}) async-start(), calls=%async_computation.28 | async-start | bytes 3538944 | tf_op jit(solution)/shard_map/reduce_scatter | solution.py:268
  914.0 162.2 %reduce-scatter.30.cloned.1.call-start = ((), (), s32[]{:S(2)}) async-start(), calls=%async_computation.30 | async-start | bytes 3538944 | tf_op jit(solution)/shard_map/reduce_scatter | solution.py:296
  1001.9 151.8 %reduce-scatter.28.cloned.1.call-start = ((), (), s32[]{:S(2)}) async-start(), calls=%async_computation.29 | async-start | bytes 3538944 | tf_op jit(solution)/shard_map/reduce_scatter | solution.py:293
  1012.9 236.9 %all-reduce.10.cloned.1.call-start = ((), (), s32[]{:S(2)}) async-start(), calls=%async_computation.40 | async-start | bytes 9437184
  1053.9 231.3 %reduce-scatter.38.cloned.1.call-start = ((), (), s32[]{:S(2)}) async-start(), calls=%async_computation.34 | async-start | bytes 2949120 | tf_op jit(solution)/shard_map/reduce_scatter | solution.py:319
  1058.1 262.4 %reduce-scatter.36.cloned.1.call-start = ((), (), s32[]{:S(2)}) async-start(), calls=%async_computation.33 | async-start | bytes 2949120 | tf_op jit(solution)/shard_map/reduce_scatter | solution.py:317
  1062.3 293.6 %reduce-scatter.34.cloned.1.call-start = ((), (), s32[]{:S(2)}) async-start(), calls=%async_computation.32 | async-start | bytes 2949120 | tf_op jit(solution)/shard_map/reduce_scatter | solution.py:316
  1066.6 354.8 %reduce-scatter.48.cloned.1.call-start = ((), (), s32[]{:S(2)}) async-start(), calls=%async_computation.39 | async-start | bytes 8601600
  1185.1 390.0 %reduce-scatter.44.cloned.1.call-start = ((), (), s32[]{:S(2)}) async-start(), calls=%async_computation.37 | async-start | bytes 26378240 | tf_op jit(solution)/shard_map/reduce_scatter | solution.py:321
  1197.0 664.9 %reduce-scatter.40.cloned.1.call-start = ((), (), s32[]{:S(2)}) async-start(), calls=%async_computation.35 | async-start | bytes 52756480 | tf_op jit(solution)/shard_map/reduce_scatter | solution.py:320
  1216.4 783.2 %all-reduce.12.cloned.1.call-start = ((), (), s32[]{:S(2)}) async-start(), calls=%async_computation.42 | async-start | bytes 6553600
  1356.0 716.3 %reduce-scatter.32.cloned.1.call-start = ((), (), s32[]{:S(2)}) async-start(), calls=%async_computation.31 | async-start | bytes 2543616 | tf_op jit(solution)/shard_map/reduce_scatter | solution.py:324
  1430.0 747.8 %reduce-scatter.50.cloned.1.call-start = ((), (), s32[]{:S(2)}) async-start(), calls=%async_computation.41 | async-start | bytes 5935104
  1575.1 786.0 %reduce-scatter.42.cloned.1.call-start = ((), (), s32[]{:S(2)}) async-start(), calls=%async_computation.36 | async-start | bytes 11870208 | tf_op jit(solution)/shard_map/reduce_scatter | solution.py:329
  (68 other events, 1744.8 us)
Sparse Core Ops, SparseCore 0:
  83.3 46.3 all-gather.18
  131.9 50.0 all-gather.16
  248.5 44.1 all-gather.26
  294.9 54.2 all-gather.34
  351.5 88.7 all-gather.30
  444.0 61.7 reduce-scatter.45
  509.4 73.2 reduce-scatter.23
  602.8 70.4 all-gather.36
  674.7 132.1 all-gather.32
  841.6 44.6 all-gather.38
  914.1 72.4 reduce-scatter.25
  1002.0 74.1 reduce-scatter.29
  1079.7 74.0 reduce-scatter.27
  1156.7 93.0 all-reduce.9
  1252.2 32.9 reduce-scatter.37
  1287.7 32.8 reduce-scatter.35
  1323.1 32.8 reduce-scatter.33
  1358.5 62.8 reduce-scatter.47
  1423.9 151.1 reduce-scatter.43
  1577.6 284.1 reduce-scatter.39
  1865.7 133.8 all-reduce.11
  2003.6 68.6 reduce-scatter.31
  2076.3 101.4 reduce-scatter.49
  2181.9 179.0 reduce-scatter.41
  (5 shorter events, 105.5 us)
where the time goes:
time: 2380 us; the launch traced here: 2370 us
  waiting for transfers between devices  1670 us (70%)
  blocking collectives  295 us (12%)
  matrix products  228 us (10%)
  local copies, waits for them, and re-layouts  120 us (5%)
  other arithmetic  29.1 us (1%)
    unnamed x34, waiting for transfers between devices  334 us
    reduce_scatter x1, waiting for transfers between devices, per_device(): lax.psum_scatter(grad_in, 'doc', scatter_dimension=2, tiled=True)  287 us
    reduce_scatter x1, waiting for transfers between devices, per_device(): lax.psum_scatter(halfway[5], 'seq', scatter_dimension=1, tiled=True)  183 us
    reduce_scatter x1, waiting for transfers between devices, per_device(): lax.psum_scatter(grad_out, 'doc', scatter_dimension=0, tiled=True)  145 us
    all_gather x1, waiting for transfers between devices, per_device(): lax.all_gather(by_rows[5], 'doc', axis=2, tiled=True)  124 us
    reduce_scatter x1, waiting for transfers between devices, per_device(): lax.psum_scatter(part_dk1.reshape(docs_here, length, inner_width), 'seq',...  75.7 us
    reduce_scatter x1, waiting for transfers between devices, per_device(): lax.psum_scatter(part_dq.reshape(docs_here, length, inner_width), 'seq',...  72.6 us
    reduce_scatter x1, waiting for transfers between devices, per_device(): lax.psum_scatter(part_numer.reshape(docs_here, length, inner_width), 'seq...  72.5 us
  transfers between devices with their start and end apart: 29, of which 25 were waited for; matrix products, arithmetic and copies ran while one was open for 12% of the time, Pallas kernels for 0%

commit v1 on v0

--- a/solution.py
+++ b/solution.py
@@ -1,6 +1,10 @@
+import functools
+
 import jax
 import jax.numpy as jnp
 from jax import lax
+from jax.experimental import pallas as pl
+from jax.experimental.pallas import tpu as pltpu
 from jax.sharding import PartitionSpec as P
 
 HEADS = 6
@@ -344,9 +348,528 @@
     )
 
 
+FOLD = 2
+
+
+def _masked_rows(is_second, shape, axis):
+    index = lax.broadcasted_iota(jnp.int32, shape, axis)
+    return (index >= HEAD_DIM) == is_second
+
+
+def _transposed(array, dtype):
+    return jnp.transpose(array.astype(jnp.float32)).astype(dtype)
+
+
+def _score_mask(chunk, size, block, count, width, causal):
+    slot = chunk * size + lax.broadcasted_iota(jnp.int32, (size, width), 0)
+    live = slot < count
+    if causal:
+        query = block * width + lax.broadcasted_iota(jnp.int32, (size, width), 1)
+        live = live & (slot <= query)
+    return live
+
+
+def _steps(info_ref, rows, wide):
+    blocks = rows // wide
+    half = blocks // 2
+    return blocks, half, blocks + half
+
+
+def _chunk_count(count, block, wide, size, causal):
+    chunks = (count + size - 1) // size
+    if causal:
+        chunks = jnp.minimum(chunks, ((block + 1) * wide + size - 1) // size)
+    return chunks
+
+
+def attend_kernel(wide, size, causal, packed, info_ref, *refs):
+    if packed:
+        qkv_ref, att_ref, mix_ref, stat_ref, vt_ref, score_ref = refs
+        lanes = 2 * HEAD_DIM
+        q_ref, k_ref, v_ref = (qkv_ref.at[:, pl.ds(i * lanes, lanes)] for i in range(3))
+    else:
+        q_ref, kv_ref, att_ref, mix_ref, stat_ref, vt_ref, score_ref = refs
+        lanes = 2 * HEAD_DIM
+        k_ref, v_ref = (kv_ref.at[:, pl.ds(i * lanes, lanes)] for i in range(2))
+    rows = q_ref.shape[0]
+    slots = k_ref.shape[0]
+    count = info_ref[0]
+    part = info_ref[1]
+    blocks, half, total_steps = _steps(info_ref, rows, wide)
+
+    def flip(c, carry):
+        at = pl.multiple_of(c * size, size)
+        vt_ref[:, pl.ds(at, size)] = _transposed(v_ref[pl.ds(at, size), :], jnp.bfloat16)
+        return carry
+
+    lax.fori_loop(0, slots // size, flip, 0)
+
+    def step(i, carry):
+        second = i >= blocks
+        block = jnp.where(second, half * part + i - blocks, i)
+        at = pl.multiple_of(block * wide, wide)
+        mine = _masked_rows(second, (lanes, wide), 0)
+        queries = jnp.where(mine, jnp.transpose(q_ref[pl.ds(at, wide), :].astype(jnp.float32)), 0.0)
+        queries = queries.astype(jnp.bfloat16)
+        chunks = _chunk_count(count, block, wide, size, causal)
+
+        def scores(c, top):
+            spot = pl.multiple_of(c * size, size)
+            s = jnp.dot(k_ref[pl.ds(spot, size), :], queries, preferred_element_type=jnp.float32)
+            s = jnp.where(_score_mask(c, size, block, count, wide, causal), s, NEGATIVE)
+            score_ref[pl.ds(spot, size), :] = s
+            return jnp.maximum(top, jnp.max(s.reshape(size // 8, 8, wide), axis=0))
+
+        top = lax.fori_loop(0, chunks, scores, jnp.full((8, wide), NEGATIVE, jnp.float32))
+        top = jnp.max(top, axis=0, keepdims=True)
+
+        def weigh(c, carry):
+            total, numer = carry
+            spot = pl.multiple_of(c * size, size)
+            e = jnp.exp(score_ref[pl.ds(spot, size), :] - top)
+            total = total + jnp.sum(e.reshape(size // 8, 8, wide), axis=0)
+            numer = numer + jnp.dot(
+                vt_ref[:, pl.ds(spot, size)], e.astype(jnp.bfloat16), preferred_element_type=jnp.float32
+            )
+            return total, numer
+
+        total, numer = lax.fori_loop(
+            0,
+            chunks,
+            weigh,
+            (jnp.zeros((8, wide), jnp.float32), jnp.zeros((lanes, wide), jnp.float32)),
+        )
+        total = jnp.sum(total, axis=0, keepdims=True)
+        mixed = jnp.where(mine, numer / total, 0.0)
+        back = jnp.transpose(mixed)
+
+        @pl.when(jnp.logical_not(second))
+        def _():
+            att_ref[pl.ds(at, wide), :] = back.astype(jnp.bfloat16)
+            mix_ref[:, pl.ds(at, wide)] = mixed
+            stat_ref[0:1, pl.ds(at, wide)] = top
+            stat_ref[1:2, pl.ds(at, wide)] = total
+
+        @pl.when(second)
+        def _():
+            kept = att_ref[pl.ds(at, wide), :].astype(jnp.float32)
+            att_ref[pl.ds(at, wide), :] = (kept + back).astype(jnp.bfloat16)
+            mix_ref[:, pl.ds(at, wide)] = mix_ref[:, pl.ds(at, wide)] + mixed
+            stat_ref[2:3, pl.ds(at, wide)] = top
+            stat_ref[3:4, pl.ds(at, wide)] = total
+
+        return carry
+
+    lax.fori_loop(0, total_steps, step, 0)
+
+
+def attend_back_kernel(wide, size, causal, packed, info_ref, *refs):
+    lanes = 2 * HEAD_DIM
+    if packed:
+        qkv_ref, dmix_ref, mix_ref, stat_ref, out_ref, kt_ref, dk_ref, dv_ref, dq_ref = refs
+        q_ref, k_ref, v_ref = (qkv_ref.at[:, pl.ds(i * lanes, lanes)] for i in range(3))
+    else:
+        q_ref, kv_ref, dmix_ref, mix_ref, stat_ref, dqo_ref, out_ref, kt_ref, dk_ref, dv_ref, dq_ref = refs
+        k_ref, v_ref = (kv_ref.at[:, pl.ds(i * lanes, lanes)] for i in range(2))
+    rows = q_ref.shape[0]
+    slots = k_ref.shape[0]
+    count = info_ref[0]
+    part = info_ref[1]
+    blocks, half, total_steps = _steps(info_ref, rows, wide)
+
+    def flip(c, carry):
+        at = pl.multiple_of(c * size, size)
+        kt_ref[:, pl.ds(at, size)] = _transposed(k_ref[pl.ds(at, size), :], jnp.bfloat16)
+        dk_ref[pl.ds(at, size), :] = jnp.zeros((size, lanes), jnp.float32)
+        dv_ref[pl.ds(at, size), :] = jnp.zeros((size, lanes), jnp.float32)
+        return carry
+
+    lax.fori_loop(0, slots // size, flip, 0)
+
+    def step(i, carry):
+        second = i >= blocks
+        block = jnp.where(second, half * part + i - blocks, i)
+        at = pl.multiple_of(block * wide, wide)
+        mine = _masked_rows(second, (lanes, wide), 0)
+        mine_lanes = _masked_rows(second, (wide, lanes), 1)
+        q_plain = q_ref[pl.ds(at, wide), :].astype(jnp.float32)
+        q_rows = jnp.where(mine_lanes, q_plain, 0.0).astype(jnp.bfloat16)
+        q_cols = jnp.where(mine, jnp.transpose(q_plain), 0.0).astype(jnp.bfloat16)
+        dmix = jnp.where(mine, jnp.transpose(dmix_ref[pl.ds(at, wide), :].astype(jnp.float32)), 0.0)
+        stats = stat_ref[:, pl.ds(at, wide)]
+        top = jnp.where(second, stats[2:3, :], stats[0:1, :])
+        total = jnp.where(second, stats[3:4, :], stats[1:2, :])
+        dn_wide = dmix / total
+        dn_cols = dn_wide.astype(jnp.bfloat16)
+        dn_rows = jnp.transpose(dn_wide).astype(jnp.bfloat16)
+        mixed = mix_ref[:, pl.ds(at, wide)]
+        dtotal = -jnp.sum(dmix * mixed, axis=0, keepdims=True) / total
+        dtotal = dtotal.astype(jnp.bfloat16).astype(jnp.float32)
+        chunks = _chunk_count(count, block, wide, size, causal)
+
+        def one(c, dq):
+            spot = pl.multiple_of(c * size, size)
+            s = jnp.dot(k_ref[pl.ds(spot, size), :], q_cols, preferred_element_type=jnp.float32)
+            s = jnp.where(_score_mask(c, size, block, count, wide, causal), s, NEGATIVE)
+            e = jnp.exp(s - top)
+            through = jnp.dot(v_ref[pl.ds(spot, size), :], dn_cols, preferred_element_type=jnp.float32)
+            ds = (e * (through + dtotal)).astype(jnp.bfloat16)
+            dv_ref[pl.ds(spot, size), :] = dv_ref[pl.ds(spot, size), :] + jnp.dot(
+                e.astype(jnp.bfloat16), dn_rows, preferred_element_type=jnp.float32
+            )
+            dk_ref[pl.ds(spot, size), :] = dk_ref[pl.ds(spot, size), :] + jnp.dot(
+                ds, q_rows, preferred_element_type=jnp.float32
+            )
+            return dq + jnp.dot(kt_ref[:, pl.ds(spot, size)], ds, preferred_element_type=jnp.float32)
+
+        dq = lax.fori_loop(0, chunks, one, jnp.zeros((lanes, wide), jnp.float32))
+        back = jnp.transpose(jnp.where(mine, dq, 0.0))
+
+        @pl.when(jnp.logical_not(second))
+        def _():
+            dq_ref[pl.ds(at, wide), :] = back
+
+        @pl.when(second)
+        def _():
+            dq_ref[pl.ds(at, wide), :] = dq_ref[pl.ds(at, wide), :] + back
+
+        return carry
+
+    lax.fori_loop(0, total_steps, step, 0)
+    shift = lanes if packed else 0
+    if packed:
+        out_ref[:, 0:lanes] = dq_ref[...].astype(jnp.bfloat16)
+    else:
+        dqo_ref[...] = dq_ref[...].astype(jnp.bfloat16)
+
+    def emit(c, carry):
+        at = pl.multiple_of(c * size, size)
+        out_ref[pl.ds(at, size), shift : shift + lanes] = dk_ref[pl.ds(at, size), :].astype(jnp.bfloat16)
+        out_ref[pl.ds(at, size), shift + lanes : shift + 2 * lanes] = dv_ref[pl.ds(at, size), :].astype(
+            jnp.bfloat16
+        )
+        return carry
+
+    lax.fori_loop(0, slots // size, emit, 0)
+
+
+def attention(info, parts, causal):
+    lanes = 2 * HEAD_DIM
+    rows = parts[0].shape[0]
+    slots = parts[-1].shape[0]
+    wide = min(256, rows // 2)
+    size = min(256 if causal else 512, slots)
+    work = rows * slots * lanes * (2 if causal else 4)
+    return pl.pallas_call(
+        functools.partial(attend_kernel, wide, size, causal, len(parts) == 1),
+        name="attend_self" if causal else "attend_cross",
+        out_shape=(
+            jax.ShapeDtypeStruct((rows, lanes), jnp.bfloat16),
+            jax.ShapeDtypeStruct((lanes, rows), jnp.float32),
+            jax.ShapeDtypeStruct((8, rows), jnp.float32),
+        ),
+        in_specs=[pl.BlockSpec(memory_space=pltpu.SMEM)]
+        + [pl.BlockSpec(memory_space=pltpu.VMEM)] * len(parts),
+        out_specs=(pl.BlockSpec(memory_space=pltpu.VMEM),) * 3,
+        scratch_shapes=[
+            pltpu.VMEM((lanes, slots), jnp.bfloat16),
+            pltpu.VMEM((slots, wide), jnp.float32),
+        ],
+        compiler_params=pltpu.CompilerParams(vmem_limit_bytes=32 * 1024 * 1024),
+        cost_estimate=pl.CostEstimate(flops=work, bytes_accessed=slots * lanes * 8, transcendentals=rows * slots),
+    )(info, *parts)
+
+
+def attention_back(info, parts, dmix, mixed, stats, causal):
+    lanes = 2 * HEAD_DIM
+    rows = parts[0].shape[0]
+    slots = parts[-1].shape[0]
+    wide = min(256, rows // 2)
+    size = min(256 if causal else 512, slots)
+    work = rows * slots * lanes * (5 if causal else 10)
+    packed = len(parts) == 1
+    outs = (jax.ShapeDtypeStruct((slots, (3 if packed else 2) * lanes), jnp.bfloat16),)
+    if not packed:
+        outs = (jax.ShapeDtypeStruct((rows, lanes), jnp.bfloat16),) + outs
+    return pl.pallas_call(
+        functools.partial(attend_back_kernel, wide, size, causal, packed),
+        name="attend_self_back" if causal else "attend_cross_back",
+        out_shape=outs,
+        in_specs=[pl.BlockSpec(memory_space=pltpu.SMEM)]
+        + [pl.BlockSpec(memory_space=pltpu.VMEM)] * (len(parts) + 3),
+        out_specs=(pl.BlockSpec(memory_space=pltpu.VMEM),) * len(outs),
+        scratch_shapes=[
+            pltpu.VMEM((lanes, slots), jnp.bfloat16),
+            pltpu.VMEM((slots, lanes), jnp.float32),
+            pltpu.VMEM((slots, lanes), jnp.float32),
+            pltpu.VMEM((rows, lanes), jnp.float32),
+        ],
+        compiler_params=pltpu.CompilerParams(vmem_limit_bytes=40 * 1024 * 1024),
+        cost_estimate=pl.CostEstimate(flops=work, bytes_accessed=slots * lanes * 8, transcendentals=rows * slots),
+    )(info, *parts, dmix, mixed, stats)
+
+
+def spread_heads(array):
+    d = HEAD_DIM
+    pick = lambda h: array[..., h * d : (h + 1) * d]
+    return jnp.stack(
+        [jnp.concatenate([pick(a), pick(b)], axis=-1) for a, b in ((0, 1), (2, 1), (3, 4), (5, 4))]
+    )
+
+
+def merge_heads(array):
+    d = HEAD_DIM
+    wide = array.astype(jnp.float32)
+    first = [wide[j, ..., :d] for j in range(4)]
+    shared = [wide[j, ..., d:] + wide[j + 1, ..., d:] for j in (0, 2)]
+    return jnp.concatenate(
+        [first[0], shared[0], first[1], first[2], shared[1], first[3]], axis=-1
+    ).astype(jnp.bfloat16)
+
+
+def by_document(array, x_rank, swap):
+    own = lax.dynamic_index_in_dim(array, x_rank, 0, False)
+    other = lax.ppermute(lax.dynamic_index_in_dim(array, 1 - x_rank, 0, False), "seq", swap)
+    first = x_rank == 0
+    return jnp.concatenate([jnp.where(first, own, other), jnp.where(first, other, own)], axis=0)
+
+
+def by_position(array, x_rank, swap):
+    pair = array.reshape((2, array.shape[0] // 2) + array.shape[1:])
+    own = lax.dynamic_index_in_dim(pair, x_rank, 0, False)
+    other = lax.ppermute(lax.dynamic_index_in_dim(pair, 1 - x_rank, 0, False), "seq", swap)
+    first = x_rank == 0
+    return jnp.stack([jnp.where(first, own, other), jnp.where(first, other, own)])
+
+
+def exchange_z(array, z_rank, shifts):
+    count = array.shape[0]
+    arrived = [
+        lax.ppermute(lax.dynamic_index_in_dim(array, (z_rank + k) % count, 0, False), "seq", shifts[k])
+        for k in range(1, count)
+    ]
+    out = array
+    for k in range(1, count):
+        out = lax.dynamic_update_index_in_dim(out, arrived[k - 1], (z_rank - k) % count, 0)
+    return out
+
+
+def gather_doc(array, pairs_core, pairs_y):
+    across = lax.ppermute(array, "doc", pairs_y)
+    beside = lax.ppermute(array, "doc", pairs_core)
+    far = lax.ppermute(across, "doc", pairs_core)
+    return jnp.concatenate([array, beside, across, far], axis=0)
+
+
+def scatter_doc(array, pairs_core, pairs_y):
+    n = array.shape[0] // 4
+    low = array.astype(jnp.bfloat16)
+    share = lax.ppermute(
+        jnp.concatenate([low[n : 2 * n], low[3 * n :]], axis=0), "doc", pairs_core
+    ).astype(jnp.float32)
+    mine = array[:n] + share[:n]
+    across = (array[2 * n : 3 * n] + share[n:]).astype(jnp.bfloat16)
+    return mine + lax.ppermute(across, "doc", pairs_y).astype(jnp.float32)
+
+
+def by_heads(
+    dec_in,
+    enc_in,
+    tgt_len,
+    enc_len,
+    self_qkv,
+    self_out,
+    cross_q,
+    cross_kv,
+    cross_out,
+    ff_in,
+    ff_out,
+    gains,
+    cotangent,
+):
+    f32, bf16 = jnp.float32, jnp.bfloat16
+    docs_here, rows_doc, width = dec_in.shape
+    slots_doc = enc_in.shape[1]
+    doc_ranks, seq_ranks = lax.axis_size("doc"), lax.axis_size("seq")
+    seq_rank = lax.axis_index("seq")
+    z_rank, x_rank = seq_rank // 2, seq_rank % 2
+    swap = [(i, i ^ 1) for i in range(seq_ranks)]
+    shifts = [[(i, (i + 2 * k) % seq_ranks) for i in range(seq_ranks)] for k in range(seq_ranks // 2)]
+    pairs_core = [(i, i ^ 1) for i in range(doc_ranks)]
+    pairs_y = [(i, i ^ 2) for i in range(doc_ranks)]
+    inner = HEADS * HEAD_DIM
+    share = inner // doc_ranks
+    depth = width // seq_ranks
+    rows = docs_here * rows_doc
+
+    small = jnp.concatenate(
+        [self_qkv[0], self_qkv[1], self_qkv[2], cross_q, cross_kv[0], cross_kv[1], self_out.T, cross_out.T],
+        axis=1,
+    )
+    every = lax.all_gather(small, ("doc", "seq"), axis=0, tiled=True).reshape(doc_ranks, width, 8 * share)
+    w_qkv = every[:, :, : 3 * share]
+    w_cq = every[:, :, 3 * share : 4 * share]
+    w_ckv = every[:, :, 4 * share : 6 * share]
+    w_so = every[:, :, 6 * share : 7 * share]
+    w_co = every[:, :, 7 * share :]
+    gain_all = lax.all_gather(gains, "seq", axis=1, tiled=True).astype(f32)
+    ff_mine = jnp.concatenate([ff_in[0], ff_in[1], ff_out.T], axis=1)
+    ff_all = lax.all_gather(ff_mine, "seq", axis=0, tiled=True)
+    hidden_here = ff_in.shape[2]
+    w_gate, w_up = ff_all[:, :hidden_here], ff_all[:, hidden_here : 2 * hidden_here]
+    w_down = ff_all[:, 2 * hidden_here :]
+
+    def project(rows_in, weight, parts):
+        out = jnp.einsum("td,edk->etk", rows_in, weight, preferred_element_type=f32).astype(bf16)
+        return [
+            jnp.concatenate([out[e, :, i * share : (i + 1) * share] for e in range(doc_ranks)], axis=-1)
+            for i in range(parts)
+        ]
+
+    def lift(inner_in, weight):
+        split = inner_in.reshape(inner_in.shape[0], doc_ranks, share)
+        return jnp.einsum("tek,edk->td", split, weight, preferred_element_type=f32)
+
+    def outer(rows_in, inner_in):
+        split = inner_in.reshape(inner_in.shape[0], doc_ranks, share)
+        return jnp.einsum("td,tek->edk", rows_in, split, preferred_element_type=f32).astype(bf16)
+
+    info_self = jnp.stack([lax.dynamic_index_in_dim(tgt_len, x_rank, 0, False), z_rank % 2])
+    info_cross = jnp.stack([lax.dynamic_index_in_dim(enc_len, x_rank, 0, False), z_rank % 2])
+
+    stream = by_document(dec_in, x_rank, swap).astype(f32)
+    cot = by_document(cotangent, x_rank, swap)
+    cot_all = gather_doc(cot, pairs_core, pairs_y)
+    normed1, inverse1 = norm_parts(stream, gain_all[0])
+    normed1 = normed1.astype(bf16)
+    qkv = jnp.concatenate([spread_heads(p) for p in project(normed1, w_qkv, 3)], axis=-1)
+    qkv_heads = exchange_z(qkv, z_rank, shifts).reshape(4 * rows, 6 * HEAD_DIM)
+    att1, mix1, stat1 = attention(info_self, (qkv_heads,), True)
+    att1 = merge_heads(exchange_z(att1.reshape(4, rows, 2 * HEAD_DIM), z_rank, shifts))
+    stream1 = stream + lift(att1, w_so)
+    normed2, inverse2 = norm_parts(stream1, gain_all[1])
+    normed2 = normed2.astype(bf16)
+    (cq,) = project(normed2, w_cq, 1)
+    cq_heads = exchange_z(spread_heads(cq), z_rank, shifts).reshape(4 * rows, 2 * HEAD_DIM)
+
+    enc_rows = enc_in.reshape(docs_here * slots_doc, width)
+    ckv = jnp.concatenate([spread_heads(p) for p in project(enc_rows, w_ckv, 2)], axis=-1)
+    ckv = ckv.reshape(4, docs_here, slots_doc, 4 * HEAD_DIM).transpose(1, 2, 0, 3)
+    ckv = by_document(ckv, x_rank, swap).transpose(1, 0, 2)
+    ckv_heads = exchange_z(ckv, z_rank, shifts).reshape(4 * docs_here * slots_doc, 4 * HEAD_DIM)
+
+    att2, mix2, stat2 = attention(info_cross, (cq_heads, ckv_heads), False)
+    att2 = merge_heads(exchange_z(att2.reshape(4, rows, 2 * HEAD_DIM), z_rank, shifts))
+    stream2 = stream1 + lift(att2, w_co)
+    normed3, inverse3 = norm_parts(stream2, gain_all[2])
+    normed3 = normed3.astype(bf16)
+
+    n3_all = gather_doc(normed3, pairs_core, pairs_y)
+    gate_pre = matmul_rows(n3_all, w_gate)
+    up_pre = matmul_rows(n3_all, w_up)
+    d_hidden = matmul_rows(cot_all, w_down)
+    hidden, gelu_pull = jax.vjp(
+        lambda gate_val, up_val: jax.nn.gelu(gate_val, approximate=True) * up_val, gate_pre, up_pre
+    )
+    d_gate, d_up = gelu_pull(d_hidden)
+    hidden, d_gate, d_up = hidden.astype(bf16), d_gate.astype(bf16), d_up.astype(bf16)
+    d_n3 = matmul_back(d_gate, w_gate) + matmul_back(d_up, w_up)
+    d_normed3 = scatter_doc(d_n3, pairs_core, pairs_y)
+    branch = scatter_doc(matmul_back(hidden, w_down), pairs_core, pairs_y)
+    ff_grads = jnp.concatenate(
+        [
+            matmul_outer(n3_all, d_gate).astype(bf16),
+            matmul_outer(n3_all, d_up).astype(bf16),
+            matmul_outer(cot_all, hidden).astype(bf16),
+        ],
+        axis=1,
+    )
+    ff_sum = lax.psum_scatter(ff_grads, "seq", scatter_dimension=0, tiled=True)
+    layer_out = by_position(stream2 + branch, x_rank, swap)
+
+    back_three, gain_grad3 = norm_back(stream2, inverse3, gain_all[2], d_normed3)
+    d_stream2 = cot.astype(f32) + back_three
+    d_branch2 = d_stream2.astype(bf16)
+    (d_mix2,) = project(d_branch2, w_co, 1)
+    d_mix2 = exchange_z(spread_heads(d_mix2), z_rank, shifts).reshape(4 * rows, 2 * HEAD_DIM)
+    d_cq, d_ckv = attention_back(info_cross, (cq_heads, ckv_heads), d_mix2, mix2, stat2, False)
+    d_cq = merge_heads(exchange_z(d_cq.reshape(4, rows, 2 * HEAD_DIM), z_rank, shifts))
+    back_two, gain_grad2 = norm_back(stream1, inverse2, gain_all[1], lift(d_cq, w_cq))
+    d_stream1 = d_stream2 + back_two
+    d_branch1 = d_stream1.astype(bf16)
+    (d_mix1,) = project(d_branch1, w_so, 1)
+    d_mix1 = exchange_z(spread_heads(d_mix1), z_rank, shifts).reshape(4 * rows, 2 * HEAD_DIM)
+    (d_qkv,) = attention_back(info_self, (qkv_heads,), d_mix1, mix1, stat1, True)
+    d_qkv = exchange_z(d_qkv.reshape(4, rows, 6 * HEAD_DIM), z_rank, shifts)
+    lanes = 2 * HEAD_DIM
+    d_q, d_k, d_v = (merge_heads(d_qkv[..., i * lanes : (i + 1) * lanes]) for i in range(3))
+
+    d_ckv = exchange_z(d_ckv.reshape(4, docs_here * slots_doc, 4 * HEAD_DIM), z_rank, shifts)
+    d_ckv = by_position(d_ckv.transpose(1, 0, 2), x_rank, swap)
+    d_ckv = d_ckv.reshape(docs_here * slots_doc, 4, 4 * HEAD_DIM).transpose(1, 0, 2)
+    d_ck, d_cv = (merge_heads(d_ckv[..., i * lanes : (i + 1) * lanes]) for i in range(2))
+    enc_grad = lift(d_ck, w_ckv[:, :, :share]) + lift(d_cv, w_ckv[:, :, share:])
+    enc_grad = enc_grad.reshape(docs_here, slots_doc, width)
+
+    d_normed1 = (
+        lift(d_q, w_qkv[:, :, :share])
+        + lift(d_k, w_qkv[:, :, share : 2 * share])
+        + lift(d_v, w_qkv[:, :, 2 * share :])
+    )
+    back_one, gain_grad1 = norm_back(stream, inverse1, gain_all[0], d_normed1)
+    dec_grad = by_position(d_stream1 + back_one, x_rank, swap)
+
+    small_grads = jnp.concatenate(
+        [
+            outer(normed1, d_q),
+            outer(normed1, d_k),
+            outer(normed1, d_v),
+            outer(normed2, d_cq),
+            outer(enc_rows, d_ck),
+            outer(enc_rows, d_cv),
+            outer(d_branch1, att1),
+            outer(d_branch2, att2),
+        ],
+        axis=-1,
+    ).reshape(doc_ranks, seq_ranks, depth, 8 * share)
+    gain_terms = jnp.stack([gain_grad1, gain_grad2, gain_grad3]).reshape(3, seq_ranks, depth)
+    gain_terms = gain_terms.transpose(1, 0, 2).reshape(1, seq_ranks, 1, 3 * depth).astype(bf16)
+    gain_terms = jnp.pad(gain_terms, ((0, 0), (0, 0), (0, 7), (0, 8 * share - 3 * depth)))
+    gain_terms = jnp.broadcast_to(gain_terms, (doc_ranks,) + gain_terms.shape[1:])
+    packed = jnp.concatenate([small_grads, gain_terms], axis=2).reshape(-1, 8 * share)
+    summed = lax.psum_scatter(packed, ("doc", "seq"), scatter_dimension=0, tiled=True).astype(f32)
+    grad_gains = summed[depth, : 3 * depth].reshape(3, depth)
+    mine = summed[:depth]
+    piece = lambda i: mine[:, i * share : (i + 1) * share]
+    ff_sum = ff_sum.astype(f32)
+    return (
+        layer_out,
+        dec_grad,
+        enc_grad,
+        jnp.stack([piece(0), piece(1), piece(2)]),
+        piece(6).T,
+        piece(3),
+        jnp.stack([piece(4), piece(5)]),
+        piece(7).T,
+        jnp.stack([ff_sum[:, :hidden_here], ff_sum[:, hidden_here : 2 * hidden_here]]),
+        ff_sum[:, 2 * hidden_here :].T,
+        grad_gains,
+    )
+
+
+def fits_by_heads(doc_ranks, seq_ranks, docs):
+    return doc_ranks == 4 and seq_ranks == 8 and docs == 8
+
+
 def solution(mesh):
+    def either(dec_in, *others):
+        docs = dec_in.shape[0] * mesh.shape["doc"]
+        if fits_by_heads(mesh.shape["doc"], mesh.shape["seq"], docs):
+            return by_heads(dec_in, *others)
+        return per_device(dec_in, *others)
+
     return jax.shard_map(
-        per_device,
+        either,
         mesh=mesh,
         in_specs=(
             P("doc", "seq", None),

time: 2380 us -> 870 us (0.37)
  waiting for transfers between devices: 1670 us -> 359 us
  blocking collectives: 295 us -> 36.4 us
  matrix products: 228 us -> 105 us
  starting transfers between devices: 11 us -> 109 us
  Pallas kernels: 0 us -> 67 us
  other arithmetic: 29.1 us -> 60.3 us
    reduce_scatter x11 -> x1, waiting for transfers between devices: 1010 us -> 97.2 us  [by_heads(): lax.psum_scatter(packed, ('doc', 'seq'), scatter_dimension=0, tiled=True)]
    unnamed x34 -> x5, waiting for transfers between devices: 334 us -> 0.07 us
    all_gather x13 -> x2, waiting for transfers between devices: 327 us -> 31.8 us  [the longest x1 31.8 us: by_heads(): lax.all_gather(small, ('doc', 'seq'), axis=0, tiled=True)]
    ppermute x0 -> x46, waiting for transfers between devices: none -> 230 us  [the longest x30 153 us: exchange_z(): lax.ppermute(lax.dynamic_index_in_dim(array, (z_rank + k) % count, 0, Fal...]
    all_gather x7 -> x1, blocking collectives: 216 us -> 36.4 us  [by_heads(): gain_all = lax.all_gather(gains, 'seq', axis=1, tiled=True).astype(f32)]
    ppermute x0 -> x46, starting transfers between devices: none -> 109 us  [the longest x30 87.9 us: exchange_z(): lax.ppermute(lax.dynamic_index_in_dim(array, (z_rank + k) % count, 0, Fal...]
    dot_general x20 -> x21, matrix products: 158 us -> 56.5 us  [the longest x8 27 us: lift(): return jnp.einsum('tek,edk->td', split, weight, preferred_element_type=f32)]
    pallas_call x0 -> x4, Pallas kernels: none -> 67 us  [the longest x2 35 us: attention_back(): pl.pallas_call(functools.partial(attend_back_kernel, wide, size, causal,...]
  transfers between devices with their start and end apart: 29 -> 50, of which waited for: 25 -> 28; matrix products, arithmetic and copies ran while one was open for 12% -> 25% of each run, Pallas kernels for 0% -> 8%
where the time goes in v1:
time: 870 us; the launch traced here: 861 us
  waiting for transfers between devices  359 us (41%)
  starting transfers between devices  109 us (13%)
  local copies, waits for them, and re-layouts  107 us (12%)
  matrix products  105 us (12%)
  Pallas kernels  67 us (8%)
  other arithmetic  60.3 us (7%)
  blocking collectives  36.4 us (4%)
  between operations  16.2 us (2%)
    ppermute x30, waiting for transfers between devices, exchange_z(): lax.ppermute(lax.dynamic_index_in_dim(array, (z_rank + k) % count, 0, Fal...  153 us
    reduce_scatter x1, waiting for transfers between devices, by_heads(): lax.psum_scatter(packed, ('doc', 'seq'), scatter_dimension=0, tiled=True)  97.2 us
    ppermute x30, starting transfers between devices, exchange_z(): lax.ppermute(lax.dynamic_index_in_dim(array, (z_rank + k) % count, 0, Fal...  87.9 us
    all_gather x1, blocking collectives, by_heads(): gain_all = lax.all_gather(gains, 'seq', axis=1, tiled=True).astype(f32)  36.4 us
    pallas_call x2, Pallas kernels, attention_back(): pl.pallas_call(functools.partial(attend_back_kernel, wide, size, causal,...  35 us
    pallas_call x2, Pallas kernels, attention(): pl.pallas_call(functools.partial(attend_kernel, wide, size, causal, len(p...  31.9 us
    all_gather x1, waiting for transfers between devices, by_heads(): lax.all_gather(small, ('doc', 'seq'), axis=0, tiled=True)  31.8 us
    dot_general x8, matrix products, lift(): return jnp.einsum('tek,edk->td', split, weight, preferred_element_type=f32)  27 us
  transfers between devices with their start and end apart: 50, of which 28 were waited for; matrix products, arithmetic and copies ran while one was open for 25% of the time, Pallas kernels for 8%

profile of v1, /device:TPU:0, one launch (start us, length us, event | category | flops | bytes accessed | tf_op | source)
XLA Modules:
  0.0 860.6 jit_solution(5492103595310376804)
XLA Ops:
  19.8 36.4 %all-gather = bf16[8,184,3]{1,2,0:T(4,128)(2,1)S(1)} all-gather(bf16[1,184,3]{1,2,0:T(4,128)(2,1)S(1)} %bitcast.669), channel_id=1, replica_groups=mesh['doc'=4,'seq'=8] {'seq'}, dimensions={0}, use_global_device_ids=true | all-gather | bytes 9936 | tf_op jit(solution)/shard_map/all_gather | solution.py:715
  63.9 31.8 %all-gather.4.cloned.1.call-done = bf16[5888,768]{1,0:T(8,128)(2,1)} async-done(((bf16[184,768]{1,0:T(8,128)(2,1)}), bf16[5888,768]{1,0:T(8,128)(2,1)}) %all-gather.4.cloned.1.call-update) | async-done | bytes 9043984 | tf_op jit(solution)/shard_map/all_gather | solution.py:709
  113.7 16.7 %collective-permute-done.2 = bf16[256,384]{0,1:T(8,128)(2,1)S(1)} collective-permute-done((bf16[256,384]{0,1:T(8,128)(2,1)S(1)}, bf16[256,384]{0,1:T(8,128)(2,1)S(1)}, u32[]{:S(2)}, u32[]{:S(2)}) %collective-permute-start.2) | collective-permute-done | bytes 196640 | tf_op jit(solution)/shard_map/ppermute | solution.py:648
  138.9 16.4 %collective-permute-start.4 = (bf16[256,128]{1,0:T(8,128)(2,1)S(1)}, bf16[256,128]{1,0:T(8,128)(2,1)S(1)}, u32[]{:S(2)}, u32[]{:S(2)}) collective-permute-start(bf16[256,128]{1,0:T(8,128)(2,1)S(1)} %dynamic-slice_bitcast_fusion.29), channel_id=1, source_target_pairs={{0,2},{1,3},{2,4},{3,5},{4,6},{5,7},{6,0},{7,1},{8,10},{9,11},{10,... | collective-permute-start | bytes 196616 | tf_op jit(solution)/shard_map/ppermute | solution.py:648
  163.2 7.9 constant_dynamic-slice_fusion.5
  207.6 17.3 %collective-permute-done.10 = bf16[512,4,256]{2,0,1:T(8,128)(2,1)} collective-permute-done((bf16[512,4,256]{2,0,1:T(8,128)(2,1)}, bf16[512,4,256]{2,0,1:T(8,128)(2,1)}, u32[]{:S(2)}, u32[]{:S(2)}) %collective-permute-start.10) | collective-permute-done | bytes 1048608 | tf_op jit(solution)/shard_map/ppermute | solution.py:632
  235.9 19.7 %collective-permute-done.11 = bf16[1024,256]{1,0:T(8,128)(2,1)S(1)} collective-permute-done((bf16[1024,256]{1,0:T(8,128)(2,1)}, bf16[1024,256]{1,0:T(8,128)(2,1)S(1)}, u32[]{:S(2)}, u32[]{:S(2)}) %collective-permute-start.11) | collective-permute-done | bytes 524320 | tf_op jit(solution)/shard_map/ppermute | solution.py:648
  255.6 28.7 %collective-permute-done.12 = bf16[1024,256]{1,0:T(8,128)(2,1)S(1)} collective-permute-done((bf16[1024,256]{1,0:T(8,128)(2,1)}, bf16[1024,256]{1,0:T(8,128)(2,1)S(1)}, u32[]{:S(2)}, u32[]{:S(2)}) %collective-permute-start.12) | collective-permute-done | bytes 524320 | tf_op jit(solution)/shard_map/ppermute | solution.py:648
  284.4 25.1 %attend_cross.1 = (bf16[1024,128]{1,0:T(8,128)(2,1)S(1)}, f32[128,1024]{1,0:T(8,128)S(1)}, f32[8,1024]{1,0:T(8,128)S(1)}) custom-call(s32[2]{0:T(128)S(1)} %pad_add_fusion.1.info_ref, bf16[1024,128]{1,0:T(8,128)(2,1)S(1)} %bitcast.617, bf16[4096,256]{1,0:T(8,128)(2,1)S(1)} %bitcast.607), custom_call_target="tpu_custom_call" | custom-call | flops 2147483648 | bytes 4194304 | tf_op jit(solution)/shard_map/attend_cross/pallas_call | solution.py:563
  309.6 11.6 %collective-permute-start.14 = (bf16[256,128]{1,0:T(8,128)(2,1)S(1)}, bf16[256,128]{1,0:T(8,128)(2,1)S(1)}, u32[]{:S(2)}, u32[]{:S(2)}) collective-permute-start(bf16[256,128]{1,0:T(8,128)(2,1)S(1)} %dynamic-slice_bitcast_fusion.23), channel_id=1, source_target_pairs={{0,2},{1,3},{2,4},{3,5},{4,6},{5,7},{6,0},{7,1},{8,10},{9,11},{10,... | collective-permute-start | bytes 196616 | tf_op jit(solution)/shard_map/ppermute | solution.py:648
  326.0 15.0 %collective-permute-start.16 = (bf16[256,128]{1,0:T(8,128)(2,1)S(1)}, bf16[256,128]{1,0:T(8,128)(2,1)S(1)}, u32[]{:S(2)}, u32[]{:S(2)}) collective-permute-start(bf16[256,128]{1,0:T(8,128)(2,1)S(1)} %get-tuple-element.220), channel_id=1, source_target_pairs={{0,6},{1,7},{2,0},{3,1},{4,2},{5,3},{6,4},{7,5},{8,14},{9,15},{10,... | collective-permute-start | bytes 196616 | tf_op jit(solution)/shard_map/ppermute | solution.py:648
  350.5 9.4 %collective-permute-done.18 = bf16[256,1472]{0,1:T(8,128)(2,1)} collective-permute-done((bf16[256,1472]{0,1:T(8,128)(2,1)}, bf16[256,1472]{0,1:T(8,128)(2,1)}, u32[]{:S(2)}, u32[]{:S(2)}) %collective-permute-start.18) | collective-permute-done | bytes 753696 | tf_op jit(solution)/shard_map/ppermute | solution.py:658
  375.4 8.2 multiply_convert_fusion
  424.8 26.5 %collective-permute-done.28 = bf16[256,1472]{0,1:T(8,128)(2,1)} collective-permute-done((bf16[256,1472]{0,1:T(8,128)(2,1)}, bf16[256,1472]{0,1:T(8,128)(2,1)}, u32[]{:S(2)}, u32[]{:S(2)}) %collective-permute-start.28) | collective-permute-done | bytes 753696 | tf_op jit(solution)/shard_map/ppermute | solution.py:672
  482.9 27.4 %attend_cross_back.1 = (bf16[1024,128]{1,0:T(8,128)(2,1)S(1)}, bf16[4096,256]{1,0:T(8,128)(2,1)S(1)}) custom-call(s32[2]{0:T(128)S(1)} %pad_add_fusion.1.info_ref, bf16[1024,128]{1,0:T(8,128)(2,1)S(1)} %bitcast.618, bf16[4096,256]{1,0:T(8,128)(2,1)S(1)} %bitcast.608, bf16[1024,128]{1,0:T(8,128)(2,1)S(1)} %bitcast.619, f32[128,1024]{1,0:T(8,128)S(1)} %copy-done.7, ...), custom_call_target="tpu_custom_call" | custom-call | flops 5368709120 | bytes 4194304 | tf_op jit(solution)/shard_map/attend_cross_back/pallas_call | solution.py:594
  544.6 17.3 %collective-permute-done.37 = bf16[256,128]{0,1:T(8,128)(2,1)S(1)} collective-permute-done((bf16[256,128]{0,1:T(8,128)(2,1)S(1)}, bf16[256,128]{0,1:T(8,128)(2,1)S(1)}, u32[]{:S(2)}, u32[]{:S(2)}) %collective-permute-start.37) | collective-permute-done | bytes 65568 | tf_op jit(solution)/shard_map/ppermute | solution.py:648
  564.3 7.6 attend_self_back.1
  572.2 15.2 %collective-permute-done.38 = bf16[256,384]{1,0:T(8,128)(2,1)S(1)} collective-permute-done((bf16[256,384]{1,0:T(8,128)(2,1)S(1)}, bf16[256,384]{1,0:T(8,128)(2,1)S(1)}, u32[]{:S(2)}, u32[]{:S(2)}) %collective-permute-start.38) | collective-permute-done | bytes 196640 | tf_op jit(solution)/shard_map/ppermute | solution.py:648
  598.0 12.9 %collective-permute-done.39 = bf16[256,384]{1,0:T(8,128)(2,1)S(1)} collective-permute-done((bf16[256,384]{1,0:T(8,128)(2,1)S(1)}, bf16[256,384]{1,0:T(8,128)(2,1)S(1)}, u32[]{:S(2)}, u32[]{:S(2)}) %collective-permute-start.39) | collective-permute-done | bytes 196640 | tf_op jit(solution)/shard_map/ppermute | solution.py:648
  637.1 9.6 %collective-permute-start.45 = (bf16[512,4,256]{2,0,1:T(8,128)(2,1)S(1)}, bf16[512,4,256]{2,0,1:T(8,128)(2,1)S(1)}, u32[]{:S(2)}, u32[]{:S(2)}) collective-permute-start(bf16[512,4,256]{2,0,1:T(8,128)(2,1)S(1)} %dynamic-slice_bitcast_fusion), channel_id=1, source_target_pairs={{0,1},{1,0},{2,3},{3,2},{4,5},{5,4},{6,7},{7,6},{8,9},{9,8},{10,11... | collective-permute-start | bytes 3145736 | tf_op jit(solution)/shard_map/ppermute | solution.py:640
  681.6 12.1 %copy.144 = bf16[4,1472,768]{2,1,0:T(8,128)(2,1)} copy(bf16[4,1472,768]{1,2,0:T(8,128)(2,1)} %fusion.29) | data formatting | bytes 18087936 | tf_op jit(solution)/shard_map/concatenate | solution.py:822
  693.7 8.5 pad_maximum_fusion
  715.0 11.7 %collective-permute-done.41 = f32[128,1472]{0,1:T(8,128)S(1)} collective-permute-done((f32[128,1472]{0,1:T(8,128)S(1)}, f32[128,1472]{0,1:T(8,128)S(1)}, u32[]{:S(2)}, u32[]{:S(2)}) %collective-permute-start.41) | collective-permute-done | bytes 753696 | tf_op jit(solution)/shard_map/ppermute | solution.py:640
  751.0 97.2 %reduce-scatter.5.cloned.1.call-done = bf16[192,768]{1,0:T(8,128)(2,1)} async-done(((bf16[6144,768]{1,0:T(8,128)(2,1)}), bf16[192,768]{1,0:T(8,128)(2,1)}) %reduce-scatter.5.cloned.1.call-update) | async-done | bytes 294928 | tf_op jit(solution)/shard_map/reduce_scatter | solution.py:840
  (463 shorter events, 354.1 us)
Async XLA Ops:
  7.2 88.6 %all-gather.4.cloned.1.call-start = ((), (), s32[]{:S(2)}) async-start(), calls=%async_computation.2 | async-start | bytes 9326592 | tf_op jit(solution)/shard_map/all_gather | solution.py:709
  10.7 353.2 %all-gather.6.cloned.1.call-start = ((), (), s32[]{:S(2)}) async-start(), calls=%async_computation.3 | async-start | bytes 8902656 | tf_op jit(solution)/shard_map/all_gather | solution.py:717
  12.6 187.1 %collective-permute-start.23 = (bf16[128,1472]{0,1:T(8,128)(2,1)}, bf16[128,1472]{0,1:T(8,128)(2,1)S(1)}, u32[]{:S(2)}, u32[]{:S(2)}) collective-permute-start(bf16[128,1472]{0,1:T(8,128)(2,1)} %dynamic-slice_bitcast_fusion.4), channel_id=1, source_target_pairs={{0,1},{1,0},{2,3},{3,2},{4,5},{5,4},{6,7},{7,6},{8,9},{9,8},{10,11... | collective-permute-start | bytes 1130504 | tf_op jit(solution)/shard_map/ppermute | solution.py:632
  16.3 45.6 %collective-permute-start = (bf16[128,1472]{0,1:T(8,128)(2,1)}, bf16[128,1472]{0,1:T(8,128)(2,1)}, u32[]{:S(2)}, u32[]{:S(2)}) collective-permute-start(bf16[128,1472]{0,1:T(8,128)(2,1)} %dynamic-slice_bitcast_fusion.5), channel_id=1, source_target_pairs={{0,1},{1,0},{2,3},{3,2},{4,5},{5,4},{6,7},{7,6},{8,9},{9,8},{10,11... | collective-permute-start | bytes 1130504 | tf_op jit(solution)/shard_map/ppermute | solution.py:632
  19.7 727.7 %reduce-scatter.7.cloned.1.call-start = ((), (), s32[]{:S(2)}) async-start(), calls=%async_computation.5 | async-start | bytes 8902656
  109.3 21.0 %collective-permute-start.2 = (bf16[256,384]{0,1:T(8,128)(2,1)S(1)}, bf16[256,384]{0,1:T(8,128)(2,1)S(1)}, u32[]{:S(2)}, u32[]{:S(2)}) collective-permute-start(bf16[256,384]{0,1:T(8,128)(2,1)S(1)} %get-tuple-element.160), channel_id=1, source_target_pairs={{0,4},{1,5},{2,6},{3,7},{4,0},{5,1},{6,2},{7,3},{8,12},{9,13},{10,... | collective-permute-start | bytes 589832 | tf_op jit(solution)/shard_map/ppermute | solution.py:648
  111.2 20.4 %collective-permute-start.3 = (bf16[256,384]{0,1:T(8,128)(2,1)S(1)}, bf16[256,384]{0,1:T(8,128)(2,1)S(1)}, u32[]{:S(2)}, u32[]{:S(2)}) collective-permute-start(bf16[256,384]{0,1:T(8,128)(2,1)S(1)} %get-tuple-element.159), channel_id=1, source_target_pairs={{0,6},{1,7},{2,0},{3,1},{4,2},{5,3},{6,4},{7,5},{8,14},{9,15},{10,... | collective-permute-start | bytes 589832 | tf_op jit(solution)/shard_map/ppermute | solution.py:648
  138.9 23.6 %collective-permute-start.4 = (bf16[256,128]{1,0:T(8,128)(2,1)S(1)}, bf16[256,128]{1,0:T(8,128)(2,1)S(1)}, u32[]{:S(2)}, u32[]{:S(2)}) collective-permute-start(bf16[256,128]{1,0:T(8,128)(2,1)S(1)} %dynamic-slice_bitcast_fusion.29), channel_id=1, source_target_pairs={{0,2},{1,3},{2,4},{3,5},{4,6},{5,7},{6,0},{7,1},{8,10},{9,11},{10,... | collective-permute-start | bytes 196616 | tf_op jit(solution)/shard_map/ppermute | solution.py:648
  176.9 48.0 %collective-permute-start.10 = (bf16[512,4,256]{2,0,1:T(8,128)(2,1)}, bf16[512,4,256]{2,0,1:T(8,128)(2,1)}, u32[]{:S(2)}, u32[]{:S(2)}) collective-permute-start(bf16[512,4,256]{2,0,1:T(8,128)(2,1)} %bitcast.650), channel_id=1, source_target_pairs={{0,1},{1,0},{2,3},{3,2},{4,5},{5,4},{6,7},{7,6},{8,9},{9,8},{10,11... | collective-permute-start | bytes 3145736 | tf_op jit(solution)/shard_map/ppermute | solution.py:632
  205.9 25.2 %collective-permute-start.9 = (bf16[256,128]{0,1:T(8,128)(2,1)S(1)}, bf16[256,128]{0,1:T(8,128)(2,1)S(1)}, u32[]{:S(2)}, u32[]{:S(2)}) collective-permute-start(bf16[256,128]{0,1:T(8,128)(2,1)S(1)} %get-tuple-element.223), channel_id=1, source_target_pairs={{0,6},{1,7},{2,0},{3,1},{4,2},{5,3},{6,4},{7,5},{8,14},{9,15},{10,... | collective-permute-start | bytes 196616 | tf_op jit(solution)/shard_map/ppermute | solution.py:648
  227.5 28.0 %collective-permute-start.11 = (bf16[1024,256]{1,0:T(8,128)(2,1)}, bf16[1024,256]{1,0:T(8,128)(2,1)S(1)}, u32[]{:S(2)}, u32[]{:S(2)}) collective-permute-start(bf16[1024,256]{1,0:T(8,128)(2,1)} %get-tuple-element.112), channel_id=1, source_target_pairs={{0,2},{1,3},{2,4},{3,5},{4,6},{5,7},{6,0},{7,1},{8,10},{9,11},{10,... | collective-permute-start | bytes 1572872 | tf_op jit(solution)/shard_map/ppermute | solution.py:648
  228.3 56.0 %collective-permute-start.12 = (bf16[1024,256]{1,0:T(8,128)(2,1)}, bf16[1024,256]{1,0:T(8,128)(2,1)S(1)}, u32[]{:S(2)}, u32[]{:S(2)}) collective-permute-start(bf16[1024,256]{1,0:T(8,128)(2,1)} %get-tuple-element.113), channel_id=1, source_target_pairs={{0,4},{1,5},{2,6},{3,7},{4,0},{5,1},{6,2},{7,3},{8,12},{9,13},{10,... | collective-permute-start | bytes 1572872 | tf_op jit(solution)/shard_map/ppermute | solution.py:648
  232.9 51.4 %collective-permute-start.13 = (bf16[1024,256]{1,0:T(8,128)(2,1)}, bf16[1024,256]{1,0:T(8,128)(2,1)S(1)}, u32[]{:S(2)}, u32[]{:S(2)}) collective-permute-start(bf16[1024,256]{1,0:T(8,128)(2,1)} %get-tuple-element.111), channel_id=1, source_target_pairs={{0,6},{1,7},{2,0},{3,1},{4,2},{5,3},{6,4},{7,5},{8,14},{9,15},{10,... | collective-permute-start | bytes 1572872 | tf_op jit(solution)/shard_map/ppermute | solution.py:648
  326.0 24.1 %collective-permute-start.25 = (bf16[256,1472]{0,1:T(8,128)(2,1)}, bf16[256,1472]{0,1:T(8,128)(2,1)}, u32[]{:S(2)}, u32[]{:S(2)}) collective-permute-start(bf16[256,1472]{0,1:T(8,128)(2,1)} %pad_maximum_fusion.12), channel_id=1, source_target_pairs={{0,16},{8,24},{16,0},{24,8},{1,17},{9,25},{17,1},{25,9},{2,18},{10... | collective-permute-start | bytes 2261000 | tf_op jit(solution)/shard_map/ppermute | solution.py:658
  396.9 20.4 %collective-permute-start.27 = (bf16[512,1472]{0,1:T(8,128)(2,1)S(1)}, bf16[512,1472]{0,1:T(8,128)(2,1)S(1)}, u32[]{:S(2)}, u32[]{:S(2)}) collective-permute-start(bf16[512,1472]{0,1:T(8,128)(2,1)S(1)} %pad_maximum_fusion.7), channel_id=1, source_target_pairs={{0,8},{8,0},{16,24},{24,16},{1,9},{9,1},{17,25},{25,17},{2,10},{10... | collective-permute-start | bytes 4521992 | tf_op jit(solution)/shard_map/ppermute | solution.py:667
  415.3 38.8 %collective-permute-start.21 = (bf16[256,1472]{0,1:T(8,128)(2,1)}, bf16[256,1472]{0,1:T(8,128)(2,1)}, u32[]{:S(2)}, u32[]{:S(2)}) collective-permute-start(bf16[256,1472]{0,1:T(8,128)(2,1)} %fusion.62), channel_id=1, source_target_pairs={{0,16},{8,24},{16,0},{24,8},{1,17},{9,25},{17,1},{25,9},{2,18},{10... | collective-permute-start | bytes 2261000 | tf_op jit(solution)/shard_map/ppermute | solution.py:672
  420.4 30.9 %collective-permute-start.28 = (bf16[256,1472]{0,1:T(8,128)(2,1)}, bf16[256,1472]{0,1:T(8,128)(2,1)}, u32[]{:S(2)}, u32[]{:S(2)}) collective-permute-start(bf16[256,1472]{0,1:T(8,128)(2,1)} %fusion.60), channel_id=1, source_target_pairs={{0,16},{8,24},{16,0},{24,8},{1,17},{9,25},{17,1},{25,9},{2,18},{10... | collective-permute-start | bytes 2261000 | tf_op jit(solution)/shard_map/ppermute | solution.py:672
  424.7 423.4 %reduce-scatter.5.cloned.1.call-start = ((), (), s32[]{:S(2)}) async-start(), calls=%async_computation.4 | async-start | bytes 9732096 | tf_op jit(solution)/shard_map/reduce_scatter | solution.py:840
  540.3 51.9 %collective-permute-start.42 = (bf16[1024,256]{1,0:T(8,128)(2,1)}, bf16[1024,256]{1,0:T(8,128)(2,1)}, u32[]{:S(2)}, u32[]{:S(2)}) collective-permute-start(bf16[1024,256]{1,0:T(8,128)(2,1)} %dynamic-slice_bitcast_fusion.3), channel_id=1, source_target_pairs={{0,2},{1,3},{2,4},{3,5},{4,6},{5,7},{6,0},{7,1},{8,10},{9,11},{10,... | collective-permute-start | bytes 1572872 | tf_op jit(solution)/shard_map/ppermute | solution.py:648
  587.5 23.4 %collective-permute-start.40 = (bf16[256,384]{1,0:T(8,128)(2,1)S(1)}, bf16[256,384]{1,0:T(8,128)(2,1)S(1)}, u32[]{:S(2)}, u32[]{:S(2)}) collective-permute-start(bf16[256,384]{1,0:T(8,128)(2,1)S(1)} %get-tuple-element.156), channel_id=1, source_target_pairs={{0,6},{1,7},{2,0},{3,1},{4,2},{5,3},{6,4},{7,5},{8,14},{9,15},{10,... | collective-permute-start | bytes 589832 | tf_op jit(solution)/shard_map/ppermute | solution.py:648
  589.3 21.6 %collective-permute-start.39 = (bf16[256,384]{1,0:T(8,128)(2,1)S(1)}, bf16[256,384]{1,0:T(8,128)(2,1)S(1)}, u32[]{:S(2)}, u32[]{:S(2)}) collective-permute-start(bf16[256,384]{1,0:T(8,128)(2,1)S(1)} %get-tuple-element.157), channel_id=1, source_target_pairs={{0,4},{1,5},{2,6},{3,7},{4,0},{5,1},{6,2},{7,3},{8,12},{9,13},{10,... | collective-permute-start | bytes 589832 | tf_op jit(solution)/shard_map/ppermute | solution.py:648
  594.4 41.5 %collective-permute-start.44 = (bf16[1024,256]{1,0:T(8,128)(2,1)}, bf16[1024,256]{1,0:T(8,128)(2,1)}, u32[]{:S(2)}, u32[]{:S(2)}) collective-permute-start(bf16[1024,256]{1,0:T(8,128)(2,1)} %get-tuple-element.108), channel_id=1, source_target_pairs={{0,6},{1,7},{2,0},{3,1},{4,2},{5,3},{6,4},{7,5},{8,14},{9,15},{10,... | collective-permute-start | bytes 1572872 | tf_op jit(solution)/shard_map/ppermute | solution.py:648
  595.9 38.9 %collective-permute-start.43 = (bf16[1024,256]{1,0:T(8,128)(2,1)}, bf16[1024,256]{1,0:T(8,128)(2,1)}, u32[]{:S(2)}, u32[]{:S(2)}) collective-permute-start(bf16[1024,256]{1,0:T(8,128)(2,1)} %get-tuple-element.109), channel_id=1, source_target_pairs={{0,4},{1,5},{2,6},{3,7},{4,0},{5,1},{6,2},{7,3},{8,12},{9,13},{10,... | collective-permute-start | bytes 1572872 | tf_op jit(solution)/shard_map/ppermute | solution.py:648
  637.1 22.3 %collective-permute-start.45 = (bf16[512,4,256]{2,0,1:T(8,128)(2,1)S(1)}, bf16[512,4,256]{2,0,1:T(8,128)(2,1)S(1)}, u32[]{:S(2)}, u32[]{:S(2)}) collective-permute-start(bf16[512,4,256]{2,0,1:T(8,128)(2,1)S(1)} %dynamic-slice_bitcast_fusion), channel_id=1, source_target_pairs={{0,1},{1,0},{2,3},{3,2},{4,5},{5,4},{6,7},{7,6},{8,9},{9,8},{10,11... | collective-permute-start | bytes 3145736 | tf_op jit(solution)/shard_map/ppermute | solution.py:640
  (92 other events, 1305.8 us)
Sparse Core Ops, SparseCore 0:
  11.6 84.1 all-gather.3
  98.0 186.0 all-gather.5
  424.8 173.1 reduce-scatter.6
  702.3 145.7 reduce-scatter.4

commit v2 on v1

--- a/solution.py
+++ b/solution.py
@@ -642,34 +642,57 @@
     return jnp.stack([jnp.where(first, own, other), jnp.where(first, other, own)])
 
 
-def exchange_z(array, z_rank, shifts):
+def send_z(array, z_rank, shifts):
     count = array.shape[0]
-    arrived = [
+    return [
         lax.ppermute(lax.dynamic_index_in_dim(array, (z_rank + k) % count, 0, False), "seq", shifts[k])
         for k in range(1, count)
     ]
+
+
+def place_z(array, arrived, z_rank):
+    count = array.shape[0]
     out = array
     for k in range(1, count):
         out = lax.dynamic_update_index_in_dim(out, arrived[k - 1], (z_rank - k) % count, 0)
     return out
 
 
+def exchange_z(array, z_rank, shifts):
+    return place_z(array, send_z(array, z_rank, shifts), z_rank)
+
+
+def add_z(array, z_rank, shifts):
+    total = lax.dynamic_index_in_dim(array, z_rank, 0, False).astype(jnp.float32)
+    for arrived in send_z(array, z_rank, shifts):
+        total = total + arrived.astype(jnp.float32)
+    return total
+
+
+def add_x(array, x_rank, swap):
+    keep = lax.dynamic_index_in_dim(array, x_rank, 1, False).astype(jnp.float32)
+    send = lax.dynamic_index_in_dim(array, 1 - x_rank, 1, False)
+    return (keep + lax.ppermute(send, "seq", swap).astype(jnp.float32)).astype(jnp.bfloat16)
+
+
 def gather_doc(array, pairs_core, pairs_y):
     across = lax.ppermute(array, "doc", pairs_y)
     beside = lax.ppermute(array, "doc", pairs_core)
     far = lax.ppermute(across, "doc", pairs_core)
-    return jnp.concatenate([array, beside, across, far], axis=0)
-
-
-def scatter_doc(array, pairs_core, pairs_y):
-    n = array.shape[0] // 4
-    low = array.astype(jnp.bfloat16)
-    share = lax.ppermute(
-        jnp.concatenate([low[n : 2 * n], low[3 * n :]], axis=0), "doc", pairs_core
-    ).astype(jnp.float32)
-    mine = array[:n] + share[:n]
-    across = (array[2 * n : 3 * n] + share[n:]).astype(jnp.bfloat16)
-    return mine + lax.ppermute(across, "doc", pairs_y).astype(jnp.float32)
+    return jnp.concatenate([array, beside], axis=0), jnp.concatenate([across, far], axis=0)
+
+
+def add_core(array, pairs_core):
+    n = array.shape[0] // 2
+    return array[:n] + lax.ppermute(array[n:].astype(jnp.bfloat16), "doc", pairs_core).astype(jnp.float32)
+
+
+def relative_doc(array, core_rank, y_rank):
+    a, b, c, d = (array[..., i, :] for i in range(4))
+    even = core_rank == 0
+    a, b, c, d = (jnp.where(even, a, b), jnp.where(even, b, a), jnp.where(even, c, d), jnp.where(even, d, c))
+    low = y_rank == 0
+    return [jnp.where(low, a, c), jnp.where(low, b, d), jnp.where(low, c, a), jnp.where(low, d, b)]
 
 
 def by_heads(
@@ -688,36 +711,38 @@
     cotangent,
 ):
     f32, bf16 = jnp.float32, jnp.bfloat16
+    tie = lax.optimization_barrier
     docs_here, rows_doc, width = dec_in.shape
     slots_doc = enc_in.shape[1]
     doc_ranks, seq_ranks = lax.axis_size("doc"), lax.axis_size("seq")
-    seq_rank = lax.axis_index("seq")
+    seq_rank, doc_rank = lax.axis_index("seq"), lax.axis_index("doc")
     z_rank, x_rank = seq_rank // 2, seq_rank % 2
+    y_rank, core_rank = doc_rank // 2, doc_rank % 2
     swap = [(i, i ^ 1) for i in range(seq_ranks)]
     shifts = [[(i, (i + 2 * k) % seq_ranks) for i in range(seq_ranks)] for k in range(seq_ranks // 2)]
     pairs_core = [(i, i ^ 1) for i in range(doc_ranks)]
     pairs_y = [(i, i ^ 2) for i in range(doc_ranks)]
     inner = HEADS * HEAD_DIM
+    lanes = 2 * HEAD_DIM
     share = inner // doc_ranks
     depth = width // seq_ranks
     rows = docs_here * rows_doc
+    slots = docs_here * slots_doc
 
     small = jnp.concatenate(
         [self_qkv[0], self_qkv[1], self_qkv[2], cross_q, cross_kv[0], cross_kv[1], self_out.T, cross_out.T],
         axis=1,
     )
-    every = lax.all_gather(small, ("doc", "seq"), axis=0, tiled=True).reshape(doc_ranks, width, 8 * share)
-    w_qkv = every[:, :, : 3 * share]
-    w_cq = every[:, :, 3 * share : 4 * share]
-    w_ckv = every[:, :, 4 * share : 6 * share]
-    w_so = every[:, :, 6 * share : 7 * share]
-    w_co = every[:, :, 7 * share :]
-    gain_all = lax.all_gather(gains, "seq", axis=1, tiled=True).astype(f32)
+    every = lax.all_gather(small, ("doc", "seq"), axis=0, tiled=True)
     ff_mine = jnp.concatenate([ff_in[0], ff_in[1], ff_out.T], axis=1)
     ff_all = lax.all_gather(ff_mine, "seq", axis=0, tiled=True)
     hidden_here = ff_in.shape[2]
-    w_gate, w_up = ff_all[:, :hidden_here], ff_all[:, hidden_here : 2 * hidden_here]
-    w_down = ff_all[:, 2 * hidden_here :]
+
+    gain_other = lax.ppermute(gains, "seq", swap)
+    gain_pair = jnp.where(x_rank == 0, jnp.stack([gains, gain_other]), jnp.stack([gain_other, gains]))
+    gain_all = jnp.broadcast_to(gain_pair, (seq_ranks // 2,) + gain_pair.shape)
+    gain_all = exchange_z(gain_all, z_rank, shifts)
+    gain_all = gain_all.transpose(2, 0, 1, 3).reshape(3, width).astype(f32)
 
     def project(rows_in, weight, parts):
         out = jnp.einsum("td,edk->etk", rows_in, weight, preferred_element_type=f32).astype(bf16)
@@ -730,52 +755,83 @@
         split = inner_in.reshape(inner_in.shape[0], doc_ranks, share)
         return jnp.einsum("tek,edk->td", split, weight, preferred_element_type=f32)
 
-    def outer(rows_in, inner_in):
-        split = inner_in.reshape(inner_in.shape[0], doc_ranks, share)
-        return jnp.einsum("td,tek->edk", rows_in, split, preferred_element_type=f32).astype(bf16)
+    def outer(inner_in, rows_in):
+        parts = relative_doc(inner_in.reshape(inner_in.shape[0], doc_ranks, share), core_rank, y_rank)
+        every_part = jnp.concatenate(parts, axis=-1)
+        return matmul_outer(every_part, rows_in).astype(bf16).reshape(doc_ranks, share, width)
 
     info_self = jnp.stack([lax.dynamic_index_in_dim(tgt_len, x_rank, 0, False), z_rank % 2])
     info_cross = jnp.stack([lax.dynamic_index_in_dim(enc_len, x_rank, 0, False), z_rank % 2])
 
     stream = by_document(dec_in, x_rank, swap).astype(f32)
     cot = by_document(cotangent, x_rank, swap)
-    cot_all = gather_doc(cot, pairs_core, pairs_y)
     normed1, inverse1 = norm_parts(stream, gain_all[0])
     normed1 = normed1.astype(bf16)
+    cot_near, cot_far = gather_doc(cot, pairs_core, pairs_y)
+    n1_near, n1_far = gather_doc(normed1, pairs_core, pairs_y)
+    every, normed1, cot_near, cot_far, n1_near, n1_far = tie(
+        (every, normed1, cot_near, cot_far, n1_near, n1_far)
+    )
+    every = every.reshape(doc_ranks, width, 8 * share)
+    w_qkv = every[:, :, : 3 * share]
+    w_cq = every[:, :, 3 * share : 4 * share]
+    w_ckv = every[:, :, 4 * share : 6 * share]
+    w_so = every[:, :, 6 * share : 7 * share]
+    w_co = every[:, :, 7 * share :]
+
     qkv = jnp.concatenate([spread_heads(p) for p in project(normed1, w_qkv, 3)], axis=-1)
-    qkv_heads = exchange_z(qkv, z_rank, shifts).reshape(4 * rows, 6 * HEAD_DIM)
+    qkv_heads = exchange_z(qkv, z_rank, shifts).reshape(4 * rows, 3 * lanes)
+    enc_rows = enc_in.reshape(slots, width)
+    ckv = jnp.concatenate([spread_heads(p) for p in project(enc_rows, w_ckv, 2)], axis=-1)
+    ckv = ckv.reshape(4, docs_here, slots_doc, 2 * lanes).transpose(1, 2, 0, 3)
+    ckv = by_document(ckv, x_rank, swap).transpose(1, 0, 2)
+    qkv_heads, ckv = tie((qkv_heads, ckv))
+    ckv_arrived = send_z(ckv, z_rank, shifts)
     att1, mix1, stat1 = attention(info_self, (qkv_heads,), True)
-    att1 = merge_heads(exchange_z(att1.reshape(4, rows, 2 * HEAD_DIM), z_rank, shifts))
+    att1 = exchange_z(att1.reshape(4, rows, lanes), z_rank, shifts)
+    att1, ckv_arrived[0] = tie((att1, ckv_arrived[0]))
+    att1 = merge_heads(att1)
     stream1 = stream + lift(att1, w_so)
     normed2, inverse2 = norm_parts(stream1, gain_all[1])
     normed2 = normed2.astype(bf16)
     (cq,) = project(normed2, w_cq, 1)
-    cq_heads = exchange_z(spread_heads(cq), z_rank, shifts).reshape(4 * rows, 2 * HEAD_DIM)
-
-    enc_rows = enc_in.reshape(docs_here * slots_doc, width)
-    ckv = jnp.concatenate([spread_heads(p) for p in project(enc_rows, w_ckv, 2)], axis=-1)
-    ckv = ckv.reshape(4, docs_here, slots_doc, 4 * HEAD_DIM).transpose(1, 2, 0, 3)
-    ckv = by_document(ckv, x_rank, swap).transpose(1, 0, 2)
-    ckv_heads = exchange_z(ckv, z_rank, shifts).reshape(4 * docs_here * slots_doc, 4 * HEAD_DIM)
+    cq_heads = exchange_z(spread_heads(cq), z_rank, shifts).reshape(4 * rows, lanes)
+    ckv_heads = place_z(ckv, ckv_arrived, z_rank).reshape(4 * slots, 2 * lanes)
 
     att2, mix2, stat2 = attention(info_cross, (cq_heads, ckv_heads), False)
-    att2 = merge_heads(exchange_z(att2.reshape(4, rows, 2 * HEAD_DIM), z_rank, shifts))
+    att2 = merge_heads(exchange_z(att2.reshape(4, rows, lanes), z_rank, shifts))
     stream2 = stream1 + lift(att2, w_co)
     normed3, inverse3 = norm_parts(stream2, gain_all[2])
     normed3 = normed3.astype(bf16)
 
-    n3_all = gather_doc(normed3, pairs_core, pairs_y)
-    gate_pre = matmul_rows(n3_all, w_gate)
-    up_pre = matmul_rows(n3_all, w_up)
-    d_hidden = matmul_rows(cot_all, w_down)
-    hidden, gelu_pull = jax.vjp(
-        lambda gate_val, up_val: jax.nn.gelu(gate_val, approximate=True) * up_val, gate_pre, up_pre
-    )
-    d_gate, d_up = gelu_pull(d_hidden)
-    hidden, d_gate, d_up = hidden.astype(bf16), d_gate.astype(bf16), d_up.astype(bf16)
-    d_n3 = matmul_back(d_gate, w_gate) + matmul_back(d_up, w_up)
-    d_normed3 = scatter_doc(d_n3, pairs_core, pairs_y)
-    branch = scatter_doc(matmul_back(hidden, w_down), pairs_core, pairs_y)
+    w_gate, w_up = ff_all[:, :hidden_here], ff_all[:, hidden_here : 2 * hidden_here]
+    w_down = ff_all[:, 2 * hidden_here :]
+
+    def inside(n3_rows, cot_rows):
+        gate_pre = matmul_rows(n3_rows, w_gate)
+        up_pre = matmul_rows(n3_rows, w_up)
+        d_hidden = matmul_rows(cot_rows, w_down)
+        hidden, gelu_pull = jax.vjp(
+            lambda gate_val, up_val: jax.nn.gelu(gate_val, approximate=True) * up_val, gate_pre, up_pre
+        )
+        d_gate, d_up = gelu_pull(d_hidden)
+        return hidden.astype(bf16), d_gate.astype(bf16), d_up.astype(bf16)
+
+    def through(d_gate, d_up):
+        return matmul_back(d_gate, w_gate) + matmul_back(d_up, w_up)
+
+    n3_near, n3_far = gather_doc(normed3, pairs_core, pairs_y)
+    hid_near, dg_near, du_near = inside(n3_near, cot_near)
+    hid_near, n3_far = tie((hid_near, n3_far))
+    hid_far, dg_far, du_far = inside(n3_far, cot_far)
+    dn3_far = add_core(through(dg_far, du_far), pairs_core).astype(bf16)
+    dn3_across = lax.ppermute(dn3_far, "doc", pairs_y)
+    dn3_near = add_core(through(dg_near, du_near), pairs_core)
+    n3_all = jnp.concatenate([n3_near, n3_far], axis=0)
+    cot_all = jnp.concatenate([cot_near, cot_far], axis=0)
+    d_gate = jnp.concatenate([dg_near, dg_far], axis=0)
+    d_up = jnp.concatenate([du_near, du_far], axis=0)
+    hidden = jnp.concatenate([hid_near, hid_far], axis=0)
     ff_grads = jnp.concatenate(
         [
             matmul_outer(n3_all, d_gate).astype(bf16),
@@ -785,72 +841,99 @@
         axis=1,
     )
     ff_sum = lax.psum_scatter(ff_grads, "seq", scatter_dimension=0, tiled=True)
-    layer_out = by_position(stream2 + branch, x_rank, swap)
+    dn3_across, ff_grads = tie((dn3_across, ff_grads))
+    d_normed3 = dn3_near + dn3_across.astype(f32)
 
     back_three, gain_grad3 = norm_back(stream2, inverse3, gain_all[2], d_normed3)
     d_stream2 = cot.astype(f32) + back_three
     d_branch2 = d_stream2.astype(bf16)
     (d_mix2,) = project(d_branch2, w_co, 1)
-    d_mix2 = exchange_z(spread_heads(d_mix2), z_rank, shifts).reshape(4 * rows, 2 * HEAD_DIM)
+    d_mix2 = exchange_z(spread_heads(d_mix2), z_rank, shifts).reshape(4 * rows, lanes)
+    d_mix2, hidden_late = tie((d_mix2, hidden))
+    branch_far = add_core(matmul_back(hidden_late[2 * rows :], w_down), pairs_core).astype(bf16)
+    branch_across = lax.ppermute(branch_far, "doc", pairs_y)
+    branch = add_core(matmul_back(hidden_late[: 2 * rows], w_down), pairs_core)
     d_cq, d_ckv = attention_back(info_cross, (cq_heads, ckv_heads), d_mix2, mix2, stat2, False)
-    d_cq = merge_heads(exchange_z(d_cq.reshape(4, rows, 2 * HEAD_DIM), z_rank, shifts))
+    d_ckv = d_ckv.reshape(4, slots, 2 * lanes)
+    d_ckv_arrived = send_z(d_ckv, z_rank, shifts)
+    d_cq = exchange_z(d_cq.reshape(4, rows, lanes), z_rank, shifts)
+    d_cq, branch_across = tie((d_cq, branch_across))
+    layer_out = by_position(stream2 + (branch + branch_across.astype(f32)), x_rank, swap)
+    d_cq = merge_heads(d_cq)
     back_two, gain_grad2 = norm_back(stream1, inverse2, gain_all[1], lift(d_cq, w_cq))
     d_stream1 = d_stream2 + back_two
     d_branch1 = d_stream1.astype(bf16)
     (d_mix1,) = project(d_branch1, w_so, 1)
-    d_mix1 = exchange_z(spread_heads(d_mix1), z_rank, shifts).reshape(4 * rows, 2 * HEAD_DIM)
+    d_mix1 = exchange_z(spread_heads(d_mix1), z_rank, shifts).reshape(4 * rows, lanes)
+    d_mix1, layer_out, *d_ckv_arrived = tie((d_mix1, layer_out, *d_ckv_arrived))
+    d_ckv = place_z(d_ckv, d_ckv_arrived, z_rank)
+    d_stream1_out = by_position(d_stream1, x_rank, swap)
     (d_qkv,) = attention_back(info_self, (qkv_heads,), d_mix1, mix1, stat1, True)
-    d_qkv = exchange_z(d_qkv.reshape(4, rows, 6 * HEAD_DIM), z_rank, shifts)
-    lanes = 2 * HEAD_DIM
+    d_qkv = exchange_z(d_qkv.reshape(4, rows, 3 * lanes), z_rank, shifts)
+    d_ckv = by_position(d_ckv.transpose(1, 0, 2), x_rank, swap)
+    d_qkv, d_ckv, d_stream1_out = tie((d_qkv, d_ckv, d_stream1_out))
     d_q, d_k, d_v = (merge_heads(d_qkv[..., i * lanes : (i + 1) * lanes]) for i in range(3))
 
-    d_ckv = exchange_z(d_ckv.reshape(4, docs_here * slots_doc, 4 * HEAD_DIM), z_rank, shifts)
-    d_ckv = by_position(d_ckv.transpose(1, 0, 2), x_rank, swap)
-    d_ckv = d_ckv.reshape(docs_here * slots_doc, 4, 4 * HEAD_DIM).transpose(1, 0, 2)
-    d_ck, d_cv = (merge_heads(d_ckv[..., i * lanes : (i + 1) * lanes]) for i in range(2))
-    enc_grad = lift(d_ck, w_ckv[:, :, :share]) + lift(d_cv, w_ckv[:, :, share:])
-    enc_grad = enc_grad.reshape(docs_here, slots_doc, width)
-
+    by_doc = jnp.concatenate(
+        [d.reshape(rows, doc_ranks, share) for d in (d_q, d_k, d_v)], axis=-1
+    )
+    own, beside, across, far = relative_doc(by_doc, core_rank, y_rank)
+    arrived = lax.ppermute(jnp.stack([beside, far]), "doc", pairs_core)
+    across = jnp.concatenate([across, arrived[1]], axis=0)
+    d_near = jnp.concatenate([own, arrived[0]], axis=0)
+    d_far = lax.ppermute(across, "doc", pairs_y)
     d_normed1 = (
         lift(d_q, w_qkv[:, :, :share])
         + lift(d_k, w_qkv[:, :, share : 2 * share])
         + lift(d_v, w_qkv[:, :, 2 * share :])
     )
     back_one, gain_grad1 = norm_back(stream, inverse1, gain_all[0], d_normed1)
-    dec_grad = by_position(d_stream1 + back_one, x_rank, swap)
-
-    small_grads = jnp.concatenate(
+    dec_grad = d_stream1_out + by_position(back_one.astype(bf16), x_rank, swap).astype(f32)
+
+    d_ckv = d_ckv.reshape(slots, 4, 2 * lanes).transpose(1, 0, 2)
+    d_ck, d_cv = (merge_heads(d_ckv[..., i * lanes : (i + 1) * lanes]) for i in range(2))
+    enc_grad = lift(d_ck, w_ckv[:, :, :share]) + lift(d_cv, w_ckv[:, :, share:])
+    enc_grad = enc_grad.reshape(docs_here, slots_doc, width)
+
+    terms = jnp.concatenate(
         [
-            outer(normed1, d_q),
-            outer(normed1, d_k),
-            outer(normed1, d_v),
-            outer(normed2, d_cq),
-            outer(enc_rows, d_ck),
-            outer(enc_rows, d_cv),
-            outer(d_branch1, att1),
-            outer(d_branch2, att2),
+            outer(d_cq, normed2),
+            outer(d_ck, enc_rows),
+            outer(d_cv, enc_rows),
+            outer(att1, d_branch1),
+            outer(att2, d_branch2),
         ],
-        axis=-1,
-    ).reshape(doc_ranks, seq_ranks, depth, 8 * share)
-    gain_terms = jnp.stack([gain_grad1, gain_grad2, gain_grad3]).reshape(3, seq_ranks, depth)
-    gain_terms = gain_terms.transpose(1, 0, 2).reshape(1, seq_ranks, 1, 3 * depth).astype(bf16)
-    gain_terms = jnp.pad(gain_terms, ((0, 0), (0, 0), (0, 7), (0, 8 * share - 3 * depth)))
-    gain_terms = jnp.broadcast_to(gain_terms, (doc_ranks,) + gain_terms.shape[1:])
-    packed = jnp.concatenate([small_grads, gain_terms], axis=2).reshape(-1, 8 * share)
-    summed = lax.psum_scatter(packed, ("doc", "seq"), scatter_dimension=0, tiled=True).astype(f32)
-    grad_gains = summed[depth, : 3 * depth].reshape(3, depth)
-    mine = summed[:depth]
-    piece = lambda i: mine[:, i * share : (i + 1) * share]
+        axis=1,
+    )
+    arrived = lax.ppermute(jnp.stack([terms[1], terms[3]]), "doc", pairs_core).astype(f32)
+    across = (terms[2].astype(f32) + arrived[1]).astype(bf16)
+    terms = (terms[0].astype(f32) + arrived[0]) + lax.ppermute(across, "doc", pairs_y).astype(f32)
+    terms = terms.astype(bf16).T.reshape(seq_ranks // 2, 2, depth, 5 * share)
+    others = add_z(add_x(terms, x_rank, swap), z_rank, shifts)
+
+    gain_terms = jnp.stack([gain_grad1, gain_grad2, gain_grad3])
+    gain_terms = gain_terms + lax.ppermute(gain_terms, "doc", pairs_core)
+    gain_terms = gain_terms + lax.ppermute(gain_terms, "doc", pairs_y)
+    gain_terms = gain_terms.reshape(3, seq_ranks, depth).transpose(1, 0, 2)
+    gain_terms = gain_terms.reshape(seq_ranks, 2, 3 * depth // 2).astype(bf16)
+    gain_terms = jnp.pad(gain_terms, ((0, 0), (0, 6), (0, 3 * share - 3 * depth // 2)))
+    grad_qkv = matmul_outer(n1_near, d_near) + matmul_outer(n1_far, d_far)
+    grad_qkv = grad_qkv.astype(bf16).reshape(seq_ranks, depth, 3 * share)
+    grad_qkv = jnp.concatenate([grad_qkv, gain_terms], axis=1)
+    grad_qkv = grad_qkv.reshape(seq_ranks // 2, 2, depth + 8, 3 * share)
+    summed = add_z(add_x(grad_qkv, x_rank, swap), z_rank, shifts)
+    grad_gains = summed[depth : depth + 2, : 3 * depth // 2].reshape(3, depth)
+    piece = lambda a, i: a[:depth, i * share : (i + 1) * share]
     ff_sum = ff_sum.astype(f32)
     return (
         layer_out,
         dec_grad,
         enc_grad,
-        jnp.stack([piece(0), piece(1), piece(2)]),
-        piece(6).T,
-        piece(3),
-        jnp.stack([piece(4), piece(5)]),
-        piece(7).T,
+        jnp.stack([piece(summed, 0), piece(summed, 1), piece(summed, 2)]),
+        piece(others, 3).T,
+        piece(others, 0),
+        jnp.stack([piece(others, 1), piece(others, 2)]),
+        piece(others, 4).T,
         jnp.stack([ff_sum[:, :hidden_here], ff_sum[:, hidden_here : 2 * hidden_here]]),
         ff_sum[:, 2 * hidden_here :].T,
         grad_gains,

time: 870 us -> 811 us (0.932)
  waiting for transfers between devices: 359 us -> 283 us
  blocking collectives: 36.4 us -> 0 us
  starting transfers between devices: 109 us -> 139 us
  other arithmetic: 60.3 us -> 80 us
  local copies, waits for them, and re-layouts: 107 us -> 121 us
  Pallas kernels: 67 us -> 56.1 us
    reduce_scatter x1 -> x0, waiting for transfers between devices: 97.2 us -> none  [by_heads(): lax.psum_scatter(packed, ('doc', 'seq'), scatter_dimension=0, tiled=True)]
    ppermute x2 -> x3, waiting for transfers between devices: 9.42 us -> 47.8 us  [gather_doc(): across = lax.ppermute(array, 'doc', pairs_y)]
    ppermute x34 -> x54, starting transfers between devices: 91.3 us -> 130 us  [the longest x39 119 us: send_z(): lax.ppermute(lax.dynamic_index_in_dim(array, (z_rank + k) % count, 0, Fal...]
    all_gather x1 -> x0, blocking collectives: 36.4 us -> none  [by_heads(): gain_all = lax.all_gather(gains, 'seq', axis=1, tiled=True).astype(f32)]
    ppermute x34 -> x54, waiting for transfers between devices: 179 us -> 203 us  [the longest x39 158 us: send_z(): lax.ppermute(lax.dynamic_index_in_dim(array, (z_rank + k) % count, 0, Fal...]
    all_gather x1, waiting for transfers between devices: 31.8 us -> 12.6 us  [by_heads(): every = lax.all_gather(small, ('doc', 'seq'), axis=0, tiled=True)]
    ppermute x3 -> x4, waiting for transfers between devices: 24.4 us -> 9.43 us  [by_position(): lax.ppermute(lax.dynamic_index_in_dim(pair, 1 - x_rank, 0, False), 'seq',...]
    dot_general x8 -> x0, matrix products: 12.6 us -> none  [outer(): jnp.einsum('td,tek->edk', rows_in, split, preferred_element_type=f32)]
  transfers between devices with their start and end apart: 50 -> 73, of which waited for: 28 -> 36; matrix products, arithmetic and copies ran while one was open for 25% -> 36% of each run, Pallas kernels for 8% -> 7%
where the time goes in v2:
time: 811 us; the launch traced here: 804 us
  waiting for transfers between devices  283 us (35%)
  starting transfers between devices  139 us (17%)
  local copies, waits for them, and re-layouts  121 us (15%)
  matrix products  108 us (13%)
  other arithmetic  80 us (10%)
  Pallas kernels  56.1 us (7%)
  between operations  16.7 us (2%)
    ppermute x39, waiting for transfers between devices, send_z(): lax.ppermute(lax.dynamic_index_in_dim(array, (z_rank + k) % count, 0, Fal...  158 us
    ppermute x39, starting transfers between devices, send_z(): lax.ppermute(lax.dynamic_index_in_dim(array, (z_rank + k) % count, 0, Fal...  119 us
    ppermute x3, waiting for transfers between devices, gather_doc(): across = lax.ppermute(array, 'doc', pairs_y)  47.8 us
    pallas_call x2, Pallas kernels, attention_back(): pl.pallas_call(functools.partial(attend_back_kernel, wide, size, causal,...  29.4 us
    dot_general x10, matrix products, matmul_outer(): lax.dot_general(left_op, right_op, (((0,), (0,)), ((), ())), preferred_el...  28.9 us
    dot_general x8, matrix products, lift(): return jnp.einsum('tek,edk->td', split, weight, preferred_element_type=f32)  27 us
    pallas_call x2, Pallas kernels, attention(): pl.pallas_call(functools.partial(attend_kernel, wide, size, causal, len(p...  26.7 us
    unnamed x199, local copies, waits for them, and re-layouts  24.4 us
  transfers between devices with their start and end apart: 73, of which 36 were waited for; matrix products, arithmetic and copies ran while one was open for 36% of the time, Pallas kernels for 7%

profile of v2, /device:TPU:0, one launch (start us, length us, event | category | flops | bytes accessed | tf_op | source)
XLA Modules:
  0.0 804.0 jit_solution(6608967265518011780)
XLA Ops:
  25.6 9.8 %collective-permute-done.5 = bf16[128,1472]{0,1:T(8,128)(2,1)S(1)} collective-permute-done((bf16[128,1472]{0,1:T(8,128)(2,1)S(1)}, bf16[128,1472]{0,1:T(8,128)(2,1)S(1)}, u32[]{:S(2)}, u32[]{:S(2)}) %collective-permute-start.5) | collective-permute-done | bytes 376864 | tf_op jit(solution)/shard_map/ppermute | solution.py:632
  40.4 20.1 %collective-permute-done.7 = bf16[256,1472]{0,1:T(8,128)(2,1)S(1)} collective-permute-done((bf16[256,1472]{0,1:T(8,128)(2,1)}, bf16[256,1472]{0,1:T(8,128)(2,1)S(1)}, u32[]{:S(2)}, u32[]{:S(2)}) %collective-permute-start.7) | collective-permute-done | bytes 753696 | tf_op jit(solution)/shard_map/ppermute | solution.py:679
  66.2 16.9 %collective-permute-done.10 = bf16[256,1472]{0,1:T(8,128)(2,1)S(1)} collective-permute-done((bf16[256,1472]{0,1:T(8,128)(2,1)S(1)}, bf16[256,1472]{0,1:T(8,128)(2,1)S(1)}, u32[]{:S(2)}, u32[]{:S(2)}) %collective-permute-start.10) | collective-permute-done | bytes 753696 | tf_op jit(solution)/shard_map/ppermute | solution.py:679
  91.5 12.6 %all-gather.3.cloned.1.call-done = bf16[5888,768]{1,0:T(8,128)(2,1)} async-done(((bf16[184,768]{1,0:T(8,128)(2,1)}), bf16[5888,768]{1,0:T(8,128)(2,1)}) %all-gather.3.cloned.1.call-update) | async-done | bytes 9043984 | tf_op jit(solution)/shard_map/all_gather | solution.py:736
  141.1 12.3 %collective-permute-done.13 = bf16[256,384]{0,1:T(8,128)(2,1)S(1)} collective-permute-done((bf16[256,384]{0,1:T(8,128)(2,1)S(1)}, bf16[256,384]{0,1:T(8,128)(2,1)S(1)}, u32[]{:S(2)}, u32[]{:S(2)}) %collective-permute-start.13) | collective-permute-done | bytes 196640 | tf_op jit(solution)/shard_map/ppermute | solution.py:648
  165.7 7.8 collective-permute-start.16
  183.6 19.2 %collective-permute-done.17 = bf16[256,128]{1,0:T(8,128)(2,1)S(1)} collective-permute-done((bf16[256,128]{1,0:T(8,128)(2,1)S(1)}, bf16[256,128]{1,0:T(8,128)(2,1)S(1)}, u32[]{:S(2)}, u32[]{:S(2)}) %collective-permute-start.17) | collective-permute-done | bytes 65568 | tf_op jit(solution)/shard_map/ppermute | solution.py:648
  214.8 15.4 %collective-permute-start.20 = (bf16[256,128]{0,1:T(8,128)(2,1)S(1)}, bf16[256,128]{0,1:T(8,128)(2,1)S(1)}, u32[]{:S(2)}, u32[]{:S(2)}) collective-permute-start(bf16[256,128]{0,1:T(8,128)(2,1)S(1)} %dynamic-slice_bitcast_fusion.33), channel_id=1, source_target_pairs={{0,2},{1,3},{2,4},{3,5},{4,6},{5,7},{6,0},{7,1},{8,10},{9,11},{10,... | collective-permute-start | bytes 196616 | tf_op jit(solution)/shard_map/ppermute | solution.py:648
  242.5 34.6 %collective-permute-done.21 = bf16[256,128]{0,1:T(8,128)(2,1)S(1)} collective-permute-done((bf16[256,128]{0,1:T(8,128)(2,1)S(1)}, bf16[256,128]{0,1:T(8,128)(2,1)S(1)}, u32[]{:S(2)}, u32[]{:S(2)}) %collective-permute-start.21) | collective-permute-done | bytes 65568 | tf_op jit(solution)/shard_map/ppermute | solution.py:648
  279.5 19.5 %attend_cross.1 = (bf16[1024,128]{1,0:T(8,128)(2,1)S(1)}, f32[128,1024]{1,0:T(8,128)S(1)}, f32[8,1024]{1,0:T(8,128)S(1)}) custom-call(s32[2]{0:T(128)S(1)} %pad_add_fusion.1.info_ref, bf16[1024,128]{1,0:T(8,128)(2,1)S(1)} %bitcast.692, bf16[4096,256]{1,0:T(8,128)(2,1)S(1)} %bitcast.680), custom_call_target="tpu_custom_call" | custom-call | flops 2147483648 | bytes 4194304 | tf_op jit(solution)/shard_map/attend_cross/pallas_call | solution.py:563
  299.0 13.2 %collective-permute-start.25 = (bf16[256,128]{1,0:T(8,128)(2,1)S(1)}, bf16[256,128]{1,0:T(8,128)(2,1)S(1)}, u32[]{:S(2)}, u32[]{:S(2)}) collective-permute-start(bf16[256,128]{1,0:T(8,128)(2,1)S(1)} %dynamic-slice_bitcast_fusion.30), channel_id=1, source_target_pairs={{0,2},{1,3},{2,4},{3,5},{4,6},{5,7},{6,0},{7,1},{8,10},{9,11},{10,... | collective-permute-start | bytes 196616 | tf_op jit(solution)/shard_map/ppermute | solution.py:648
  341.1 10.8 %collective-permute-done.30 = bf16[256,1472]{0,1:T(8,128)(2,1)S(1)} collective-permute-done((bf16[256,1472]{0,1:T(8,128)(2,1)}, bf16[256,1472]{0,1:T(8,128)(2,1)S(1)}, u32[]{:S(2)}, u32[]{:S(2)}) %collective-permute-start.30) | collective-permute-done | bytes 753696 | tf_op jit(solution)/shard_map/ppermute | solution.py:679
  388.2 15.4 %collective-permute-done.33 = bf16[256,1472]{0,1:T(8,128)(2,1)} collective-permute-done((bf16[256,1472]{0,1:T(8,128)(2,1)}, bf16[256,1472]{0,1:T(8,128)(2,1)}, u32[]{:S(2)}, u32[]{:S(2)}) %collective-permute-start.33) | collective-permute-done | bytes 753696 | tf_op jit(solution)/shard_map/ppermute | solution.py:828
  433.7 21.5 %attend_cross_back.1 = (bf16[1024,128]{1,0:T(8,128)(2,1)S(1)}, bf16[4096,256]{1,0:T(8,128)(2,1)S(1)}) custom-call(s32[2]{0:T(128)S(1)} %pad_add_fusion.1.info_ref, bf16[1024,128]{1,0:T(8,128)(2,1)S(1)} %bitcast.693, bf16[4096,256]{1,0:T(8,128)(2,1)S(1)} %bitcast.681, bf16[1024,128]{1,0:T(8,128)(2,1)S(1)} %bitcast.695, f32[128,1024]{1,0:T(8,128)S(1)} %copy-done.5, ...), custom_call_target="tpu_custom_call" | custom-call | flops 5368709120 | bytes 4194304 | tf_op jit(solution)/shard_map/attend_cross_back/pallas_call | solution.py:594
  468.4 8.9 %collective-permute-done.38 = bf16[256,128]{1,0:T(8,128)(2,1)S(1)} collective-permute-done((bf16[256,128]{1,0:T(8,128)(2,1)S(1)}, bf16[256,128]{1,0:T(8,128)(2,1)S(1)}, u32[]{:S(2)}, u32[]{:S(2)}) %collective-permute-start.38) | collective-permute-done | bytes 65568 | tf_op jit(solution)/shard_map/ppermute | solution.py:648
  477.3 30.7 %collective-permute-done.39 = bf16[256,128]{1,0:T(8,128)(2,1)S(1)} collective-permute-done((bf16[256,128]{1,0:T(8,128)(2,1)S(1)}, bf16[256,128]{1,0:T(8,128)(2,1)S(1)}, u32[]{:S(2)}, u32[]{:S(2)}) %collective-permute-start.39) | collective-permute-done | bytes 65568 | tf_op jit(solution)/shard_map/ppermute | solution.py:648
  508.0 10.8 %collective-permute-start.49 = (bf16[1024,256]{1,0:T(8,128)(2,1)}, bf16[1024,256]{1,0:T(8,128)(2,1)}, u32[]{:S(2)}, u32[]{:S(2)}) collective-permute-start(bf16[1024,256]{1,0:T(8,128)(2,1)} %get-tuple-element.154), channel_id=1, source_target_pairs={{0,6},{1,7},{2,0},{3,1},{4,2},{5,3},{6,4},{7,5},{8,14},{9,15},{10,... | collective-permute-start | bytes 1572872 | tf_op jit(solution)/shard_map/ppermute | solution.py:648
  528.4 13.3 %collective-permute-start.42 = (bf16[256,128]{0,1:T(8,128)(2,1)S(1)}, bf16[256,128]{0,1:T(8,128)(2,1)}, u32[]{:S(2)}, u32[]{:S(2)}) collective-permute-start(bf16[256,128]{0,1:T(8,128)(2,1)S(1)} %dynamic-slice_bitcast_fusion.21), channel_id=1, source_target_pairs={{0,2},{1,3},{2,4},{3,5},{4,6},{5,7},{6,0},{7,1},{8,10},{9,11},{10,... | collective-permute-start | bytes 196616 | tf_op jit(solution)/shard_map/ppermute | solution.py:648
  588.5 8.0 attend_self_back.1
  618.1 8.4 %collective-permute-done.53 = bf16[512,4,256]{2,0,1:T(8,128)(2,1)S(1)} collective-permute-done((bf16[512,4,256]{2,0,1:T(8,128)(2,1)S(1)}, bf16[512,4,256]{2,0,1:T(8,128)(2,1)S(1)}, u32[]{:S(2)}, u32[]{:S(2)}) %collective-permute-start.53) | collective-permute-done | bytes 1048608 | tf_op jit(solution)/shard_map/ppermute | solution.py:640
  718.3 7.4 dynamic-slice_maximum_fusion
  732.8 11.2 %collective-permute-done.60 = bf16[4,192,288]{1,0,2:T(4,128)(2,1)S(1)} collective-permute-done((bf16[4,192,288]{1,0,2:T(4,128)(2,1)}, bf16[4,192,288]{1,0,2:T(4,128)(2,1)S(1)}, u32[]{:S(2)}, u32[]{:S(2)}) %collective-permute-start.60) | collective-permute-done | bytes 442400 | tf_op jit(solution)/shard_map/ppermute | solution.py:675
  762.8 11.6 %collective-permute-done.66 = bf16[4,184,480]{2,1,0:T(8,128)(2,1)S(1)} collective-permute-done((bf16[4,184,480]{2,1,0:T(8,128)(2,1)S(1)}, bf16[4,184,480]{2,1,0:T(8,128)(2,1)S(1)}, u32[]{:S(2)}, u32[]{:S(2)}) %collective-permute-start.66) | collective-permute-done | bytes 706592 | tf_op jit(solution)/shard_map/ppermute | solution.py:675
  781.9 9.9 %collective-permute-done.68 = bf16[184,480]{1,0:T(8,128)(2,1)S(1)} collective-permute-done((bf16[184,480]{1,0:T(8,128)(2,1)S(1)}, bf16[184,480]{1,0:T(8,128)(2,1)S(1)}, u32[]{:S(2)}, u32[]{:S(2)}) %collective-permute-start.68) | collective-permute-done | bytes 176672 | tf_op jit(solution)/shard_map/ppermute | solution.py:648
  (627 shorter events, 438.1 us)
Async XLA Ops:
  7.2 96.9 %all-gather.3.cloned.1.call-start = ((), (), s32[]{:S(2)}) async-start(), calls=%async_computation.1 | async-start | bytes 9326592 | tf_op jit(solution)/shard_map/all_gather | solution.py:736
  10.0 317.7 %all-gather.5.cloned.1.call-start = ((), (), s32[]{:S(2)}) async-start(), calls=%async_computation.2 | async-start | bytes 8902656 | tf_op jit(solution)/shard_map/all_gather | solution.py:738
  39.2 43.9 %collective-permute-start.10 = (bf16[256,1472]{0,1:T(8,128)(2,1)S(1)}, bf16[256,1472]{0,1:T(8,128)(2,1)S(1)}, u32[]{:S(2)}, u32[]{:S(2)}) collective-permute-start(bf16[256,1472]{0,1:T(8,128)(2,1)S(1)} %fusion.62), channel_id=1, source_target_pairs={{0,16},{8,24},{16,0},{24,8},{1,17},{9,25},{17,1},{25,9},{2,18},{10... | collective-permute-start | bytes 2261000 | tf_op jit(solution)/shard_map/ppermute | solution.py:679
  39.8 43.4 %collective-permute-start.6 = (bf16[256,1472]{0,1:T(8,128)(2,1)}, bf16[256,1472]{0,1:T(8,128)(2,1)}, u32[]{:S(2)}, u32[]{:S(2)}) collective-permute-start(bf16[256,1472]{0,1:T(8,128)(2,1)} %pad_maximum_fusion.20), channel_id=1, source_target_pairs={{0,8},{8,0},{16,24},{24,16},{1,9},{9,1},{17,25},{25,17},{2,10},{10... | collective-permute-start | bytes 2261000 | tf_op jit(solution)/shard_map/ppermute | solution.py:680
  39.8 45.8 %collective-permute-start.9 = (bf16[256,1472]{0,1:T(8,128)(2,1)S(1)}, bf16[256,1472]{0,1:T(8,128)(2,1)}, u32[]{:S(2)}, u32[]{:S(2)}) collective-permute-start(bf16[256,1472]{0,1:T(8,128)(2,1)S(1)} %fusion.62), channel_id=1, source_target_pairs={{0,8},{8,0},{16,24},{24,16},{1,9},{9,1},{17,25},{25,17},{2,10},{10... | collective-permute-start | bytes 2261000 | tf_op jit(solution)/shard_map/ppermute | solution.py:680
  60.4 27.5 %collective-permute-start.8 = (bf16[256,1472]{0,1:T(8,128)(2,1)S(1)}, bf16[256,1472]{0,1:T(8,128)(2,1)}, u32[]{:S(2)}, u32[]{:S(2)}) collective-permute-start(bf16[256,1472]{0,1:T(8,128)(2,1)S(1)} %collective-permute-done.7), channel_id=1, source_target_pairs={{0,8},{8,0},{16,24},{24,16},{1,9},{9,1},{17,25},{25,17},{2,10},{10... | collective-permute-start | bytes 2261000 | tf_op jit(solution)/shard_map/ppermute | solution.py:681
  61.5 731.9 %reduce-scatter.4.cloned.1.call-start = ((), (), s32[]{:S(2)}) async-start(), calls=%async_computation.3 | async-start | bytes 8902656
  174.4 30.6 %collective-permute-start.19 = (bf16[1024,256]{1,0:T(8,128)(2,1)}, bf16[1024,256]{1,0:T(8,128)(2,1)}, u32[]{:S(2)}, u32[]{:S(2)}) collective-permute-start(bf16[1024,256]{1,0:T(8,128)(2,1)} %dynamic-slice_bitcast_fusion.7), channel_id=1, source_target_pairs={{0,2},{1,3},{2,4},{3,5},{4,6},{5,7},{6,0},{7,1},{8,10},{9,11},{10,... | collective-permute-start | bytes 1572872 | tf_op jit(solution)/shard_map/ppermute | solution.py:648
  232.3 45.0 %collective-permute-start.23 = (bf16[1024,256]{1,0:T(8,128)(2,1)}, bf16[1024,256]{1,0:T(8,128)(2,1)}, u32[]{:S(2)}, u32[]{:S(2)}) collective-permute-start(bf16[1024,256]{1,0:T(8,128)(2,1)} %get-tuple-element.158), channel_id=1, source_target_pairs={{0,4},{1,5},{2,6},{3,7},{4,0},{5,1},{6,2},{7,3},{8,12},{9,13},{10,... | collective-permute-start | bytes 1572872 | tf_op jit(solution)/shard_map/ppermute | solution.py:648
  237.4 39.7 %collective-permute-start.21 = (bf16[256,128]{0,1:T(8,128)(2,1)S(1)}, bf16[256,128]{0,1:T(8,128)(2,1)S(1)}, u32[]{:S(2)}, u32[]{:S(2)}) collective-permute-start(bf16[256,128]{0,1:T(8,128)(2,1)S(1)} %get-tuple-element.298), channel_id=1, source_target_pairs={{0,4},{1,5},{2,6},{3,7},{4,0},{5,1},{6,2},{7,3},{8,12},{9,13},{10,... | collective-permute-start | bytes 196616 | tf_op jit(solution)/shard_map/ppermute | solution.py:648
  239.7 38.7 %collective-permute-start.24 = (bf16[1024,256]{1,0:T(8,128)(2,1)}, bf16[1024,256]{1,0:T(8,128)(2,1)}, u32[]{:S(2)}, u32[]{:S(2)}) collective-permute-start(bf16[1024,256]{1,0:T(8,128)(2,1)} %get-tuple-element.157), channel_id=1, source_target_pairs={{0,6},{1,7},{2,0},{3,1},{4,2},{5,3},{6,4},{7,5},{8,14},{9,15},{10,... | collective-permute-start | bytes 1572872 | tf_op jit(solution)/shard_map/ppermute | solution.py:648
  242.4 34.7 %collective-permute-start.22 = (bf16[256,128]{0,1:T(8,128)(2,1)S(1)}, bf16[256,128]{0,1:T(8,128)(2,1)S(1)}, u32[]{:S(2)}, u32[]{:S(2)}) collective-permute-start(bf16[256,128]{0,1:T(8,128)(2,1)S(1)} %get-tuple-element.297), channel_id=1, source_target_pairs={{0,6},{1,7},{2,0},{3,1},{4,2},{5,3},{6,4},{7,5},{8,14},{9,15},{10,... | collective-permute-start | bytes 196616 | tf_op jit(solution)/shard_map/ppermute | solution.py:648
  359.8 43.8 %collective-permute-start.29 = (bf16[256,1472]{0,1:T(8,128)(2,1)}, bf16[256,1472]{0,1:T(8,128)(2,1)S(1)}, u32[]{:S(2)}, u32[]{:S(2)}) collective-permute-start(bf16[256,1472]{0,1:T(8,128)(2,1)} %slice.1757), channel_id=1, source_target_pairs={{0,8},{8,0},{16,24},{24,16},{1,9},{9,1},{17,25},{25,17},{2,10},{10... | collective-permute-start | bytes 2261000 | tf_op jit(solution)/shard_map/ppermute | solution.py:687
  433.6 29.7 %collective-permute-start.40 = (bf16[256,1472]{0,1:T(8,128)(2,1)S(1)}, bf16[256,1472]{0,1:T(8,128)(2,1)S(1)}, u32[]{:S(2)}, u32[]{:S(2)}) collective-permute-start(bf16[256,1472]{0,1:T(8,128)(2,1)S(1)} %slice.1755), channel_id=1, source_target_pairs={{0,8},{8,0},{16,24},{24,16},{1,9},{9,1},{17,25},{25,17},{2,10},{10... | collective-permute-start | bytes 2261000 | tf_op jit(solution)/shard_map/ppermute | solution.py:687
  463.3 78.4 %collective-permute-start.45 = (bf16[256,1472]{0,1:T(8,128)(2,1)}, bf16[256,1472]{0,1:T(8,128)(2,1)}, u32[]{:S(2)}, u32[]{:S(2)}) collective-permute-start(bf16[256,1472]{0,1:T(8,128)(2,1)} %slice.1754), channel_id=1, source_target_pairs={{0,8},{8,0},{16,24},{24,16},{1,9},{9,1},{17,25},{25,17},{2,10},{10... | collective-permute-start | bytes 2261000 | tf_op jit(solution)/shard_map/ppermute | solution.py:687
  464.1 54.7 %collective-permute-start.41 = (bf16[256,1472]{0,1:T(8,128)(2,1)S(1)}, bf16[256,1472]{0,1:T(8,128)(2,1)S(1)}, u32[]{:S(2)}, u32[]{:S(2)}) collective-permute-start(bf16[256,1472]{0,1:T(8,128)(2,1)S(1)} %fusion.77), channel_id=1, source_target_pairs={{0,16},{8,24},{16,0},{24,8},{1,17},{9,25},{17,1},{25,9},{2,18},{10... | collective-permute-start | bytes 2261000 | tf_op jit(solution)/shard_map/ppermute | solution.py:854
  466.5 121.9 %collective-permute-start.47 = (bf16[1024,256]{1,0:T(8,128)(2,1)}, bf16[1024,256]{1,0:T(8,128)(2,1)}, u32[]{:S(2)}, u32[]{:S(2)}) collective-permute-start(bf16[1024,256]{1,0:T(8,128)(2,1)} %get-tuple-element.156), channel_id=1, source_target_pairs={{0,2},{1,3},{2,4},{3,5},{4,6},{5,7},{6,0},{7,1},{8,10},{9,11},{10,... | collective-permute-start | bytes 1572872 | tf_op jit(solution)/shard_map/ppermute | solution.py:648
  467.4 121.0 %collective-permute-start.48 = (bf16[1024,256]{1,0:T(8,128)(2,1)}, bf16[1024,256]{1,0:T(8,128)(2,1)}, u32[]{:S(2)}, u32[]{:S(2)}) collective-permute-start(bf16[1024,256]{1,0:T(8,128)(2,1)} %get-tuple-element.155), channel_id=1, source_target_pairs={{0,4},{1,5},{2,6},{3,7},{4,0},{5,1},{6,2},{7,3},{8,12},{9,13},{10,... | collective-permute-start | bytes 1572872 | tf_op jit(solution)/shard_map/ppermute | solution.py:648
  477.3 30.7 %collective-permute-start.39 = (bf16[256,128]{1,0:T(8,128)(2,1)S(1)}, bf16[256,128]{1,0:T(8,128)(2,1)S(1)}, u32[]{:S(2)}, u32[]{:S(2)}) collective-permute-start(bf16[256,128]{1,0:T(8,128)(2,1)S(1)} %get-tuple-element.284), channel_id=1, source_target_pairs={{0,6},{1,7},{2,0},{3,1},{4,2},{5,3},{6,4},{7,5},{8,14},{9,15},{10,... | collective-permute-start | bytes 196616 | tf_op jit(solution)/shard_map/ppermute | solution.py:648
  508.0 80.4 %collective-permute-start.49 = (bf16[1024,256]{1,0:T(8,128)(2,1)}, bf16[1024,256]{1,0:T(8,128)(2,1)}, u32[]{:S(2)}, u32[]{:S(2)}) collective-permute-start(bf16[1024,256]{1,0:T(8,128)(2,1)} %get-tuple-element.154), channel_id=1, source_target_pairs={{0,6},{1,7},{2,0},{3,1},{4,2},{5,3},{6,4},{7,5},{8,14},{9,15},{10,... | collective-permute-start | bytes 1572872 | tf_op jit(solution)/shard_map/ppermute | solution.py:648
  528.4 36.3 %collective-permute-start.42 = (bf16[256,128]{0,1:T(8,128)(2,1)S(1)}, bf16[256,128]{0,1:T(8,128)(2,1)}, u32[]{:S(2)}, u32[]{:S(2)}) collective-permute-start(bf16[256,128]{0,1:T(8,128)(2,1)S(1)} %dynamic-slice_bitcast_fusion.21), channel_id=1, source_target_pairs={{0,2},{1,3},{2,4},{3,5},{4,6},{5,7},{6,0},{7,1},{8,10},{9,11},{10,... | collective-permute-start | bytes 196616 | tf_op jit(solution)/shard_map/ppermute | solution.py:648
  648.8 81.7 %collective-permute-start.55 = (bf16[128,1472]{0,1:T(8,128)(2,1)}, bf16[128,1472]{0,1:T(8,128)(2,1)}, u32[]{:S(2)}, u32[]{:S(2)}) collective-permute-start(bf16[128,1472]{0,1:T(8,128)(2,1)} %bitcast.672), channel_id=1, source_target_pairs={{0,1},{1,0},{2,3},{3,2},{4,5},{5,4},{6,7},{7,6},{8,9},{9,8},{10,11... | collective-permute-start | bytes 1130504 | tf_op jit(solution)/shard_map/ppermute | solution.py:640
  663.8 31.4 %collective-permute-start.58 = (f32[3,1472]{1,0:T(4,128)}, f32[3,1472]{1,0:T(4,128)}, u32[]{:S(2)}, u32[]{:S(2)}) collective-permute-start(f32[3,1472]{1,0:T(4,128)} %pad_maximum_fusion.29), channel_id=1, source_target_pairs={{0,8},{8,0},{16,24},{24,16},{1,9},{9,1},{17,25},{25,17},{2,10},{10... | collective-permute-start | bytes 53000 | tf_op jit(solution)/shard_map/ppermute | solution.py:915
  717.2 34.9 %collective-permute-start.65 = (bf16[480,1472]{1,0:T(8,128)(2,1)}, bf16[480,1472]{1,0:T(8,128)(2,1)}, u32[]{:S(2)}, u32[]{:S(2)}) collective-permute-start(bf16[480,1472]{1,0:T(8,128)(2,1)} %fusion.85), channel_id=1, source_target_pairs={{0,16},{8,24},{16,0},{24,8},{1,17},{9,25},{17,1},{25,9},{2,18},{10... | collective-permute-start | bytes 4239368 | tf_op jit(solution)/shard_map/ppermute | solution.py:910
  (144 other events, 1668.1 us)
Sparse Core Ops, SparseCore 0:
  11.6 92.5 all-gather.2
  106.3 167.1 all-gather.4
  413.5 183.7 reduce-scatter.3

commit v3 on v2

--- a/solution.py
+++ b/solution.py
@@ -348,9 +348,6 @@
     )
 
 
-FOLD = 2
-
-
 def _masked_rows(is_second, shape, axis):
     index = lax.broadcasted_iota(jnp.int32, shape, axis)
     return (index >= HEAD_DIM) == is_second
@@ -379,6 +376,13 @@
     chunks = (count + size - 1) // size
     if causal:
         chunks = jnp.minimum(chunks, ((block + 1) * wide + size - 1) // size)
+    return chunks
+
+
+def _full_count(count, block, wide, size, causal):
+    chunks = count // size
+    if causal:
+        chunks = jnp.minimum(chunks, block * wide // size)
     return chunks
 
 
@@ -413,14 +417,19 @@
         queries = queries.astype(jnp.bfloat16)
         chunks = _chunk_count(count, block, wide, size, causal)
 
-        def scores(c, top):
+        full = _full_count(count, block, wide, size, causal)
+
+        def scores(masked, c, top):
             spot = pl.multiple_of(c * size, size)
             s = jnp.dot(k_ref[pl.ds(spot, size), :], queries, preferred_element_type=jnp.float32)
-            s = jnp.where(_score_mask(c, size, block, count, wide, causal), s, NEGATIVE)
+            if masked:
+                s = jnp.where(_score_mask(c, size, block, count, wide, causal), s, NEGATIVE)
             score_ref[pl.ds(spot, size), :] = s
             return jnp.maximum(top, jnp.max(s.reshape(size // 8, 8, wide), axis=0))
 
-        top = lax.fori_loop(0, chunks, scores, jnp.full((8, wide), NEGATIVE, jnp.float32))
+        top = jnp.full((8, wide), NEGATIVE, jnp.float32)
+        top = lax.fori_loop(0, full, functools.partial(scores, False), top)
+        top = lax.fori_loop(full, chunks, functools.partial(scores, True), top)
         top = jnp.max(top, axis=0, keepdims=True)
 
         def weigh(c, carry):
@@ -507,10 +516,13 @@
         dtotal = dtotal.astype(jnp.bfloat16).astype(jnp.float32)
         chunks = _chunk_count(count, block, wide, size, causal)
 
-        def one(c, dq):
+        full = _full_count(count, block, wide, size, causal)
+
+        def one(masked, c, dq):
             spot = pl.multiple_of(c * size, size)
             s = jnp.dot(k_ref[pl.ds(spot, size), :], q_cols, preferred_element_type=jnp.float32)
-            s = jnp.where(_score_mask(c, size, block, count, wide, causal), s, NEGATIVE)
+            if masked:
+                s = jnp.where(_score_mask(c, size, block, count, wide, causal), s, NEGATIVE)
             e = jnp.exp(s - top)
             through = jnp.dot(v_ref[pl.ds(spot, size), :], dn_cols, preferred_element_type=jnp.float32)
             ds = (e * (through + dtotal)).astype(jnp.bfloat16)
@@ -522,7 +534,9 @@
             )
             return dq + jnp.dot(kt_ref[:, pl.ds(spot, size)], ds, preferred_element_type=jnp.float32)
 
-        dq = lax.fori_loop(0, chunks, one, jnp.zeros((lanes, wide), jnp.float32))
+        dq = jnp.zeros((lanes, wide), jnp.float32)
+        dq = lax.fori_loop(0, full, functools.partial(one, False), dq)
+        dq = lax.fori_loop(full, chunks, functools.partial(one, True), dq)
         back = jnp.transpose(jnp.where(mine, dq, 0.0))
 
         @pl.when(jnp.logical_not(second))
@@ -609,90 +623,16 @@
     )(info, *parts, dmix, mixed, stats)
 
 
-def spread_heads(array):
-    d = HEAD_DIM
-    pick = lambda h: array[..., h * d : (h + 1) * d]
-    return jnp.stack(
-        [jnp.concatenate([pick(a), pick(b)], axis=-1) for a, b in ((0, 1), (2, 1), (3, 4), (5, 4))]
-    )
-
-
-def merge_heads(array):
-    d = HEAD_DIM
-    wide = array.astype(jnp.float32)
-    first = [wide[j, ..., :d] for j in range(4)]
-    shared = [wide[j, ..., d:] + wide[j + 1, ..., d:] for j in (0, 2)]
-    return jnp.concatenate(
-        [first[0], shared[0], first[1], first[2], shared[1], first[3]], axis=-1
-    ).astype(jnp.bfloat16)
-
-
-def by_document(array, x_rank, swap):
-    own = lax.dynamic_index_in_dim(array, x_rank, 0, False)
-    other = lax.ppermute(lax.dynamic_index_in_dim(array, 1 - x_rank, 0, False), "seq", swap)
-    first = x_rank == 0
-    return jnp.concatenate([jnp.where(first, own, other), jnp.where(first, other, own)], axis=0)
-
-
-def by_position(array, x_rank, swap):
-    pair = array.reshape((2, array.shape[0] // 2) + array.shape[1:])
-    own = lax.dynamic_index_in_dim(pair, x_rank, 0, False)
-    other = lax.ppermute(lax.dynamic_index_in_dim(pair, 1 - x_rank, 0, False), "seq", swap)
-    first = x_rank == 0
-    return jnp.stack([jnp.where(first, own, other), jnp.where(first, other, own)])
-
-
-def send_z(array, z_rank, shifts):
-    count = array.shape[0]
-    return [
-        lax.ppermute(lax.dynamic_index_in_dim(array, (z_rank + k) % count, 0, False), "seq", shifts[k])
-        for k in range(1, count)
-    ]
-
-
-def place_z(array, arrived, z_rank):
-    count = array.shape[0]
-    out = array
-    for k in range(1, count):
-        out = lax.dynamic_update_index_in_dim(out, arrived[k - 1], (z_rank - k) % count, 0)
-    return out
-
-
-def exchange_z(array, z_rank, shifts):
-    return place_z(array, send_z(array, z_rank, shifts), z_rank)
-
-
-def add_z(array, z_rank, shifts):
-    total = lax.dynamic_index_in_dim(array, z_rank, 0, False).astype(jnp.float32)
-    for arrived in send_z(array, z_rank, shifts):
-        total = total + arrived.astype(jnp.float32)
-    return total
-
-
-def add_x(array, x_rank, swap):
-    keep = lax.dynamic_index_in_dim(array, x_rank, 1, False).astype(jnp.float32)
-    send = lax.dynamic_index_in_dim(array, 1 - x_rank, 1, False)
-    return (keep + lax.ppermute(send, "seq", swap).astype(jnp.float32)).astype(jnp.bfloat16)
-
-
-def gather_doc(array, pairs_core, pairs_y):
-    across = lax.ppermute(array, "doc", pairs_y)
-    beside = lax.ppermute(array, "doc", pairs_core)
-    far = lax.ppermute(across, "doc", pairs_core)
-    return jnp.concatenate([array, beside], axis=0), jnp.concatenate([across, far], axis=0)
-
-
-def add_core(array, pairs_core):
-    n = array.shape[0] // 2
-    return array[:n] + lax.ppermute(array[n:].astype(jnp.bfloat16), "doc", pairs_core).astype(jnp.float32)
-
-
-def relative_doc(array, core_rank, y_rank):
-    a, b, c, d = (array[..., i, :] for i in range(4))
-    even = core_rank == 0
-    a, b, c, d = (jnp.where(even, a, b), jnp.where(even, b, a), jnp.where(even, c, d), jnp.where(even, d, c))
-    low = y_rank == 0
-    return [jnp.where(low, a, c), jnp.where(low, b, d), jnp.where(low, c, a), jnp.where(low, d, b)]
+def take(array, index, axis=0):
+    return lax.dynamic_index_in_dim(array, index, axis, False)
+
+
+def put(array, piece, index):
+    return lax.dynamic_update_index_in_dim(array, piece, index, 0)
+
+
+def twins(first, own, other):
+    return jnp.where(first, jnp.stack([own, other]), jnp.stack([other, own]))
 
 
 def by_heads(
@@ -717,61 +657,170 @@
     doc_ranks, seq_ranks = lax.axis_size("doc"), lax.axis_size("seq")
     seq_rank, doc_rank = lax.axis_index("seq"), lax.axis_index("doc")
     z_rank, x_rank = seq_rank // 2, seq_rank % 2
-    y_rank, core_rank = doc_rank // 2, doc_rank % 2
-    swap = [(i, i ^ 1) for i in range(seq_ranks)]
-    shifts = [[(i, (i + 2 * k) % seq_ranks) for i in range(seq_ranks)] for k in range(seq_ranks // 2)]
-    pairs_core = [(i, i ^ 1) for i in range(doc_ranks)]
-    pairs_y = [(i, i ^ 2) for i in range(doc_ranks)]
-    inner = HEADS * HEAD_DIM
+    units = seq_ranks // 2
+    column_pairs = [(i, i ^ 1) for i in range(seq_ranks)]
+    shifts = [[(i, (i + 2 * k) % seq_ranks) for i in range(seq_ranks)] for k in range(units)]
     lanes = 2 * HEAD_DIM
-    share = inner // doc_ranks
+    share = HEADS * HEAD_DIM // doc_ranks
+    rest = share - HEAD_DIM
     depth = width // seq_ranks
     rows = docs_here * rows_doc
     slots = docs_here * slots_doc
+    hidden_here = ff_in.shape[2]
+    even = doc_rank % 2 == 0
+    first = x_rank == 0
+
+    def swap_x(array):
+        return lax.ppermute(array, "seq", column_pairs)
+
+    def swap_y(array):
+        return lax.ppermute(array, "doc", [(i, i ^ 2) for i in range(doc_ranks)])
+
+    def swap_core(array):
+        return lax.ppermute(array, "doc", [(i, i ^ 1) for i in range(doc_ranks)])
+
+    def shift_z(array, k):
+        return lax.ppermute(array, "seq", shifts[k % units])
+
+    def by_document(array):
+        pair = twins(first, take(array, x_rank), swap_x(take(array, 1 - x_rank)))
+        return pair.reshape((-1,) + pair.shape[2:])
+
+    def by_position(array):
+        pair = array.reshape((2, array.shape[0] // 2) + array.shape[1:])
+        return twins(first, take(pair, x_rank), swap_x(take(pair, 1 - x_rank)))
+
+    def gather_z(array):
+        out = jnp.broadcast_to(array, (units,) + array.shape)
+        for k in range(1, units):
+            out = put(out, shift_z(array, k), (z_rank - k) % units)
+        return out
+
+    def send_units(array):
+        return [take(array, z_rank)] + [
+            shift_z(take(array, (z_rank + k) % units), k) for k in range(1, units)
+        ]
+
+    def to_unit(array):
+        out = array
+        for k, arrived in enumerate(send_units(array)):
+            out = put(out, arrived, (z_rank - k) % units)
+        return out.reshape((-1,) + out.shape[2:])
+
+    def to_rows(array):
+        array = array.reshape((units, -1) + array.shape[1:])
+        out = array
+        for k in range(units):
+            piece = take(array, (z_rank + k) % units)
+            piece = shift_z(piece, k) if k else piece
+            out = put(out, piece, (z_rank - k) % units)
+        return out
+
+    def return_units(pieces):
+        out = jnp.zeros((units,) + pieces[0].shape, pieces[0].dtype)
+        for k, piece in enumerate(pieces):
+            arrived = shift_z(piece, units - k) if k else piece
+            out = put(out, arrived, (z_rank + k) % units)
+        return out
+
+    def gather_doc(array):
+        across, beside = swap_y(array), swap_core(array)
+        return jnp.concatenate([array, beside], axis=0), jnp.concatenate([across, swap_core(across)], axis=0)
+
+    def add_core(array):
+        n = array.shape[0] // 2
+        return array[:n] + swap_core(array[n:].astype(bf16)).astype(f32)
+
+    def add_x(array):
+        arrived = swap_x(take(array, 1 - x_rank, 1))
+        return (take(array, x_rank, 1).astype(f32) + arrived.astype(f32)).astype(bf16)
+
+    def add_z(array):
+        total = take(array, z_rank).astype(f32)
+        for k in range(1, units):
+            total = total + shift_z(take(array, (z_rank + k) % units), k).astype(f32)
+        return total
+
+    def whole_first(block):
+        return jnp.where(even, block, jnp.concatenate([block[:, rest:], block[:, :rest]], axis=1))
+
+    def whole_back(block):
+        return jnp.where(even, block, jnp.concatenate([block[:, HEAD_DIM:], block[:, :HEAD_DIM]], axis=1))
+
+    def spread(out, parts):
+        pieces = []
+        for j in range(doc_ranks):
+            line = []
+            for i in range(parts):
+                line.append(out[j, :, i * share : (i + 1) * share])
+                line.append(out[j ^ 1, :, i * share + HEAD_DIM : (i + 1) * share])
+            pieces.append(jnp.concatenate(line, axis=1))
+        return jnp.stack(pieces)
+
+    def merge(array, parts):
+        wide_in = array.astype(f32)
+        pieces = []
+        for j in range(doc_ranks):
+            line = []
+            for i in range(parts):
+                at = i * lanes
+                line.append(wide_in[j, :, at : at + HEAD_DIM])
+                line.append(
+                    wide_in[j, :, at + HEAD_DIM : at + share] + wide_in[j ^ 1, :, at + share : at + lanes]
+                )
+            pieces.append(jnp.concatenate(line, axis=1))
+        return jnp.stack(pieces).astype(bf16)
+
+    def spread_weight(block, parts):
+        return spread(block, parts)
+
+    def project_wide(rows_in, weight):
+        return jnp.einsum("td,jdk->jtk", rows_in, weight, preferred_element_type=f32).astype(bf16)
+
+    def project(rows_in, weight, parts):
+        return spread(project_wide(rows_in, weight), parts)
+
+    def lift(inner_in, weight):
+        return jnp.einsum("jtk,jdk->td", inner_in, weight, preferred_element_type=f32)
+
+    def fold(terms, parts):
+        terms = terms.reshape(doc_ranks, parts, lanes, width)
+        other = jnp.stack([terms[j ^ 1, :, share:] for j in range(doc_ranks)]).astype(f32)
+        split = (terms[:, :, HEAD_DIM:share].astype(f32) + other).astype(bf16)
+        return jnp.concatenate([terms[:, :, :HEAD_DIM], split], axis=2).reshape(doc_ranks, parts * share, width)
+
+    def outer(inner_in, rows_in):
+        return jnp.einsum("jtk,td->jkd", inner_in, rows_in, preferred_element_type=f32).astype(bf16)
+
+    part = z_rank % 2
+    info_self = jnp.stack([take(tgt_len, x_rank), part])
+    info_cross = jnp.stack([take(enc_len, x_rank), part])
 
     small = jnp.concatenate(
-        [self_qkv[0], self_qkv[1], self_qkv[2], cross_q, cross_kv[0], cross_kv[1], self_out.T, cross_out.T],
+        [
+            whole_first(b)
+            for b in (
+                self_qkv[0],
+                self_qkv[1],
+                self_qkv[2],
+                cross_q,
+                cross_kv[0],
+                cross_kv[1],
+                self_out.T,
+                cross_out.T,
+            )
+        ],
         axis=1,
     )
     every = lax.all_gather(small, ("doc", "seq"), axis=0, tiled=True)
     ff_mine = jnp.concatenate([ff_in[0], ff_in[1], ff_out.T], axis=1)
     ff_all = lax.all_gather(ff_mine, "seq", axis=0, tiled=True)
-    hidden_here = ff_in.shape[2]
-
-    gain_other = lax.ppermute(gains, "seq", swap)
-    gain_pair = jnp.where(x_rank == 0, jnp.stack([gains, gain_other]), jnp.stack([gain_other, gains]))
-    gain_all = jnp.broadcast_to(gain_pair, (seq_ranks // 2,) + gain_pair.shape)
-    gain_all = exchange_z(gain_all, z_rank, shifts)
-    gain_all = gain_all.transpose(2, 0, 1, 3).reshape(3, width).astype(f32)
-
-    def project(rows_in, weight, parts):
-        out = jnp.einsum("td,edk->etk", rows_in, weight, preferred_element_type=f32).astype(bf16)
-        return [
-            jnp.concatenate([out[e, :, i * share : (i + 1) * share] for e in range(doc_ranks)], axis=-1)
-            for i in range(parts)
-        ]
-
-    def lift(inner_in, weight):
-        split = inner_in.reshape(inner_in.shape[0], doc_ranks, share)
-        return jnp.einsum("tek,edk->td", split, weight, preferred_element_type=f32)
-
-    def outer(inner_in, rows_in):
-        parts = relative_doc(inner_in.reshape(inner_in.shape[0], doc_ranks, share), core_rank, y_rank)
-        every_part = jnp.concatenate(parts, axis=-1)
-        return matmul_outer(every_part, rows_in).astype(bf16).reshape(doc_ranks, share, width)
-
-    info_self = jnp.stack([lax.dynamic_index_in_dim(tgt_len, x_rank, 0, False), z_rank % 2])
-    info_cross = jnp.stack([lax.dynamic_index_in_dim(enc_len, x_rank, 0, False), z_rank % 2])
-
-    stream = by_document(dec_in, x_rank, swap).astype(f32)
-    cot = by_document(cotangent, x_rank, swap)
+    gain_pair = twins(first, gains, swap_x(gains))
+    gain_all = gather_z(gain_pair).transpose(2, 0, 1, 3).reshape(3, width).astype(f32)
+    stream = by_document(dec_in).astype(f32)
     normed1, inverse1 = norm_parts(stream, gain_all[0])
     normed1 = normed1.astype(bf16)
-    cot_near, cot_far = gather_doc(cot, pairs_core, pairs_y)
-    n1_near, n1_far = gather_doc(normed1, pairs_core, pairs_y)
-    every, normed1, cot_near, cot_far, n1_near, n1_far = tie(
-        (every, normed1, cot_near, cot_far, n1_near, n1_far)
-    )
+    every, normed1, cotangent = tie((every, normed1, cotangent))
     every = every.reshape(doc_ranks, width, 8 * share)
     w_qkv = every[:, :, : 3 * share]
     w_cq = every[:, :, 3 * share : 4 * share]
@@ -779,27 +828,33 @@
     w_so = every[:, :, 6 * share : 7 * share]
     w_co = every[:, :, 7 * share :]
 
-    qkv = jnp.concatenate([spread_heads(p) for p in project(normed1, w_qkv, 3)], axis=-1)
-    qkv_heads = exchange_z(qkv, z_rank, shifts).reshape(4 * rows, 3 * lanes)
+    qkv_rows = project(normed1, w_qkv, 3)
+    qkv_heads = to_unit(qkv_rows)
     enc_rows = enc_in.reshape(slots, width)
-    ckv = jnp.concatenate([spread_heads(p) for p in project(enc_rows, w_ckv, 2)], axis=-1)
-    ckv = ckv.reshape(4, docs_here, slots_doc, 2 * lanes).transpose(1, 2, 0, 3)
-    ckv = by_document(ckv, x_rank, swap).transpose(1, 0, 2)
-    qkv_heads, ckv = tie((qkv_heads, ckv))
-    ckv_arrived = send_z(ckv, z_rank, shifts)
+    w_kv = spread_weight(w_ckv, 2)
+    ckv = project_wide(enc_rows, w_kv).reshape(units, docs_here, slots_doc, 2 * lanes)
+    ckv_other = swap_x(take(ckv, 1 - x_rank, 1))
+    ckv_own = to_unit(take(ckv, x_rank, 1))
+    qkv_heads, ckv, cotangent = tie((qkv_heads, ckv, cotangent))
     att1, mix1, stat1 = attention(info_self, (qkv_heads,), True)
-    att1 = exchange_z(att1.reshape(4, rows, lanes), z_rank, shifts)
-    att1, ckv_arrived[0] = tie((att1, ckv_arrived[0]))
-    att1 = merge_heads(att1)
+    att1 = to_rows(att1)
+    att1, ckv_other = tie((att1, ckv_other))
+    ckv_other = to_unit(ckv_other)
+    att1 = merge(att1, 1)
+    cot = by_document(cotangent)
+    cot_near, cot_far = gather_doc(cot)
     stream1 = stream + lift(att1, w_so)
     normed2, inverse2 = norm_parts(stream1, gain_all[1])
     normed2 = normed2.astype(bf16)
-    (cq,) = project(normed2, w_cq, 1)
-    cq_heads = exchange_z(spread_heads(cq), z_rank, shifts).reshape(4 * rows, lanes)
-    ckv_heads = place_z(ckv, ckv_arrived, z_rank).reshape(4 * slots, 2 * lanes)
-
+    cq_heads = to_unit(project(normed2, w_cq, 1))
+    cq_heads, normed1 = tie((cq_heads, normed1))
+    n1_near, n1_far = gather_doc(normed1)
+    halves = (ckv_own.reshape(units, slots_doc, 2 * lanes), ckv_other.reshape(units, slots_doc, 2 * lanes))
+    ckv_heads = jnp.where(first, jnp.stack(halves, axis=1), jnp.stack(halves[::-1], axis=1))
+    ckv_heads = ckv_heads.reshape(units * slots, 2 * lanes)
     att2, mix2, stat2 = attention(info_cross, (cq_heads, ckv_heads), False)
-    att2 = merge_heads(exchange_z(att2.reshape(4, rows, lanes), z_rank, shifts))
+    att2 = merge(to_rows(att2), 1)
+    att2, n1_near, n1_far, cot_near, cot_far = tie((att2, n1_near, n1_far, cot_near, cot_far))
     stream2 = stream1 + lift(att2, w_co)
     normed3, inverse3 = norm_parts(stream2, gain_all[2])
     normed3 = normed3.astype(bf16)
@@ -820,13 +875,12 @@
     def through(d_gate, d_up):
         return matmul_back(d_gate, w_gate) + matmul_back(d_up, w_up)
 
-    n3_near, n3_far = gather_doc(normed3, pairs_core, pairs_y)
+    n3_near, n3_far = gather_doc(normed3)
     hid_near, dg_near, du_near = inside(n3_near, cot_near)
     hid_near, n3_far = tie((hid_near, n3_far))
     hid_far, dg_far, du_far = inside(n3_far, cot_far)
-    dn3_far = add_core(through(dg_far, du_far), pairs_core).astype(bf16)
-    dn3_across = lax.ppermute(dn3_far, "doc", pairs_y)
-    dn3_near = add_core(through(dg_near, du_near), pairs_core)
+    dn3_across = swap_y(add_core(through(dg_far, du_far)).astype(bf16))
+    dn3_near = add_core(through(dg_near, du_near))
     n3_all = jnp.concatenate([n3_near, n3_far], axis=0)
     cot_all = jnp.concatenate([cot_near, cot_far], axis=0)
     d_gate = jnp.concatenate([dg_near, dg_far], axis=0)
@@ -847,83 +901,71 @@
     back_three, gain_grad3 = norm_back(stream2, inverse3, gain_all[2], d_normed3)
     d_stream2 = cot.astype(f32) + back_three
     d_branch2 = d_stream2.astype(bf16)
-    (d_mix2,) = project(d_branch2, w_co, 1)
-    d_mix2 = exchange_z(spread_heads(d_mix2), z_rank, shifts).reshape(4 * rows, lanes)
+    d_mix2 = to_unit(project(d_branch2, w_co, 1))
     d_mix2, hidden_late = tie((d_mix2, hidden))
-    branch_far = add_core(matmul_back(hidden_late[2 * rows :], w_down), pairs_core).astype(bf16)
-    branch_across = lax.ppermute(branch_far, "doc", pairs_y)
-    branch = add_core(matmul_back(hidden_late[: 2 * rows], w_down), pairs_core)
+    branch_across = swap_y(add_core(matmul_back(hidden_late[2 * rows :], w_down)).astype(bf16))
+    branch = add_core(matmul_back(hidden_late[: 2 * rows], w_down))
     d_cq, d_ckv = attention_back(info_cross, (cq_heads, ckv_heads), d_mix2, mix2, stat2, False)
-    d_ckv = d_ckv.reshape(4, slots, 2 * lanes)
-    d_ckv_arrived = send_z(d_ckv, z_rank, shifts)
-    d_cq = exchange_z(d_cq.reshape(4, rows, lanes), z_rank, shifts)
-    d_cq, branch_across = tie((d_cq, branch_across))
-    layer_out = by_position(stream2 + (branch + branch_across.astype(f32)), x_rank, swap)
-    d_cq = merge_heads(d_cq)
+    d_ckv = d_ckv.reshape(units, 2, slots_doc, 2 * lanes)
+    d_cq = to_rows(d_cq)
+    d_cq, d_ckv, branch_across = tie((d_cq, d_ckv, branch_across))
+    d_ckv_other = to_rows(take(d_ckv, 1 - x_rank, 1).reshape(-1, 2 * lanes))
+    d_cq = merge(d_cq, 1)
     back_two, gain_grad2 = norm_back(stream1, inverse2, gain_all[1], lift(d_cq, w_cq))
     d_stream1 = d_stream2 + back_two
     d_branch1 = d_stream1.astype(bf16)
-    (d_mix1,) = project(d_branch1, w_so, 1)
-    d_mix1 = exchange_z(spread_heads(d_mix1), z_rank, shifts).reshape(4 * rows, lanes)
-    d_mix1, layer_out, *d_ckv_arrived = tie((d_mix1, layer_out, *d_ckv_arrived))
-    d_ckv = place_z(d_ckv, d_ckv_arrived, z_rank)
-    d_stream1_out = by_position(d_stream1, x_rank, swap)
+    d_branch1, d_ckv = tie((d_branch1, d_ckv))
+    d_mix1 = to_unit(project(d_branch1, w_so, 1))
+    d_ckv_own = to_rows(take(d_ckv, x_rank, 1).reshape(-1, 2 * lanes))
+    d_mix1, d_ckv_other = tie((d_mix1, d_ckv_other))
+    d_ckv_other = swap_x(d_ckv_other)
     (d_qkv,) = attention_back(info_self, (qkv_heads,), d_mix1, mix1, stat1, True)
-    d_qkv = exchange_z(d_qkv.reshape(4, rows, 3 * lanes), z_rank, shifts)
-    d_ckv = by_position(d_ckv.transpose(1, 0, 2), x_rank, swap)
-    d_qkv, d_ckv, d_stream1_out = tie((d_qkv, d_ckv, d_stream1_out))
-    d_q, d_k, d_v = (merge_heads(d_qkv[..., i * lanes : (i + 1) * lanes]) for i in range(3))
-
-    by_doc = jnp.concatenate(
-        [d.reshape(rows, doc_ranks, share) for d in (d_q, d_k, d_v)], axis=-1
-    )
-    own, beside, across, far = relative_doc(by_doc, core_rank, y_rank)
-    arrived = lax.ppermute(jnp.stack([beside, far]), "doc", pairs_core)
-    across = jnp.concatenate([across, arrived[1]], axis=0)
-    d_near = jnp.concatenate([own, arrived[0]], axis=0)
-    d_far = lax.ppermute(across, "doc", pairs_y)
-    d_normed1 = (
-        lift(d_q, w_qkv[:, :, :share])
-        + lift(d_k, w_qkv[:, :, share : 2 * share])
-        + lift(d_v, w_qkv[:, :, 2 * share :])
-    )
-    back_one, gain_grad1 = norm_back(stream, inverse1, gain_all[0], d_normed1)
-    dec_grad = d_stream1_out + by_position(back_one.astype(bf16), x_rank, swap).astype(f32)
-
-    d_ckv = d_ckv.reshape(slots, 4, 2 * lanes).transpose(1, 0, 2)
-    d_ck, d_cv = (merge_heads(d_ckv[..., i * lanes : (i + 1) * lanes]) for i in range(2))
-    enc_grad = lift(d_ck, w_ckv[:, :, :share]) + lift(d_cv, w_ckv[:, :, share:])
-    enc_grad = enc_grad.reshape(docs_here, slots_doc, width)
+    d_qkv, d_ckv_own, d_ckv_other, d_stream1, branch = tie((d_qkv, d_ckv_own, d_ckv_other, d_stream1, branch))
+    d_qkv = to_rows(d_qkv)
+    d_ckv = jnp.where(first, jnp.stack([d_ckv_own, d_ckv_other], axis=1), jnp.stack([d_ckv_other, d_ckv_own], axis=1))
+    d_ckv = d_ckv.reshape(units, slots, 2 * lanes)
+    enc_grad = lift(d_ckv, w_kv).reshape(docs_here, slots_doc, width)
+    layer_out = by_position(stream2 + (branch + branch_across.astype(f32)))
+    d_qkv, enc_grad, layer_out = tie((d_qkv, enc_grad, layer_out))
+    d_qkv = merge(d_qkv, 3)
+
+    def beside(array, k):
+        return take(array, doc_rank ^ k)
+
+    arrived = swap_core(jnp.stack([beside(d_qkv, 1), beside(d_qkv, 3)]))
+    d_near = jnp.concatenate([beside(d_qkv, 0), arrived[0]], axis=0)
+    d_far = swap_y(jnp.concatenate([beside(d_qkv, 2), arrived[1]], axis=0))
+    back_one, gain_grad1 = norm_back(stream, inverse1, gain_all[0], lift(d_qkv, w_qkv))
+    dec_grad = by_position(d_stream1 + back_one)
 
     terms = jnp.concatenate(
         [
             outer(d_cq, normed2),
-            outer(d_ck, enc_rows),
-            outer(d_cv, enc_rows),
+            fold(outer(d_ckv, enc_rows), 2),
             outer(att1, d_branch1),
             outer(att2, d_branch2),
         ],
         axis=1,
     )
-    arrived = lax.ppermute(jnp.stack([terms[1], terms[3]]), "doc", pairs_core).astype(f32)
-    across = (terms[2].astype(f32) + arrived[1]).astype(bf16)
-    terms = (terms[0].astype(f32) + arrived[0]) + lax.ppermute(across, "doc", pairs_y).astype(f32)
-    terms = terms.astype(bf16).T.reshape(seq_ranks // 2, 2, depth, 5 * share)
-    others = add_z(add_x(terms, x_rank, swap), z_rank, shifts)
+    arrived = swap_core(jnp.stack([beside(terms, 1), beside(terms, 3)])).astype(f32)
+    across = swap_y((beside(terms, 2).astype(f32) + arrived[1]).astype(bf16))
+    terms = (beside(terms, 0).astype(f32) + arrived[0]) + across.astype(f32)
+    terms = terms.astype(bf16).T.reshape(units, 2, depth, 5 * share)
+    others = add_z(add_x(terms))
 
     gain_terms = jnp.stack([gain_grad1, gain_grad2, gain_grad3])
-    gain_terms = gain_terms + lax.ppermute(gain_terms, "doc", pairs_core)
-    gain_terms = gain_terms + lax.ppermute(gain_terms, "doc", pairs_y)
+    gain_terms = gain_terms + swap_core(gain_terms)
+    gain_terms = gain_terms + swap_y(gain_terms)
     gain_terms = gain_terms.reshape(3, seq_ranks, depth).transpose(1, 0, 2)
     gain_terms = gain_terms.reshape(seq_ranks, 2, 3 * depth // 2).astype(bf16)
     gain_terms = jnp.pad(gain_terms, ((0, 0), (0, 6), (0, 3 * share - 3 * depth // 2)))
     grad_qkv = matmul_outer(n1_near, d_near) + matmul_outer(n1_far, d_far)
     grad_qkv = grad_qkv.astype(bf16).reshape(seq_ranks, depth, 3 * share)
     grad_qkv = jnp.concatenate([grad_qkv, gain_terms], axis=1)
-    grad_qkv = grad_qkv.reshape(seq_ranks // 2, 2, depth + 8, 3 * share)
-    summed = add_z(add_x(grad_qkv, x_rank, swap), z_rank, shifts)
+    grad_qkv = grad_qkv.reshape(units, 2, depth + 8, 3 * share)
+    summed = add_z(add_x(grad_qkv))
     grad_gains = summed[depth : depth + 2, : 3 * depth // 2].reshape(3, depth)
-    piece = lambda a, i: a[:depth, i * share : (i + 1) * share]
+    piece = lambda a, i: whole_back(a[:depth, i * share : (i + 1) * share])
     ff_sum = ff_sum.astype(f32)
     return (
         layer_out,

time: 811 us -> 754 us (0.930)
  waiting for transfers between devices: 283 us -> 264 us
  matrix products: 108 us -> 92 us
  other arithmetic: 80 us -> 65.1 us
    ppermute x70 -> x75, waiting for transfers between devices: 271 us -> 202 us  [the longest x45 116 us: shift_z(): return lax.ppermute(array, 'seq', shifts[k % units])]
    all_gather x1, waiting for transfers between devices: 12.6 us -> 61.5 us  [by_heads(): every = lax.all_gather(small, ('doc', 'seq'), axis=0, tiled=True)]
    dynamic_slice x6 -> x32, local copies, waits for them, and re-layouts: 12.5 us -> 33.3 us  [take(): return lax.dynamic_index_in_dim(array, index, axis, False)]
    concatenate x18 -> x2, local copies, waits for them, and re-layouts: 16.5 us -> 0.92 us  [the longest x1 0.91 us: by_heads(): jnp.concatenate([whole_first(b) for b in (self_qkv[0], self_qkv[1], self_...]
    dot_general x10 -> x5, matrix products: 28.9 us -> 14.1 us  [matmul_outer(): lax.dot_general(left_op, right_op, (((0,), (0,)), ((), ())), preferred_el...]
    dynamic_update_slice x28 -> x51, local copies, waits for them, and re-layouts: 6.61 us -> 18.2 us  [put(): return lax.dynamic_update_index_in_dim(array, piece, index, 0)]
    convert_element_type x5 -> x0, local copies, waits for them, and re-layouts: 10.3 us -> none  [outer(): matmul_outer(every_part, rows_in).astype(bf16)]
    unnamed x199 -> x217, local copies, waits for them, and re-layouts: 24.4 us -> 30.2 us
  transfers between devices with their start and end apart: 73 -> 78, of which waited for: 36 -> 28; matrix products, arithmetic and copies ran while one was open for 36% -> 33% of each run, Pallas kernels for 7% -> 7%
where the time goes in v3:
time: 754 us; the launch traced here: 748 us
  waiting for transfers between devices  264 us (35%)
  starting transfers between devices  137 us (18%)
  local copies, waits for them, and re-layouts  119 us (16%)
  matrix products  92 us (12%)
  other arithmetic  65.1 us (9%)
  Pallas kernels  55.2 us (7%)
  between operations  17.2 us (2%)
    ppermute x45, waiting for transfers between devices, shift_z(): return lax.ppermute(array, 'seq', shifts[k % units])  116 us
    ppermute x45, starting transfers between devices, shift_z(): return lax.ppermute(array, 'seq', shifts[k % units])  97.4 us
    all_gather x1, waiting for transfers between devices, by_heads(): every = lax.all_gather(small, ('doc', 'seq'), axis=0, tiled=True)  61.5 us
    ppermute x8, waiting for transfers between devices, swap_y(): return lax.ppermute(array, 'doc', [(i, i ^ 2) for i in range(doc_ranks)])  45.7 us
    ppermute x9, waiting for transfers between devices, swap_x(): return lax.ppermute(array, 'seq', column_pairs)  38.8 us
    dynamic_slice x32, local copies, waits for them, and re-layouts, take(): return lax.dynamic_index_in_dim(array, index, axis, False)  33.3 us
    unnamed x217, local copies, waits for them, and re-layouts  30.2 us
    pallas_call x2, Pallas kernels, attention_back(): pl.pallas_call(functools.partial(attend_back_kernel, wide, size, causal,...  29.1 us
  transfers between devices with their start and end apart: 78, of which 28 were waited for; matrix products, arithmetic and copies ran while one was open for 33% of the time, Pallas kernels for 7%

profile of v3, /device:TPU:0, one launch (start us, length us, event | category | flops | bytes accessed | tf_op | source)
XLA Modules:
  0.0 748.5 jit_solution(6527712708851481564)
XLA Ops:
  36.4 61.5 %all-gather.3.cloned.1.call-done = bf16[5888,768]{1,0:T(8,128)(2,1)} async-done(((bf16[184,768]{1,0:T(8,128)(2,1)}), bf16[5888,768]{1,0:T(8,128)(2,1)}) %all-gather.3.cloned.1.call-update) | async-done | bytes 9043984 | tf_op jit(solution)/shard_map/all_gather | solution.py:815
  158.4 6.8 attend_self.1
  175.4 8.8 %collective-permute-start.10 = (bf16[256,128]{0,1:T(8,128)(2,1)S(1)}, bf16[256,128]{0,1:T(8,128)(2,1)S(1)}, u32[]{:S(2)}, u32[]{:S(2)}) collective-permute-start(bf16[256,128]{0,1:T(8,128)(2,1)S(1)} %bitcast.862), channel_id=1, source_target_pairs={{0,4},{1,5},{2,6},{3,7},{4,0},{5,1},{6,2},{7,3},{8,12},{9,13},{10,... | collective-permute-start | bytes 196616 | tf_op jit(solution)/shard_map/ppermute | solution.py:683
  184.2 7.6 %collective-permute-done.10 = bf16[256,128]{0,1:T(8,128)(2,1)S(1)} collective-permute-done((bf16[256,128]{0,1:T(8,128)(2,1)S(1)}, bf16[256,128]{0,1:T(8,128)(2,1)S(1)}, u32[]{:S(2)}, u32[]{:S(2)}) %collective-permute-start.10) | collective-permute-done | bytes 65568 | tf_op jit(solution)/shard_map/ppermute | solution.py:683
  191.9 8.2 %collective-permute-done.11 = bf16[256,128]{0,1:T(8,128)(2,1)S(1)} collective-permute-done((bf16[256,128]{0,1:T(8,128)(2,1)S(1)}, bf16[256,128]{0,1:T(8,128)(2,1)S(1)}, u32[]{:S(2)}, u32[]{:S(2)}) %collective-permute-start.11) | collective-permute-done | bytes 65568 | tf_op jit(solution)/shard_map/ppermute | solution.py:683
  204.5 14.9 %collective-permute-done.8 = bf16[128,1472]{0,1:T(8,128)(2,1)S(1)} collective-permute-done((bf16[128,1472]{0,1:T(8,128)(2,1)S(1)}, bf16[128,1472]{0,1:T(8,128)(2,1)S(1)}, u32[]{:S(2)}, u32[]{:S(2)}) %collective-permute-start.8) | collective-permute-done | bytes 376864 | tf_op jit(solution)/shard_map/ppermute | solution.py:674
  243.5 10.3 %collective-permute-done.19 = bf16[512,256]{1,0:T(8,128)(2,1)} collective-permute-done((bf16[512,256]{1,0:T(8,128)(2,1)}, bf16[512,256]{1,0:T(8,128)(2,1)}, u32[]{:S(2)}, u32[]{:S(2)}) %collective-permute-start.19) | collective-permute-done | bytes 262176 | tf_op jit(solution)/shard_map/ppermute | solution.py:683
  254.8 17.5 %collective-permute-done.20 = bf16[512,256]{1,0:T(8,128)(2,1)} collective-permute-done((bf16[512,256]{1,0:T(8,128)(2,1)}, bf16[512,256]{1,0:T(8,128)(2,1)}, u32[]{:S(2)}, u32[]{:S(2)}) %collective-permute-start.20) | collective-permute-done | bytes 262176 | tf_op jit(solution)/shard_map/ppermute | solution.py:683
  274.9 19.4 %attend_cross.1 = (bf16[1024,128]{1,0:T(8,128)(2,1)S(1)}, f32[128,1024]{1,0:T(8,128)S(1)}, f32[8,1024]{1,0:T(8,128)S(1)}) custom-call(s32[2]{0:T(128)S(1)} %pad_add_fusion.1.info_ref, bf16[1024,128]{1,0:T(8,128)(2,1)S(1)} %bitcast.794, bf16[4096,256]{1,0:T(8,128)(2,1)S(1)} %bitcast.784), custom_call_target="tpu_custom_call" | custom-call | flops 2147483648 | bytes 4194304 | tf_op jit(solution)/shard_map/attend_cross/pallas_call | solution.py:577
  295.3 9.1 %collective-permute-start.22 = (bf16[256,128]{0,1:T(8,128)(2,1)S(1)}, bf16[256,128]{0,1:T(8,128)(2,1)S(1)}, u32[]{:S(2)}, u32[]{:S(2)}) collective-permute-start(bf16[256,128]{0,1:T(8,128)(2,1)S(1)} %bitcast.860), channel_id=1, source_target_pairs={{0,2},{1,3},{2,4},{3,5},{4,6},{5,7},{6,0},{7,1},{8,10},{9,11},{10,... | collective-permute-start | bytes 196616 | tf_op jit(solution)/shard_map/ppermute | solution.py:683
  391.5 11.0 %collective-permute-done.36 = bf16[256,1472]{0,1:T(8,128)(2,1)} collective-permute-done((bf16[256,1472]{0,1:T(8,128)(2,1)}, bf16[256,1472]{0,1:T(8,128)(2,1)}, u32[]{:S(2)}, u32[]{:S(2)}) %collective-permute-start.36) | collective-permute-done | bytes 753696 | tf_op jit(solution)/shard_map/ppermute | solution.py:677
  426.8 21.4 %attend_cross_back.1 = (bf16[1024,128]{1,0:T(8,128)(2,1)S(1)}, bf16[4096,256]{1,0:T(8,128)(2,1)S(1)}) custom-call(s32[2]{0:T(128)S(1)} %pad_add_fusion.1.info_ref, bf16[1024,128]{1,0:T(8,128)(2,1)S(1)} %bitcast.795, bf16[4096,256]{1,0:T(8,128)(2,1)S(1)} %bitcast.785, bf16[1024,128]{1,0:T(8,128)(2,1)S(1)} %bitcast.797, f32[128,1024]{1,0:T(8,128)S(1)} %copy-done.6, ...), custom_call_target="tpu_custom_call" | custom-call | flops 5368709120 | bytes 4194304 | tf_op jit(solution)/shard_map/attend_cross_back/pallas_call | solution.py:608
  450.6 6.7 collective-permute-start.40
  470.7 7.5 %collective-permute-start.44 = (bf16[256,1472]{0,1:T(8,128)(2,1)S(1)}, bf16[256,1472]{0,1:T(8,128)(2,1)S(1)}, u32[]{:S(2)}, u32[]{:S(2)}) collective-permute-start(bf16[256,1472]{0,1:T(8,128)(2,1)S(1)} %fusion.71), channel_id=1, source_target_pairs={{0,16},{8,24},{16,0},{24,8},{1,17},{9,25},{17,1},{25,9},{2,18},{10... | collective-permute-start | bytes 2261000 | tf_op jit(solution)/shard_map/ppermute | solution.py:677
  479.7 15.7 %collective-permute-done.44 = bf16[256,1472]{0,1:T(8,128)(2,1)S(1)} collective-permute-done((bf16[256,1472]{0,1:T(8,128)(2,1)S(1)}, bf16[256,1472]{0,1:T(8,128)(2,1)S(1)}, u32[]{:S(2)}, u32[]{:S(2)}) %collective-permute-start.44) | collective-permute-done | bytes 753696 | tf_op jit(solution)/shard_map/ppermute | solution.py:677
  519.0 13.0 %collective-permute-done.48 = bf16[512,256]{1,0:T(8,128)(2,1)} collective-permute-done((bf16[512,256]{1,0:T(8,128)(2,1)}, bf16[512,256]{1,0:T(8,128)(2,1)}, u32[]{:S(2)}, u32[]{:S(2)}) %collective-permute-start.48) | collective-permute-done | bytes 262176 | tf_op jit(solution)/shard_map/ppermute | solution.py:683
  533.7 19.3 %collective-permute-done.49 = bf16[512,256]{1,0:T(8,128)(2,1)} collective-permute-done((bf16[512,256]{1,0:T(8,128)(2,1)}, bf16[512,256]{1,0:T(8,128)(2,1)}, u32[]{:S(2)}, u32[]{:S(2)}) %collective-permute-start.49) | collective-permute-done | bytes 262176 | tf_op jit(solution)/shard_map/ppermute | solution.py:683
  555.4 13.4 %collective-permute-start.51 = (bf16[512,256]{1,0:T(8,128)(2,1)}, bf16[512,256]{1,0:T(8,128)(2,1)S(1)}, u32[]{:S(2)}, u32[]{:S(2)}) collective-permute-start(bf16[512,256]{1,0:T(8,128)(2,1)} %get-tuple-element.136), channel_id=1, source_target_pairs={{0,2},{1,3},{2,4},{3,5},{4,6},{5,7},{6,0},{7,1},{8,10},{9,11},{10,... | collective-permute-start | bytes 786440 | tf_op jit(solution)/shard_map/ppermute | solution.py:683
  577.9 7.7 %attend_self_back.1 = bf16[1024,384]{1,0:T(8,128)(2,1)S(1)} custom-call(s32[2]{0:T(128)S(1)} %pad_add_fusion.info_ref, bf16[1024,384]{1,0:T(8,128)(2,1)S(1)} %bitcast.793, bf16[1024,128]{1,0:T(8,128)(2,1)S(1)} %bitcast.796, f32[128,1024]{1,0:T(8,128)S(1)} %copy-done.4, f32[8,1024]{1,0:T(8,128)S(1)} %get-tuple-element.81.refs_3_), custom_call_target="tpu_custom_call" | custom-call | flops 671088640 | bytes 1048576 | tf_op jit(solution)/shard_map/attend_self_back/pallas_call | solution.py:608
  612.1 6.9 bitcast_convert_fusion
  675.0 9.9 %collective-permute-done.65 = bf16[4,192,288]{2,1,0:T(8,128)(2,1)S(1)} collective-permute-done((bf16[4,192,288]{2,1,0:T(8,128)(2,1)S(1)}, bf16[4,192,288]{2,1,0:T(8,128)(2,1)S(1)}, u32[]{:S(2)}, u32[]{:S(2)}) %collective-permute-start.65) | collective-permute-done | bytes 442400 | tf_op jit(solution)/shard_map/ppermute | solution.py:674
  688.0 10.5 %collective-permute-done.70 = bf16[480,1472]{1,0:T(8,128)(2,1)} collective-permute-done((bf16[480,1472]{1,0:T(8,128)(2,1)}, bf16[480,1472]{1,0:T(8,128)(2,1)}, u32[]{:S(2)}, u32[]{:S(2)}) %collective-permute-start.70) | collective-permute-done | bytes 1413152 | tf_op jit(solution)/shard_map/ppermute | solution.py:677
  706.1 14.0 %collective-permute-done.71 = bf16[4,184,480]{2,1,0:T(8,128)(2,1)S(1)} collective-permute-done((bf16[4,184,480]{2,1,0:T(8,128)(2,1)S(1)}, bf16[4,184,480]{2,1,0:T(8,128)(2,1)S(1)}, u32[]{:S(2)}, u32[]{:S(2)}) %collective-permute-start.71) | collective-permute-done | bytes 706592 | tf_op jit(solution)/shard_map/ppermute | solution.py:674
  726.7 9.2 %collective-permute-done.73 = bf16[184,480]{1,0:T(8,128)(2,1)S(1)} collective-permute-done((bf16[184,480]{1,0:T(8,128)(2,1)S(1)}, bf16[184,480]{1,0:T(8,128)(2,1)S(1)}, u32[]{:S(2)}, u32[]{:S(2)}) %collective-permute-start.73) | collective-permute-done | bytes 176672 | tf_op jit(solution)/shard_map/ppermute | solution.py:683
  (651 shorter events, 400.9 us)
Async XLA Ops:
  7.2 90.8 %all-gather.3.cloned.1.call-start = ((), (), s32[]{:S(2)}) async-start(), calls=%async_computation.1 | async-start | bytes 9326592 | tf_op jit(solution)/shard_map/all_gather | solution.py:815
  15.3 317.7 %all-gather.5.cloned.1.call-start = ((), (), s32[]{:S(2)}) async-start(), calls=%async_computation.2 | async-start | bytes 8902656 | tf_op jit(solution)/shard_map/all_gather | solution.py:817
  19.7 718.2 %reduce-scatter.4.cloned.1.call-start = ((), (), s32[]{:S(2)}) async-start(), calls=%async_computation.3 | async-start | bytes 8902656
  107.0 44.0 %collective-permute-start.5 = (bf16[256,384]{0,1:T(8,128)(2,1)}, bf16[256,384]{0,1:T(8,128)(2,1)}, u32[]{:S(2)}, u32[]{:S(2)}) collective-permute-start(bf16[256,384]{0,1:T(8,128)(2,1)} %get-tuple-element.183), channel_id=1, source_target_pairs={{0,2},{1,3},{2,4},{3,5},{4,6},{5,7},{6,0},{7,1},{8,10},{9,11},{10,... | collective-permute-start | bytes 589832 | tf_op jit(solution)/shard_map/ppermute | solution.py:683
  108.3 45.2 %collective-permute-start.6 = (bf16[256,384]{0,1:T(8,128)(2,1)}, bf16[256,384]{0,1:T(8,128)(2,1)}, u32[]{:S(2)}, u32[]{:S(2)}) collective-permute-start(bf16[256,384]{0,1:T(8,128)(2,1)} %get-tuple-element.182), channel_id=1, source_target_pairs={{0,4},{1,5},{2,6},{3,7},{4,0},{5,1},{6,2},{7,3},{8,12},{9,13},{10,... | collective-permute-start | bytes 589832 | tf_op jit(solution)/shard_map/ppermute | solution.py:683
  109.4 47.7 %collective-permute-start.7 = (bf16[256,384]{0,1:T(8,128)(2,1)}, bf16[256,384]{0,1:T(8,128)(2,1)}, u32[]{:S(2)}, u32[]{:S(2)}) collective-permute-start(bf16[256,384]{0,1:T(8,128)(2,1)} %get-tuple-element.181), channel_id=1, source_target_pairs={{0,6},{1,7},{2,0},{3,1},{4,2},{5,3},{6,4},{7,5},{8,14},{9,15},{10,... | collective-permute-start | bytes 589832 | tf_op jit(solution)/shard_map/ppermute | solution.py:683
  135.8 86.1 %collective-permute-start.12 = (bf16[4,512,256]{2,1,0:T(8,128)(2,1)}, bf16[4,512,256]{2,1,0:T(8,128)(2,1)}, u32[]{:S(2)}, u32[]{:S(2)}) collective-permute-start(bf16[4,512,256]{2,1,0:T(8,128)(2,1)} %bitcast.826), channel_id=1, source_target_pairs={{0,1},{1,0},{2,3},{3,2},{4,5},{5,4},{6,7},{7,6},{8,9},{9,8},{10,11... | collective-permute-start | bytes 3145736 | tf_op jit(solution)/shard_map/ppermute | solution.py:674
  148.3 53.2 %collective-permute-start.16 = (bf16[512,256]{1,0:T(8,128)(2,1)}, bf16[512,256]{1,0:T(8,128)(2,1)}, u32[]{:S(2)}, u32[]{:S(2)}) collective-permute-start(bf16[512,256]{1,0:T(8,128)(2,1)} %bitcast.847), channel_id=1, source_target_pairs={{0,2},{1,3},{2,4},{3,5},{4,6},{5,7},{6,0},{7,1},{8,10},{9,11},{10,... | collective-permute-start | bytes 786440 | tf_op jit(solution)/shard_map/ppermute | solution.py:683
  151.0 51.5 %collective-permute-start.17 = (bf16[512,256]{1,0:T(8,128)(2,1)}, bf16[512,256]{1,0:T(8,128)(2,1)}, u32[]{:S(2)}, u32[]{:S(2)}) collective-permute-start(bf16[512,256]{1,0:T(8,128)(2,1)} %bitcast.846), channel_id=1, source_target_pairs={{0,4},{1,5},{2,6},{3,7},{4,0},{5,1},{6,2},{7,3},{8,12},{9,13},{10,... | collective-permute-start | bytes 786440 | tf_op jit(solution)/shard_map/ppermute | solution.py:683
  153.5 50.0 %collective-permute-start.18 = (bf16[512,256]{1,0:T(8,128)(2,1)}, bf16[512,256]{1,0:T(8,128)(2,1)}, u32[]{:S(2)}, u32[]{:S(2)}) collective-permute-start(bf16[512,256]{1,0:T(8,128)(2,1)} %bitcast.126), channel_id=1, source_target_pairs={{0,6},{1,7},{2,0},{3,1},{4,2},{5,3},{6,4},{7,5},{8,14},{9,15},{10,... | collective-permute-start | bytes 786440 | tf_op jit(solution)/shard_map/ppermute | solution.py:683
  220.5 84.1 %collective-permute-start.28 = (bf16[256,1472]{0,1:T(8,128)(2,1)}, bf16[256,1472]{0,1:T(8,128)(2,1)}, u32[]{:S(2)}, u32[]{:S(2)}) collective-permute-start(bf16[256,1472]{0,1:T(8,128)(2,1)} %copy_bitcast_fusion), channel_id=1, source_target_pairs={{0,8},{8,0},{16,24},{24,16},{1,9},{9,1},{17,25},{25,17},{2,10},{10... | collective-permute-start | bytes 2261000 | tf_op jit(solution)/shard_map/ppermute | solution.py:680
  220.6 90.1 %collective-permute-start.29 = (bf16[256,1472]{0,1:T(8,128)(2,1)}, bf16[256,1472]{0,1:T(8,128)(2,1)}, u32[]{:S(2)}, u32[]{:S(2)}) collective-permute-start(bf16[256,1472]{0,1:T(8,128)(2,1)} %copy_bitcast_fusion), channel_id=1, source_target_pairs={{0,16},{8,24},{16,0},{24,8},{1,17},{9,25},{17,1},{25,9},{2,18},{10... | collective-permute-start | bytes 2261000 | tf_op jit(solution)/shard_map/ppermute | solution.py:677
  237.5 34.8 %collective-permute-start.20 = (bf16[512,256]{1,0:T(8,128)(2,1)}, bf16[512,256]{1,0:T(8,128)(2,1)}, u32[]{:S(2)}, u32[]{:S(2)}) collective-permute-start(bf16[512,256]{1,0:T(8,128)(2,1)} %get-tuple-element.165), channel_id=1, source_target_pairs={{0,4},{1,5},{2,6},{3,7},{4,0},{5,1},{6,2},{7,3},{8,12},{9,13},{10,... | collective-permute-start | bytes 786440 | tf_op jit(solution)/shard_map/ppermute | solution.py:683
  239.1 34.5 %collective-permute-start.21 = (bf16[512,256]{1,0:T(8,128)(2,1)}, bf16[512,256]{1,0:T(8,128)(2,1)}, u32[]{:S(2)}, u32[]{:S(2)}) collective-permute-start(bf16[512,256]{1,0:T(8,128)(2,1)} %get-tuple-element.164), channel_id=1, source_target_pairs={{0,6},{1,7},{2,0},{3,1},{4,2},{5,3},{6,4},{7,5},{8,14},{9,15},{10,... | collective-permute-start | bytes 786440 | tf_op jit(solution)/shard_map/ppermute | solution.py:683
  253.8 61.5 %collective-permute-start.25 = (bf16[256,1472]{0,1:T(8,128)(2,1)}, bf16[256,1472]{0,1:T(8,128)(2,1)}, u32[]{:S(2)}, u32[]{:S(2)}) collective-permute-start(bf16[256,1472]{0,1:T(8,128)(2,1)} %copy-done.39), channel_id=1, source_target_pairs={{0,8},{8,0},{16,24},{24,16},{1,9},{9,1},{17,25},{25,17},{2,10},{10... | collective-permute-start | bytes 2261000 | tf_op jit(solution)/shard_map/ppermute | solution.py:680
  272.3 42.9 %collective-permute-start.26 = (bf16[256,1472]{0,1:T(8,128)(2,1)}, bf16[256,1472]{0,1:T(8,128)(2,1)}, u32[]{:S(2)}, u32[]{:S(2)}) collective-permute-start(bf16[256,1472]{0,1:T(8,128)(2,1)} %copy-done.39), channel_id=1, source_target_pairs={{0,16},{8,24},{16,0},{24,8},{1,17},{9,25},{17,1},{25,9},{2,18},{10... | collective-permute-start | bytes 2261000 | tf_op jit(solution)/shard_map/ppermute | solution.py:677
  358.3 44.2 %collective-permute-start.32 = (bf16[256,1472]{0,1:T(8,128)(2,1)}, bf16[256,1472]{0,1:T(8,128)(2,1)S(1)}, u32[]{:S(2)}, u32[]{:S(2)}) collective-permute-start(bf16[256,1472]{0,1:T(8,128)(2,1)} %slice.1644), channel_id=1, source_target_pairs={{0,8},{8,0},{16,24},{24,16},{1,9},{9,1},{17,25},{25,17},{2,10},{10... | collective-permute-start | bytes 2261000 | tf_op jit(solution)/shard_map/ppermute | solution.py:680
  512.3 40.7 %collective-permute-start.49 = (bf16[512,256]{1,0:T(8,128)(2,1)}, bf16[512,256]{1,0:T(8,128)(2,1)}, u32[]{:S(2)}, u32[]{:S(2)}) collective-permute-start(bf16[512,256]{1,0:T(8,128)(2,1)} %get-tuple-element.138), channel_id=1, source_target_pairs={{0,4},{1,5},{2,6},{3,7},{4,0},{5,1},{6,2},{7,3},{8,12},{9,13},{10,... | collective-permute-start | bytes 786440 | tf_op jit(solution)/shard_map/ppermute | solution.py:683
  515.1 39.6 %collective-permute-start.50 = (bf16[512,256]{1,0:T(8,128)(2,1)}, bf16[512,256]{1,0:T(8,128)(2,1)S(1)}, u32[]{:S(2)}, u32[]{:S(2)}) collective-permute-start(bf16[512,256]{1,0:T(8,128)(2,1)} %get-tuple-element.137), channel_id=1, source_target_pairs={{0,6},{1,7},{2,0},{3,1},{4,2},{5,3},{6,4},{7,5},{8,14},{9,15},{10,... | collective-permute-start | bytes 786440 | tf_op jit(solution)/shard_map/ppermute | solution.py:683
  591.1 48.6 %collective-permute-start.56 = (bf16[256,384]{0,1:T(8,128)(2,1)}, bf16[256,384]{0,1:T(8,128)(2,1)}, u32[]{:S(2)}, u32[]{:S(2)}) collective-permute-start(bf16[256,384]{0,1:T(8,128)(2,1)} %bitcast.240), channel_id=1, source_target_pairs={{0,2},{1,3},{2,4},{3,5},{4,6},{5,7},{6,0},{7,1},{8,10},{9,11},{10,... | collective-permute-start | bytes 589832 | tf_op jit(solution)/shard_map/ppermute | solution.py:683
  598.0 43.3 %collective-permute-start.57 = (bf16[256,384]{0,1:T(8,128)(2,1)}, bf16[256,384]{0,1:T(8,128)(2,1)S(1)}, u32[]{:S(2)}, u32[]{:S(2)}) collective-permute-start(bf16[256,384]{0,1:T(8,128)(2,1)} %bitcast.242), channel_id=1, source_target_pairs={{0,4},{1,5},{2,6},{3,7},{4,0},{5,1},{6,2},{7,3},{8,12},{9,13},{10,... | collective-permute-start | bytes 589832 | tf_op jit(solution)/shard_map/ppermute | solution.py:683
  600.2 41.2 %collective-permute-start.58 = (bf16[256,384]{0,1:T(8,128)(2,1)}, bf16[256,384]{0,1:T(8,128)(2,1)S(1)}, u32[]{:S(2)}, u32[]{:S(2)}) collective-permute-start(bf16[256,384]{0,1:T(8,128)(2,1)} %bitcast.244), channel_id=1, source_target_pairs={{0,6},{1,7},{2,0},{3,1},{4,2},{5,3},{6,4},{7,5},{8,14},{9,15},{10,... | collective-permute-start | bytes 589832 | tf_op jit(solution)/shard_map/ppermute | solution.py:683
  606.3 35.1 %collective-permute-start.59 = (f32[128,1472]{0,1:T(8,128)}, f32[128,1472]{0,1:T(8,128)}, u32[]{:S(2)}, u32[]{:S(2)}) collective-permute-start(f32[128,1472]{0,1:T(8,128)} %bitcast.254), channel_id=1, source_target_pairs={{0,1},{1,0},{2,3},{3,2},{4,5},{5,4},{6,7},{7,6},{8,9},{9,8},{10,11... | collective-permute-start | bytes 2261000 | tf_op jit(solution)/shard_map/ppermute | solution.py:674
  664.9 33.6 %collective-permute-start.70 = (bf16[480,1472]{1,0:T(8,128)(2,1)}, bf16[480,1472]{1,0:T(8,128)(2,1)}, u32[]{:S(2)}, u32[]{:S(2)}) collective-permute-start(bf16[480,1472]{1,0:T(8,128)(2,1)} %fusion.76), channel_id=1, source_target_pairs={{0,16},{8,24},{16,0},{24,8},{1,17},{9,25},{17,1},{25,9},{2,18},{10... | collective-permute-start | bytes 4239368 | tf_op jit(solution)/shard_map/ppermute | solution.py:677
  (156 other events, 2001.7 us)
Sparse Core Ops, SparseCore 0:
  15.4 82.5 all-gather.2
  100.1 181.1 all-gather.4
  388.6 180.8 reduce-scatter.3

commit v4 on v3

--- a/solution.py
+++ b/solution.py
@@ -621,6 +621,38 @@
         compiler_params=pltpu.CompilerParams(vmem_limit_bytes=40 * 1024 * 1024),
         cost_estimate=pl.CostEstimate(flops=work, bytes_accessed=slots * lanes * 8, transcendentals=rows * slots),
     )(info, *parts, dmix, mixed, stats)
+
+
+def project_units_kernel(where_ref, rows_ref, weight_ref, out_ref):
+    out_ref[0, 0] = jnp.dot(
+        rows_ref[0], weight_ref[0], preferred_element_type=jnp.float32
+    ).astype(jnp.bfloat16)
+
+
+def project_units(rows, weight, x_rank, z_rank):
+    docs, count, width = rows.shape
+    units, _, lanes = weight.shape
+    where = jnp.stack([x_rank, z_rank]).astype(jnp.int32)
+    return pl.pallas_call(
+        project_units_kernel,
+        name="project_units",
+        out_shape=jax.ShapeDtypeStruct((docs, units, count, lanes), jnp.bfloat16),
+        grid_spec=pltpu.PrefetchScalarGridSpec(
+            num_scalar_prefetch=1,
+            grid=(docs, units),
+            in_specs=[
+                pl.BlockSpec((1, count, width), lambda h, k, at: ((at[0] + h) % docs, 0, 0)),
+                pl.BlockSpec((1, width, lanes), lambda h, k, at: ((at[1] + k) % units, 0, 0)),
+            ],
+            out_specs=pl.BlockSpec((1, 1, count, lanes), lambda h, k, at: (h, k, 0, 0)),
+        ),
+        compiler_params=pltpu.CompilerParams(vmem_limit_bytes=24 * 1024 * 1024),
+        cost_estimate=pl.CostEstimate(
+            flops=2 * docs * count * width * units * lanes,
+            bytes_accessed=2 * (docs * count * width + units * width * lanes + docs * units * count * lanes),
+            transcendentals=0,
+        ),
+    )(where, rows, weight)
 
 
 def take(array, index, axis=0):
@@ -707,6 +739,12 @@
             out = put(out, arrived, (z_rank - k) % units)
         return out.reshape((-1,) + out.shape[2:])
 
+    def collect(pieces):
+        out = jnp.broadcast_to(pieces[0], (units,) + pieces[0].shape)
+        for k in range(1, units):
+            out = put(out, shift_z(pieces[k], k), (z_rank - k) % units)
+        return out
+
     def to_rows(array):
         array = array.reshape((units, -1) + array.shape[1:])
         out = array
@@ -820,7 +858,12 @@
     stream = by_document(dec_in).astype(f32)
     normed1, inverse1 = norm_parts(stream, gain_all[0])
     normed1 = normed1.astype(bf16)
-    every, normed1, cotangent = tie((every, normed1, cotangent))
+    cot = by_document(cotangent)
+    cot_near, cot_far = gather_doc(cot)
+    n1_near, n1_far = gather_doc(normed1)
+    every, normed1, cot_near, cot_far, n1_near, n1_far = tie(
+        (every, normed1, cot_near, cot_far, n1_near, n1_far)
+    )
     every = every.reshape(doc_ranks, width, 8 * share)
     w_qkv = every[:, :, : 3 * share]
     w_cq = every[:, :, 3 * share : 4 * share]
@@ -829,32 +872,29 @@
     w_co = every[:, :, 7 * share :]
 
     qkv_rows = project(normed1, w_qkv, 3)
+    qkv_rows, w_ckv = tie((qkv_rows, w_ckv))
     qkv_heads = to_unit(qkv_rows)
     enc_rows = enc_in.reshape(slots, width)
     w_kv = spread_weight(w_ckv, 2)
-    ckv = project_wide(enc_rows, w_kv).reshape(units, docs_here, slots_doc, 2 * lanes)
-    ckv_other = swap_x(take(ckv, 1 - x_rank, 1))
-    ckv_own = to_unit(take(ckv, x_rank, 1))
-    qkv_heads, ckv, cotangent = tie((qkv_heads, ckv, cotangent))
+    ckv = project_units(enc_in, w_kv, x_rank, z_rank)
+    ckv_other = swap_x(ckv[1])
+    ckv_own = collect([ckv[0, k] for k in range(units)])
+    qkv_heads, ckv = tie((qkv_heads, ckv))
     att1, mix1, stat1 = attention(info_self, (qkv_heads,), True)
+    att1, ckv_own = tie((att1, ckv_own))
     att1 = to_rows(att1)
     att1, ckv_other = tie((att1, ckv_other))
-    ckv_other = to_unit(ckv_other)
+    ckv_other = collect([ckv_other[k] for k in range(units)])
     att1 = merge(att1, 1)
-    cot = by_document(cotangent)
-    cot_near, cot_far = gather_doc(cot)
     stream1 = stream + lift(att1, w_so)
     normed2, inverse2 = norm_parts(stream1, gain_all[1])
     normed2 = normed2.astype(bf16)
     cq_heads = to_unit(project(normed2, w_cq, 1))
-    cq_heads, normed1 = tie((cq_heads, normed1))
-    n1_near, n1_far = gather_doc(normed1)
-    halves = (ckv_own.reshape(units, slots_doc, 2 * lanes), ckv_other.reshape(units, slots_doc, 2 * lanes))
+    halves = (ckv_own, ckv_other)
     ckv_heads = jnp.where(first, jnp.stack(halves, axis=1), jnp.stack(halves[::-1], axis=1))
     ckv_heads = ckv_heads.reshape(units * slots, 2 * lanes)
     att2, mix2, stat2 = attention(info_cross, (cq_heads, ckv_heads), False)
     att2 = merge(to_rows(att2), 1)
-    att2, n1_near, n1_far, cot_near, cot_far = tie((att2, n1_near, n1_far, cot_near, cot_far))
     stream2 = stream1 + lift(att2, w_co)
     normed3, inverse3 = norm_parts(stream2, gain_all[2])
     normed3 = normed3.astype(bf16)

time: 754 us -> 769 us (1.020)
  starting transfers between devices: 137 us -> 169 us
  local copies, waits for them, and re-layouts: 119 us -> 91.6 us
  other arithmetic: 65.1 us -> 72.9 us
    all_gather x1, waiting for transfers between devices: 61.5 us -> 11.1 us  [by_heads(): every = lax.all_gather(small, ('doc', 'seq'), axis=0, tiled=True)]
    ppermute x8, waiting for transfers between devices: 45.7 us -> 82.1 us  [swap_y(): return lax.ppermute(array, 'doc', [(i, i ^ 2) for i in range(doc_ranks)])]
    ppermute x45, waiting for transfers between devices: 116 us -> 141 us  [shift_z(): return lax.ppermute(array, 'seq', shifts[k % units])]
    ppermute x45, starting transfers between devices: 97.4 us -> 121 us  [shift_z(): return lax.ppermute(array, 'seq', shifts[k % units])]
    dynamic_slice x32 -> x28, local copies, waits for them, and re-layouts: 33.3 us -> 16.4 us  [take(): return lax.dynamic_index_in_dim(array, index, axis, False)]
    dynamic_update_slice x51 -> x49, local copies, waits for them, and re-layouts: 18.2 us -> 11.7 us  [put(): return lax.dynamic_update_index_in_dim(array, piece, index, 0)]
    unnamed x217 -> x214, local copies, waits for them, and re-layouts: 30.2 us -> 27.2 us
  transfers between devices with their start and end apart: 78 -> 78, of which waited for: 28 -> 35; matrix products, arithmetic and copies ran while one was open for 33% -> 30% of each run, Pallas kernels for 7% -> 7%
where the time goes in v4:
time: 769 us; the launch traced here: 758 us
  waiting for transfers between devices  268 us (35%)
  starting transfers between devices  169 us (22%)
  local copies, waits for them, and re-layouts  91.6 us (12%)
  matrix products  90 us (12%)
  other arithmetic  72.9 us (9%)
  Pallas kernels  49.8 us (6%)
  between operations  17.2 us (2%)
    ppermute x45, waiting for transfers between devices, shift_z(): return lax.ppermute(array, 'seq', shifts[k % units])  141 us
    ppermute x45, starting transfers between devices, shift_z(): return lax.ppermute(array, 'seq', shifts[k % units])  121 us
    ppermute x8, waiting for transfers between devices, swap_y(): return lax.ppermute(array, 'doc', [(i, i ^ 2) for i in range(doc_ranks)])  82.1 us
    ppermute x9, waiting for transfers between devices, swap_x(): return lax.ppermute(array, 'seq', column_pairs)  32.8 us
    ppermute x8, starting transfers between devices, swap_y(): return lax.ppermute(array, 'doc', [(i, i ^ 2) for i in range(doc_ranks)])  27.5 us
    unnamed x214, local copies, waits for them, and re-layouts  27.2 us
    pallas_call x2, Pallas kernels, attention_back(): pl.pallas_call(functools.partial(attend_back_kernel, wide, size, causal,...  23.5 us
    pallas_call x2, Pallas kernels, attention(): pl.pallas_call(functools.partial(attend_kernel, wide, size, causal, len(p...  21 us
  transfers between devices with their start and end apart: 78, of which 35 were waited for; matrix products, arithmetic and copies ran while one was open for 30% of the time, Pallas kernels for 7%

profile of v4, /device:TPU:0, one launch (start us, length us, event | category | flops | bytes accessed | tf_op | source)
XLA Modules:
  0.0 758.5 jit_solution(13092518211111705819)
XLA Ops:
  26.2 10.1 %collective-permute-done.5 = bf16[128,1472]{0,1:T(8,128)(2,1)S(1)} collective-permute-done((bf16[128,1472]{0,1:T(8,128)(2,1)S(1)}, bf16[128,1472]{0,1:T(8,128)(2,1)S(1)}, u32[]{:S(2)}, u32[]{:S(2)}) %collective-permute-start.5) | collective-permute-done | bytes 376864 | tf_op jit(solution)/shard_map/ppermute | solution.py:706
  47.6 13.9 %collective-permute-done.7 = bf16[256,1472]{0,1:T(8,128)(2,1)} collective-permute-done((bf16[256,1472]{0,1:T(8,128)(2,1)}, bf16[256,1472]{0,1:T(8,128)(2,1)}, u32[]{:S(2)}, u32[]{:S(2)}) %collective-permute-start.7) | collective-permute-done | bytes 753696 | tf_op jit(solution)/shard_map/ppermute | solution.py:709
  62.5 22.9 %collective-permute-done.10 = bf16[256,1472]{0,1:T(8,128)(2,1)} collective-permute-done((bf16[256,1472]{0,1:T(8,128)(2,1)}, bf16[256,1472]{0,1:T(8,128)(2,1)}, u32[]{:S(2)}, u32[]{:S(2)}) %collective-permute-start.10) | collective-permute-done | bytes 753696 | tf_op jit(solution)/shard_map/ppermute | solution.py:709
  95.6 11.1 %all-gather.3.cloned.1.call-done = bf16[5888,768]{1,0:T(8,128)(2,1)} async-done(((bf16[184,768]{1,0:T(8,128)(2,1)}), bf16[5888,768]{1,0:T(8,128)(2,1)}) %all-gather.3.cloned.1.call-update) | async-done | bytes 9043984 | tf_op jit(solution)/shard_map/all_gather | solution.py:853
  158.6 26.2 %collective-permute-done.16 = bf16[512,256]{1,0:T(8,128)(2,1)S(1)} collective-permute-done((bf16[512,256]{1,0:T(8,128)(2,1)}, bf16[512,256]{1,0:T(8,128)(2,1)S(1)}, u32[]{:S(2)}, u32[]{:S(2)}) %collective-permute-start.16) | collective-permute-done | bytes 262176 | tf_op jit(solution)/shard_map/ppermute | solution.py:715
  226.7 11.2 %collective-permute-done.25 = bf16[512,256]{1,0:T(8,128)(2,1)} collective-permute-done((bf16[512,256]{1,0:T(8,128)(2,1)}, bf16[512,256]{1,0:T(8,128)(2,1)}, u32[]{:S(2)}, u32[]{:S(2)}) %collective-permute-start.25) | collective-permute-done | bytes 262176 | tf_op jit(solution)/shard_map/ppermute | solution.py:715
  238.9 21.1 %collective-permute-done.26 = bf16[512,256]{1,0:T(8,128)(2,1)S(1)} collective-permute-done((bf16[512,256]{1,0:T(8,128)(2,1)}, bf16[512,256]{1,0:T(8,128)(2,1)S(1)}, u32[]{:S(2)}, u32[]{:S(2)}) %collective-permute-start.26) | collective-permute-done | bytes 262176 | tf_op jit(solution)/shard_map/ppermute | solution.py:715
  260.4 13.9 %attend_cross.1 = (bf16[1024,128]{1,0:T(8,128)(2,1)S(1)}, f32[128,1024]{1,0:T(8,128)S(1)}, f32[8,1024]{1,0:T(8,128)S(1)}) custom-call(s32[2]{0:T(128)S(1)} %pad_add_fusion.2.info_ref, bf16[1024,128]{1,0:T(8,128)(2,1)S(1)} %bitcast.779, bf16[4096,256]{1,0:T(8,128)(2,1)S(1)} %bitcast.769), custom_call_target="tpu_custom_call" | custom-call | flops 2147483648 | bytes 4194304 | tf_op jit(solution)/shard_map/attend_cross/pallas_call | solution.py:577
  275.4 22.3 %collective-permute-start.28 = (bf16[256,128]{0,1:T(8,128)(2,1)S(1)}, bf16[256,128]{0,1:T(8,128)(2,1)S(1)}, u32[]{:S(2)}, u32[]{:S(2)}) collective-permute-start(bf16[256,128]{0,1:T(8,128)(2,1)S(1)} %bitcast.850), channel_id=1, source_target_pairs={{0,2},{1,3},{2,4},{3,5},{4,6},{5,7},{6,0},{7,1},{8,10},{9,11},{10,... | collective-permute-start | bytes 196616 | tf_op jit(solution)/shard_map/ppermute | solution.py:715
  312.4 9.7 %collective-permute-start.33 = (bf16[256,1472]{0,1:T(8,128)(2,1)S(1)}, bf16[256,1472]{0,1:T(8,128)(2,1)S(1)}, u32[]{:S(2)}, u32[]{:S(2)}) collective-permute-start(bf16[256,1472]{0,1:T(8,128)(2,1)S(1)} %multiply_convert_fusion.4), channel_id=1, source_target_pairs={{0,16},{8,24},{16,0},{24,8},{1,17},{9,25},{17,1},{25,9},{2,18},{10... | collective-permute-start | bytes 2261000 | tf_op jit(solution)/shard_map/ppermute | solution.py:709
  328.9 10.6 %collective-permute-done.33 = bf16[256,1472]{0,1:T(8,128)(2,1)S(1)} collective-permute-done((bf16[256,1472]{0,1:T(8,128)(2,1)S(1)}, bf16[256,1472]{0,1:T(8,128)(2,1)S(1)}, u32[]{:S(2)}, u32[]{:S(2)}) %collective-permute-start.33) | collective-permute-done | bytes 753696 | tf_op jit(solution)/shard_map/ppermute | solution.py:709
  379.8 10.8 %collective-permute-done.36 = bf16[256,1472]{0,1:T(8,128)(2,1)} collective-permute-done((bf16[256,1472]{0,1:T(8,128)(2,1)}, bf16[256,1472]{0,1:T(8,128)(2,1)}, u32[]{:S(2)}, u32[]{:S(2)}) %collective-permute-start.36) | collective-permute-done | bytes 753696 | tf_op jit(solution)/shard_map/ppermute | solution.py:709
  416.0 15.4 %attend_cross_back.1 = (bf16[1024,128]{1,0:T(8,128)(2,1)S(1)}, bf16[4096,256]{1,0:T(8,128)(2,1)S(1)}) custom-call(s32[2]{0:T(128)S(1)} %pad_add_fusion.2.info_ref, bf16[1024,128]{1,0:T(8,128)(2,1)S(1)} %bitcast.780, bf16[4096,256]{1,0:T(8,128)(2,1)S(1)} %bitcast.770, bf16[1024,128]{1,0:T(8,128)(2,1)S(1)} %bitcast.782, f32[128,1024]{1,0:T(8,128)S(1)} %copy-done.6, ...), custom_call_target="tpu_custom_call" | custom-call | flops 5368709120 | bytes 4194304 | tf_op jit(solution)/shard_map/attend_cross_back/pallas_call | solution.py:608
  451.3 10.6 %collective-permute-start.44 = (bf16[256,1472]{0,1:T(8,128)(2,1)S(1)}, bf16[256,1472]{0,1:T(8,128)(2,1)S(1)}, u32[]{:S(2)}, u32[]{:S(2)}) collective-permute-start(bf16[256,1472]{0,1:T(8,128)(2,1)S(1)} %fusion.72), channel_id=1, source_target_pairs={{0,16},{8,24},{16,0},{24,8},{1,17},{9,25},{17,1},{25,9},{2,18},{10... | collective-permute-start | bytes 2261000 | tf_op jit(solution)/shard_map/ppermute | solution.py:709
  463.3 15.6 %collective-permute-done.44 = bf16[256,1472]{0,1:T(8,128)(2,1)S(1)} collective-permute-done((bf16[256,1472]{0,1:T(8,128)(2,1)S(1)}, bf16[256,1472]{0,1:T(8,128)(2,1)S(1)}, u32[]{:S(2)}, u32[]{:S(2)}) %collective-permute-start.44) | collective-permute-done | bytes 753696 | tf_op jit(solution)/shard_map/ppermute | solution.py:709
  501.1 8.9 %collective-permute-done.48 = bf16[512,256]{1,0:T(8,128)(2,1)} collective-permute-done((bf16[512,256]{1,0:T(8,128)(2,1)}, bf16[512,256]{1,0:T(8,128)(2,1)}, u32[]{:S(2)}, u32[]{:S(2)}) %collective-permute-start.48) | collective-permute-done | bytes 262176 | tf_op jit(solution)/shard_map/ppermute | solution.py:715
  511.7 20.5 %collective-permute-done.49 = bf16[512,256]{1,0:T(8,128)(2,1)S(1)} collective-permute-done((bf16[512,256]{1,0:T(8,128)(2,1)}, bf16[512,256]{1,0:T(8,128)(2,1)S(1)}, u32[]{:S(2)}, u32[]{:S(2)}) %collective-permute-start.49) | collective-permute-done | bytes 262176 | tf_op jit(solution)/shard_map/ppermute | solution.py:715
  533.7 10.7 %collective-permute-start.54 = (bf16[4,512,256]{2,1,0:T(8,128)(2,1)}, bf16[4,512,256]{2,1,0:T(8,128)(2,1)S(1)}, u32[]{:S(2)}, u32[]{:S(2)}) collective-permute-start(bf16[4,512,256]{2,1,0:T(8,128)(2,1)} %bitcast_dynamic-update-slice_fusion.4), channel_id=1, source_target_pairs={{0,1},{1,0},{2,3},{3,2},{4,5},{5,4},{6,7},{7,6},{8,9},{9,8},{10,11... | collective-permute-start | bytes 3145736 | tf_op jit(solution)/shard_map/ppermute | solution.py:706
  544.3 15.9 %collective-permute-start.51 = (bf16[512,256]{1,0:T(8,128)(2,1)S(1)}, bf16[512,256]{1,0:T(8,128)(2,1)S(1)}, u32[]{:S(2)}, u32[]{:S(2)}) collective-permute-start(bf16[512,256]{1,0:T(8,128)(2,1)S(1)} %copy-done.65), channel_id=1, source_target_pairs={{0,2},{1,3},{2,4},{3,5},{4,6},{5,7},{6,0},{7,1},{8,10},{9,11},{10,... | collective-permute-start | bytes 786440 | tf_op jit(solution)/shard_map/ppermute | solution.py:715
  568.2 8.1 %attend_self_back.1 = bf16[1024,384]{1,0:T(8,128)(2,1)S(1)} custom-call(s32[2]{0:T(128)S(1)} %pad_add_fusion.info_ref, bf16[1024,384]{1,0:T(8,128)(2,1)S(1)} %bitcast.778, bf16[1024,128]{1,0:T(8,128)(2,1)S(1)} %bitcast.781, f32[128,1024]{1,0:T(8,128)S(1)} %copy-done.4, f32[8,1024]{1,0:T(8,128)S(1)} %get-tuple-element.79.refs_3_), custom_call_target="tpu_custom_call" | custom-call | flops 671088640 | bytes 1048576 | tf_op jit(solution)/shard_map/attend_self_back/pallas_call | solution.py:608
  581.6 9.7 %collective-permute-start.56 = (bf16[256,384]{0,1:T(8,128)(2,1)}, bf16[256,384]{0,1:T(8,128)(2,1)}, u32[]{:S(2)}, u32[]{:S(2)}) collective-permute-start(bf16[256,384]{0,1:T(8,128)(2,1)} %bitcast.240), channel_id=1, source_target_pairs={{0,2},{1,3},{2,4},{3,5},{4,6},{5,7},{6,0},{7,1},{8,10},{9,11},{10,... | collective-permute-start | bytes 589832 | tf_op jit(solution)/shard_map/ppermute | solution.py:715
  681.6 11.6 %collective-permute-done.65 = bf16[4,192,288]{1,0,2:T(4,128)(2,1)S(1)} collective-permute-done((bf16[4,192,288]{1,0,2:T(4,128)(2,1)}, bf16[4,192,288]{1,0,2:T(4,128)(2,1)S(1)}, u32[]{:S(2)}, u32[]{:S(2)}) %collective-permute-start.65) | collective-permute-done | bytes 442400 | tf_op jit(solution)/shard_map/ppermute | solution.py:706
  710.6 11.1 %collective-permute-done.71 = bf16[4,184,480]{2,1,0:T(8,128)(2,1)S(1)} collective-permute-done((bf16[4,184,480]{2,1,0:T(8,128)(2,1)}, bf16[4,184,480]{2,1,0:T(8,128)(2,1)S(1)}, u32[]{:S(2)}, u32[]{:S(2)}) %collective-permute-start.71) | collective-permute-done | bytes 706592 | tf_op jit(solution)/shard_map/ppermute | solution.py:706
  730.7 13.1 %collective-permute-done.73 = bf16[184,480]{0,1:T(8,128)(2,1)S(1)} collective-permute-done((bf16[184,480]{0,1:T(8,128)(2,1)S(1)}, bf16[184,480]{0,1:T(8,128)(2,1)S(1)}, u32[]{:S(2)}, u32[]{:S(2)}) %collective-permute-start.73) | collective-permute-done | bytes 176672 | tf_op jit(solution)/shard_map/ppermute | solution.py:715
  (664 shorter events, 406.5 us)
Async XLA Ops:
  7.2 99.6 %all-gather.3.cloned.1.call-start = ((), (), s32[]{:S(2)}) async-start(), calls=%async_computation.1 | async-start | bytes 9326592 | tf_op jit(solution)/shard_map/all_gather | solution.py:853
  12.7 295.5 %all-gather.5.cloned.1.call-start = ((), (), s32[]{:S(2)}) async-start(), calls=%async_computation.2 | async-start | bytes 8902656 | tf_op jit(solution)/shard_map/all_gather | solution.py:855
  37.4 48.0 %collective-permute-start.6 = (bf16[256,1472]{0,1:T(8,128)(2,1)}, bf16[256,1472]{0,1:T(8,128)(2,1)}, u32[]{:S(2)}, u32[]{:S(2)}) collective-permute-start(bf16[256,1472]{0,1:T(8,128)(2,1)} %copy_bitcast_fusion), channel_id=1, source_target_pairs={{0,8},{8,0},{16,24},{24,16},{1,9},{9,1},{17,25},{25,17},{2,10},{10... | collective-permute-start | bytes 2261000 | tf_op jit(solution)/shard_map/ppermute | solution.py:712
  40.3 45.1 %collective-permute-start.10 = (bf16[256,1472]{0,1:T(8,128)(2,1)}, bf16[256,1472]{0,1:T(8,128)(2,1)}, u32[]{:S(2)}, u32[]{:S(2)}) collective-permute-start(bf16[256,1472]{0,1:T(8,128)(2,1)} %fusion.65), channel_id=1, source_target_pairs={{0,16},{8,24},{16,0},{24,8},{1,17},{9,25},{17,1},{25,9},{2,18},{10... | collective-permute-start | bytes 2261000 | tf_op jit(solution)/shard_map/ppermute | solution.py:709
  41.0 47.1 %collective-permute-start.9 = (bf16[256,1472]{0,1:T(8,128)(2,1)}, bf16[256,1472]{0,1:T(8,128)(2,1)}, u32[]{:S(2)}, u32[]{:S(2)}) collective-permute-start(bf16[256,1472]{0,1:T(8,128)(2,1)} %fusion.65), channel_id=1, source_target_pairs={{0,8},{8,0},{16,24},{24,16},{1,9},{9,1},{17,25},{25,17},{2,10},{10... | collective-permute-start | bytes 2261000 | tf_op jit(solution)/shard_map/ppermute | solution.py:712
  42.1 705.9 %reduce-scatter.4.cloned.1.call-start = ((), (), s32[]{:S(2)}) async-start(), calls=%async_computation.3 | async-start | bytes 8902656
  61.5 29.1 %collective-permute-start.8 = (bf16[256,1472]{0,1:T(8,128)(2,1)}, bf16[256,1472]{0,1:T(8,128)(2,1)}, u32[]{:S(2)}, u32[]{:S(2)}) collective-permute-start(bf16[256,1472]{0,1:T(8,128)(2,1)} %collective-permute-done.7), channel_id=1, source_target_pairs={{0,8},{8,0},{16,24},{24,16},{1,9},{9,1},{17,25},{25,17},{2,10},{10... | collective-permute-start | bytes 2261000 | tf_op jit(solution)/shard_map/ppermute | solution.py:712
  133.1 51.7 %collective-permute-start.16 = (bf16[512,256]{1,0:T(8,128)(2,1)}, bf16[512,256]{1,0:T(8,128)(2,1)S(1)}, u32[]{:S(2)}, u32[]{:S(2)}) collective-permute-start(bf16[512,256]{1,0:T(8,128)(2,1)} %get-tuple-element.172), channel_id=1, source_target_pairs={{0,4},{1,5},{2,6},{3,7},{4,0},{5,1},{6,2},{7,3},{8,12},{9,13},{10,... | collective-permute-start | bytes 786440 | tf_op jit(solution)/shard_map/ppermute | solution.py:715
  135.7 49.1 %collective-permute-start.17 = (bf16[512,256]{1,0:T(8,128)(2,1)}, bf16[512,256]{1,0:T(8,128)(2,1)S(1)}, u32[]{:S(2)}, u32[]{:S(2)}) collective-permute-start(bf16[512,256]{1,0:T(8,128)(2,1)} %get-tuple-element.171), channel_id=1, source_target_pairs={{0,6},{1,7},{2,0},{3,1},{4,2},{5,3},{6,4},{7,5},{8,14},{9,15},{10,... | collective-permute-start | bytes 786440 | tf_op jit(solution)/shard_map/ppermute | solution.py:715
  144.5 58.1 %collective-permute-start.21 = (bf16[4,512,256]{2,1,0:T(8,128)(2,1)}, bf16[4,512,256]{2,1,0:T(8,128)(2,1)}, u32[]{:S(2)}, u32[]{:S(2)}) collective-permute-start(bf16[4,512,256]{2,1,0:T(8,128)(2,1)} %slice_bitcast_fusion), channel_id=1, source_target_pairs={{0,1},{1,0},{2,3},{3,2},{4,5},{5,4},{6,7},{7,6},{8,9},{9,8},{10,11... | collective-permute-start | bytes 3145736 | tf_op jit(solution)/shard_map/ppermute | solution.py:706
  221.2 38.8 %collective-permute-start.26 = (bf16[512,256]{1,0:T(8,128)(2,1)}, bf16[512,256]{1,0:T(8,128)(2,1)S(1)}, u32[]{:S(2)}, u32[]{:S(2)}) collective-permute-start(bf16[512,256]{1,0:T(8,128)(2,1)} %get-tuple-element.198), channel_id=1, source_target_pairs={{0,4},{1,5},{2,6},{3,7},{4,0},{5,1},{6,2},{7,3},{8,12},{9,13},{10,... | collective-permute-start | bytes 786440 | tf_op jit(solution)/shard_map/ppermute | solution.py:715
  222.6 37.4 %collective-permute-start.27 = (bf16[512,256]{1,0:T(8,128)(2,1)}, bf16[512,256]{1,0:T(8,128)(2,1)S(1)}, u32[]{:S(2)}, u32[]{:S(2)}) collective-permute-start(bf16[512,256]{1,0:T(8,128)(2,1)} %get-tuple-element.197), channel_id=1, source_target_pairs={{0,6},{1,7},{2,0},{3,1},{4,2},{5,3},{6,4},{7,5},{8,14},{9,15},{10,... | collective-permute-start | bytes 786440 | tf_op jit(solution)/shard_map/ppermute | solution.py:715
  347.4 43.2 %collective-permute-start.32 = (bf16[256,1472]{0,1:T(8,128)(2,1)}, bf16[256,1472]{0,1:T(8,128)(2,1)}, u32[]{:S(2)}, u32[]{:S(2)}) collective-permute-start(bf16[256,1472]{0,1:T(8,128)(2,1)} %slice.1653), channel_id=1, source_target_pairs={{0,8},{8,0},{16,24},{24,16},{1,9},{9,1},{17,25},{25,17},{2,10},{10... | collective-permute-start | bytes 2261000 | tf_op jit(solution)/shard_map/ppermute | solution.py:712
  451.3 27.6 %collective-permute-start.44 = (bf16[256,1472]{0,1:T(8,128)(2,1)S(1)}, bf16[256,1472]{0,1:T(8,128)(2,1)S(1)}, u32[]{:S(2)}, u32[]{:S(2)}) collective-permute-start(bf16[256,1472]{0,1:T(8,128)(2,1)S(1)} %fusion.72), channel_id=1, source_target_pairs={{0,16},{8,24},{16,0},{24,8},{1,17},{9,25},{17,1},{25,9},{2,18},{10... | collective-permute-start | bytes 2261000 | tf_op jit(solution)/shard_map/ppermute | solution.py:709
  495.5 36.7 %collective-permute-start.49 = (bf16[512,256]{1,0:T(8,128)(2,1)}, bf16[512,256]{1,0:T(8,128)(2,1)S(1)}, u32[]{:S(2)}, u32[]{:S(2)}) collective-permute-start(bf16[512,256]{1,0:T(8,128)(2,1)} %get-tuple-element.169), channel_id=1, source_target_pairs={{0,4},{1,5},{2,6},{3,7},{4,0},{5,1},{6,2},{7,3},{8,12},{9,13},{10,... | collective-permute-start | bytes 786440 | tf_op jit(solution)/shard_map/ppermute | solution.py:715
  497.9 35.1 %collective-permute-start.50 = (bf16[512,256]{1,0:T(8,128)(2,1)}, bf16[512,256]{1,0:T(8,128)(2,1)S(1)}, u32[]{:S(2)}, u32[]{:S(2)}) collective-permute-start(bf16[512,256]{1,0:T(8,128)(2,1)} %get-tuple-element.168), channel_id=1, source_target_pairs={{0,6},{1,7},{2,0},{3,1},{4,2},{5,3},{6,4},{7,5},{8,14},{9,15},{10,... | collective-permute-start | bytes 786440 | tf_op jit(solution)/shard_map/ppermute | solution.py:715
  533.7 44.6 %collective-permute-start.54 = (bf16[4,512,256]{2,1,0:T(8,128)(2,1)}, bf16[4,512,256]{2,1,0:T(8,128)(2,1)S(1)}, u32[]{:S(2)}, u32[]{:S(2)}) collective-permute-start(bf16[4,512,256]{2,1,0:T(8,128)(2,1)} %bitcast_dynamic-update-slice_fusion.4), channel_id=1, source_target_pairs={{0,1},{1,0},{2,3},{3,2},{4,5},{5,4},{6,7},{7,6},{8,9},{9,8},{10,11... | collective-permute-start | bytes 3145736 | tf_op jit(solution)/shard_map/ppermute | solution.py:706
  581.6 49.1 %collective-permute-start.56 = (bf16[256,384]{0,1:T(8,128)(2,1)}, bf16[256,384]{0,1:T(8,128)(2,1)}, u32[]{:S(2)}, u32[]{:S(2)}) collective-permute-start(bf16[256,384]{0,1:T(8,128)(2,1)} %bitcast.240), channel_id=1, source_target_pairs={{0,2},{1,3},{2,4},{3,5},{4,6},{5,7},{6,0},{7,1},{8,10},{9,11},{10,... | collective-permute-start | bytes 589832 | tf_op jit(solution)/shard_map/ppermute | solution.py:715
  592.2 40.1 %collective-permute-start.57 = (bf16[256,384]{0,1:T(8,128)(2,1)}, bf16[256,384]{0,1:T(8,128)(2,1)S(1)}, u32[]{:S(2)}, u32[]{:S(2)}) collective-permute-start(bf16[256,384]{0,1:T(8,128)(2,1)} %bitcast.242), channel_id=1, source_target_pairs={{0,4},{1,5},{2,6},{3,7},{4,0},{5,1},{6,2},{7,3},{8,12},{9,13},{10,... | collective-permute-start | bytes 589832 | tf_op jit(solution)/shard_map/ppermute | solution.py:715
  593.3 39.0 %collective-permute-start.58 = (bf16[256,384]{0,1:T(8,128)(2,1)}, bf16[256,384]{0,1:T(8,128)(2,1)S(1)}, u32[]{:S(2)}, u32[]{:S(2)}) collective-permute-start(bf16[256,384]{0,1:T(8,128)(2,1)} %bitcast.244), channel_id=1, source_target_pairs={{0,6},{1,7},{2,0},{3,1},{4,2},{5,3},{6,4},{7,5},{8,14},{9,15},{10,... | collective-permute-start | bytes 589832 | tf_op jit(solution)/shard_map/ppermute | solution.py:715
  603.6 28.7 %collective-permute-start.59 = (f32[128,1472]{0,1:T(8,128)}, f32[128,1472]{0,1:T(8,128)}, u32[]{:S(2)}, u32[]{:S(2)}) collective-permute-start(f32[128,1472]{0,1:T(8,128)} %bitcast.254), channel_id=1, source_target_pairs={{0,1},{1,0},{2,3},{3,2},{4,5},{5,4},{6,7},{7,6},{8,9},{9,8},{10,11... | collective-permute-start | bytes 2261000 | tf_op jit(solution)/shard_map/ppermute | solution.py:706
  630.7 28.7 %collective-permute-start.69 = (bf16[2,480,1472]{2,1,0:T(8,128)(2,1)}, bf16[2,480,1472]{2,1,0:T(8,128)(2,1)}, u32[]{:S(2)}, u32[]{:S(2)}) collective-permute-start(bf16[2,480,1472]{2,1,0:T(8,128)(2,1)} %pad_maximum_fusion.4), channel_id=1, source_target_pairs={{0,8},{8,0},{16,24},{24,16},{1,9},{9,1},{17,25},{25,17},{2,10},{10... | collective-permute-start | bytes 8478728 | tf_op jit(solution)/shard_map/ppermute | solution.py:712
  641.3 37.0 %collective-permute-start.60 = (f32[128,1472]{0,1:T(8,128)}, f32[128,1472]{0,1:T(8,128)}, u32[]{:S(2)}, u32[]{:S(2)}) collective-permute-start(f32[128,1472]{0,1:T(8,128)} %bitcast.285), channel_id=1, source_target_pairs={{0,1},{1,0},{2,3},{3,2},{4,5},{5,4},{6,7},{7,6},{8,9},{9,8},{10,11... | collective-permute-start | bytes 2261000 | tf_op jit(solution)/shard_map/ppermute | solution.py:706
  666.2 33.7 %collective-permute-start.70 = (bf16[480,1472]{1,0:T(8,128)(2,1)}, bf16[480,1472]{1,0:T(8,128)(2,1)}, u32[]{:S(2)}, u32[]{:S(2)}) collective-permute-start(bf16[480,1472]{1,0:T(8,128)(2,1)} %fusion.76), channel_id=1, source_target_pairs={{0,16},{8,24},{16,0},{24,8},{1,17},{9,25},{17,1},{25,9},{2,18},{10... | collective-permute-start | bytes 4239368 | tf_op jit(solution)/shard_map/ppermute | solution.py:709
  (149 other events, 1668.5 us)
Sparse Core Ops, SparseCore 0:
  12.9 93.8 all-gather.2
  109.0 182.7 all-gather.4
  376.8 178.1 reduce-scatter.3
